TPU v7x, 128 devices: a whole 4x4x4 slice. The times are simulated.
128 devices in a mesh: ep: 8 (over y, core), tp: 16 (over z, x).
Axes of the slice: x: 4, y: 4, z: 4, core: 2. Of those that a mesh axis runs over, the one named last changes fastest.
Arguments:
- query_key_value: bfloat16 [32, 512, 3, 1792], P('ep', 'tp'), may hold values from -6 to 6
- residual: bfloat16 [32, 512, 1792], P('ep', 'tp'), may hold values from -6 to 6
- norm_gain: float32 [1792], replicated, may hold values from 0.1 to 1.9
- expert_ids: int32 [32, 512, 2], P('ep', 'tp'), may hold values from 0 to 15, as said below
- route_gates: float32 [32, 512, 2], P('ep', 'tp'), may hold values from 0.2 to 1
- slot_index: int32 [32, 512, 2], P('ep', 'tp'), may hold values from -1 to 15, as said below
- w_gate: bfloat16 [16, 1792, 7168], P('ep', None, 'tp'), may hold values from -0.125 to 0.125
- w_up: bfloat16 [16, 1792, 7168], P('ep', None, 'tp'), may hold values from -0.125 to 0.125
- w_down: bfloat16 [16, 7168, 1792], P('ep', 'tp'), may hold values from -0.0625 to 0.0625
Outputs:
- block_out: bfloat16 [32, 512, 1792], P('ep', 'tp')
Inputs may be any that keep to these rules, and one draw needn't show every extreme that they name: `expert_ids`: each token names two different experts. One expert is the first choice of 16 or more tokens of every device (a device holds 4 frames by 32 sites). `slot_index`: the rank of an assignment among the assignments of the same expert on the same device, counted in the order frame, site, choice; -1 where that rank is 16 or more. Every device fills all 16 slots of some expert.
All inputs are finite; a program needn't handle non-finite values.
Results may differ from a plain program's by a relative error of at most 0.0095.
Values may be sent and summed in bfloat16 or wider, within the bound.
No kernel may reach another device: no remote copies, remote signals or barrier semaphores. Data moves between devices by JAX's collectives and lax.ppermute only.
A program may use at most 128 MiB of HBM per device.

v0:
```python
import math

import jax
import jax.numpy as jnp
from jax import lax
from jax.experimental import pallas as pl
from jax.experimental.pallas import tpu as pltpu
from jax.sharding import PartitionSpec as P


HD = 64
SITE_GROUP = 8
LANES = 2 * HD
SIDE = 4


def nt_dot(left, right):
    return lax.dot_general(
        left, right, (((1,), (1,)), ((), ())), preferred_element_type=jnp.float32
    )


def attend_kernel(qkv_ref, out_ref):
    sources, _, frames, sites, width = qkv_ref.shape
    rows = sources * frames * sites
    row_site = lax.broadcasted_iota(jnp.int32, (2 * rows, rows), 0) % sites
    col_site = lax.broadcasted_iota(jnp.int32, (2 * rows, rows), 1) % sites
    same_site = row_site == col_site
    low_head = lax.broadcasted_iota(jnp.int32, (rows, LANES), 1) < HD
    for pair in range(width // LANES):
        cols = pl.ds(pair * LANES, LANES)
        query = qkv_ref[:, 0, :, :, cols].reshape(rows, LANES)
        key = qkv_ref[:, 1, :, :, cols].reshape(rows, LANES)
        value = qkv_ref[:, 2, :, :, cols].reshape(rows, LANES)
        zero = jnp.zeros_like(query)
        both = jnp.concatenate(
            [jnp.where(low_head, query, zero), jnp.where(low_head, zero, query)], axis=0
        )
        scores = nt_dot(both, key) * (1.0 / math.sqrt(HD))
        scores = jnp.where(same_site, scores, -jnp.inf)
        expo = jnp.exp(scores - jnp.max(scores, axis=-1, keepdims=True))
        probs = (expo / jnp.sum(expo, axis=-1, keepdims=True)).astype(jnp.bfloat16)
        mixed = jnp.dot(probs, value, preferred_element_type=jnp.float32)
        mixed = jnp.where(low_head, mixed[:rows], mixed[rows:])
        out_ref[:, :, :, cols] = mixed.astype(out_ref.dtype).reshape(
            sources, frames, sites, LANES
        )


def route_kernel(att_ref, res_ref, gain_ref, target_ref, hidden_ref, rows_ref):
    _, frames, sites, half = att_ref.shape
    groups = att_ref.shape[0] // 2
    tokens = frames * groups * sites
    attended = jnp.concatenate(
        [
            jnp.concatenate(
                [
                    att_ref[2 * group + side, frame].astype(jnp.float32)
                    for frame in range(frames)
                    for group in range(groups)
                ],
                axis=0,
            )
            for side in range(2)
        ],
        axis=1,
    )
    hidden = res_ref[...].reshape(tokens, 2 * half).astype(jnp.float32) + attended
    hidden_ref[...] = hidden
    scale = lax.rsqrt(jnp.mean(hidden * hidden, axis=-1, keepdims=True) + 1e-06)
    normed = (hidden * scale * gain_ref[...]).astype(jnp.bfloat16)
    row = lax.broadcasted_iota(jnp.int32, (rows_ref.shape[0], tokens), 0)
    hit = (row == target_ref[0:1, :]) | (row == target_ref[1:2, :])
    picker = jnp.where(hit, 1.0, 0.0).astype(jnp.bfloat16)
    rows_ref[...] = jnp.dot(picker, normed, preferred_element_type=jnp.float32).astype(
        jnp.bfloat16
    )


def combine_kernel(hidden_ref, rows_ref, target_ref, gate_ref, out_ref):
    tokens = hidden_ref.shape[0]
    returned = rows_ref[...]
    col = lax.broadcasted_iota(jnp.int32, (tokens, returned.shape[0]), 1)
    moved = jnp.zeros(hidden_ref.shape, jnp.float32)
    for choice in range(2):
        target = target_ref[:, choice : choice + 1]
        picker = jnp.where(col == target, 1.0, 0.0).astype(jnp.bfloat16)
        weight = jnp.where(target >= 0, gate_ref[:, choice : choice + 1], 0.0)
        moved = moved + weight * jnp.dot(picker, returned, preferred_element_type=jnp.float32)
    out_ref[...] = (hidden_ref[...] + moved).astype(out_ref.dtype)


def mlp_kernel(index, pieces, *refs):
    rows_in = refs[:pieces]
    gate, up, down, near = refs[pieces : pieces + 4]
    outs = refs[pieces + 4 : 2 * pieces + 4]
    rows_buf, weight_buf, row_sem, weight_sem = refs[2 * pieces + 4 :]
    count = outs[0].shape[0]
    row_copies = [
        pltpu.make_async_copy(
            rows_in[i], rows_buf.at[pl.ds(i * count, count)], row_sem.at[i]
        )
        for i in range(pieces)
    ]
    sources = (
        gate.at[index],
        up.at[index],
        near.at[0],
        near.at[1],
        down.at[index],
        near.at[2],
    )
    weight_copies = [
        pltpu.make_async_copy(source, weight_buf.at[i], weight_sem.at[i])
        for i, source in enumerate(sources)
    ]
    for copy in row_copies + weight_copies:
        copy.start()
    for copy in row_copies:
        copy.wait()
    rows = rows_buf[...]
    actives = []
    for slice_index in range(2):
        weight_copies[2 * slice_index].wait()
        gate_val = nt_dot(rows, weight_buf[2 * slice_index])
        weight_copies[2 * slice_index + 1].wait()
        up_val = nt_dot(rows, weight_buf[2 * slice_index + 1])
        actives.append(
            (gate_val / (1.0 + jnp.exp(-gate_val)) * up_val).astype(jnp.bfloat16)
        )
    weight_copies[4].wait()
    total = jnp.dot(actives[0], weight_buf[4], preferred_element_type=jnp.float32)
    weight_copies[5].wait()
    total = total + jnp.dot(actives[1], weight_buf[5], preferred_element_type=jnp.float32)
    for i in range(pieces):
        outs[i][...] = total[i * count : (i + 1) * count].astype(outs[i].dtype)


def mlp(pieces, index, gate, up, down, near):
    count, width = pieces[0].shape
    hidden_units = gate.shape[1]
    anywhere = pl.BlockSpec(memory_space=pl.ANY)
    out = jax.ShapeDtypeStruct((count, width), jnp.bfloat16)
    return pl.pallas_call(
        lambda *refs: mlp_kernel(index, len(pieces), *refs),
        in_specs=[anywhere] * (len(pieces) + 4),
        out_shape=tuple(out for _ in pieces),
        scratch_shapes=[
            pltpu.VMEM((len(pieces) * count, width), jnp.bfloat16),
            pltpu.VMEM((6, hidden_units, width), jnp.bfloat16),
            pltpu.SemaphoreType.DMA((len(pieces),)),
            pltpu.SemaphoreType.DMA((6,)),
        ],
        name="mlp",
    )(*pieces, gate, up, down, near)


def pack_kernel(index, gate, up, down, out_ref, sem):
    parts = 4
    block = gate.shape[1] // parts
    copies = []
    for i, source in enumerate((gate, up, down)):
        for j in range(parts):
            cut = pl.ds(j * block, block)
            copies.append(
                pltpu.make_async_copy(
                    source.at[index, cut], out_ref.at[i, cut], sem.at[i * parts + j]
                )
            )
    for copy in copies:
        copy.start()
    for copy in copies:
        copy.wait()


def pack(index, gate, up, down):
    anywhere = pl.BlockSpec(memory_space=pl.ANY)
    return pl.pallas_call(
        lambda *refs: pack_kernel(index, *refs),
        in_specs=[anywhere] * 3,
        out_specs=anywhere,
        out_shape=jax.ShapeDtypeStruct((3, *gate.shape[1:]), gate.dtype),
        scratch_shapes=[pltpu.SemaphoreType.DMA((12,))],
        name="pack",
    )(gate, up, down)


def hop(sizes, move):
    count_y, count_z, count_x = sizes

    def index(y, c, z, x):
        return (
            ((y % count_y) * 2 + c) * (count_z * count_x)
            + (z % count_z) * count_x
            + x % count_x
        )

    return [
        (index(y, c, z, x), index(*move(y, c, z, x)))
        for y in range(count_y)
        for c in range(2)
        for z in range(count_z)
        for x in range(count_x)
    ]


def block(
    query_key_value, residual, norm_gain, expert_ids, route_gates, slot_index, w_gate, w_up, w_down
):
    frames_local, sites_local, model_width = residual.shape
    groups = lax.axis_size("ep")
    halves = 2
    site_groups = sites_local // SITE_GROUP
    assert site_groups * halves == groups
    half = model_width // halves
    tokens = frames_local * sites_local
    experts_local = w_gate.shape[0]
    experts_all = experts_local * groups
    capacity = 2 * tokens // experts_all
    bf16 = jnp.bfloat16

    spread = query_key_value.reshape(
        frames_local, site_groups, SITE_GROUP, 3, halves, half
    ).transpose(1, 4, 3, 0, 2, 5)
    spread = spread.reshape(groups, 3, frames_local, SITE_GROUP, half)
    gate = w_gate.transpose(0, 2, 1)
    up = w_up.transpose(0, 2, 1)
    together = lax.all_to_all(spread, "ep", split_axis=0, concat_axis=0, tiled=True)
    mixed = pl.pallas_call(
        attend_kernel,
        out_shape=jax.ShapeDtypeStruct((groups, frames_local, SITE_GROUP, half), bf16),
        name="attend",
    )(together)
    attended = lax.all_to_all(mixed, "ep", split_axis=0, concat_axis=0, tiled=True)

    sizes = (groups // 2, SIDE, lax.axis_size("tp") // SIDE)

    def along_x(steps):
        return hop(sizes, lambda y, c, z, x: (y, c, z, x + steps))

    def along_z(steps):
        return hop(sizes, lambda y, c, z, x: (y, c, z + steps, x))

    def send(value, pairs):
        return lax.ppermute(value, ("ep", "tp"), pairs)

    packed_a = pack(0, gate, up, w_down)
    packed_b = pack(1, gate, up, w_down)
    near_a = send(packed_a, hop(sizes, lambda y, c, z, x: (y, c, z, x - 1 + 2 * c)))
    near_b = send(packed_b, hop(sizes, lambda y, c, z, x: (y, c, z - 1 + 2 * c, x)))
    near = [near_a, near_b]

    target = jnp.where(slot_index >= 0, expert_ids * capacity + slot_index, -1)
    target = target.reshape(tokens, 2)
    gates = route_gates.reshape(tokens, 2)
    slots = experts_all * capacity
    hidden, rows = pl.pallas_call(
        route_kernel,
        out_shape=(
            jax.ShapeDtypeStruct((tokens, model_width), jnp.float32),
            jax.ShapeDtypeStruct((slots, model_width), bf16),
        ),
        name="route",
    )(attended, residual, norm_gain.reshape(1, model_width), target.T)
    arrived = lax.all_to_all(
        rows.reshape(groups, experts_local, capacity, model_width),
        "ep",
        split_axis=0,
        concat_axis=0,
        tiled=True,
    )
    part_rows = groups * capacity
    mine = [arrived[:, e].reshape(part_rows, model_width) for e in range(2)]
    far = (along_x, along_z)
    ring = (along_z, along_x)
    here = []
    for e in range(2):
        here.append(jnp.concatenate([mine[e], send(mine[e], far[e](2))]))

    def send_all(values, steps):
        out = []
        for e in range(2):
            out.append(send(values[e], ring[e](steps)))
        return out

    def run(e, pieces):
        return mlp(pieces, e, gate, up, w_down, near[e])

    ahead = send_all(here, 1)
    behind = send_all(here, -1)
    parts = [list(run(e, [here[e]])) for e in range(2)]
    parts, ahead, behind = lax.optimization_barrier((parts, ahead, behind))
    from_ahead = send_all([rows_in[:part_rows] for rows_in in ahead], 1)
    from_behind = send_all([rows_in[part_rows:] for rows_in in behind], -1)
    across = [jnp.concatenate([from_ahead[e], from_behind[e]]) for e in range(2)]
    done = parts
    for e in range(2):
        rows_in, done = lax.optimization_barrier(([ahead[e], behind[e]], done))
        done = run(e, rows_in)
        for part, steps in ((done[0], -1), (done[1], 1)):
            parts[e].append(send(part, ring[e](steps)))
    for e in range(2):
        rows_in, done = lax.optimization_barrier((across[e], done))
        done = run(e, [rows_in])
        parts[e].append(send(done[0], ring[e](2)))

    def add(pieces):
        total = pieces[0].astype(jnp.float32)
        for piece in pieces[1:]:
            total = total + piece.astype(jnp.float32)
        return total.astype(bf16)

    summed = []
    for e in range(2):
        opposite = add([part[part_rows:] for part in parts[e]])
        summed.append(add([part[:part_rows] for part in parts[e]] + [send(opposite, far[e](2))]))
    ready = jnp.stack([part.reshape(groups, capacity, model_width) for part in summed], axis=1)
    back = lax.all_to_all(ready, "ep", split_axis=0, concat_axis=0, tiled=True)
    combined = pl.pallas_call(
        combine_kernel,
        out_shape=jax.ShapeDtypeStruct((tokens, model_width), bf16),
        name="combine",
    )(hidden, back.reshape(slots, model_width), target, gates)
    return combined.reshape(frames_local, sites_local, model_width)


def solution(mesh):
    return jax.shard_map(
        block,
        mesh=mesh,
        in_specs=(
            P("ep", "tp", None, None),
            P("ep", "tp", None),
            P(),
            P("ep", "tp", None),
            P("ep", "tp", None),
            P("ep", "tp", None),
            P("ep", None, "tp"),
            P("ep", None, "tp"),
            P("ep", "tp", None),
        ),
        out_specs=P("ep", "tp", None),
        check_vma=False,
    )
```

profile of v0, /device:TPU:1, one launch (start us, length us, event | category | flops | bytes accessed | tf_op | source)
XLA Modules:
  0.0 545.4 jit_solution(1147064850505137512)
XLA Ops:
  0.0 147.1 %pack.2 = bf16[3,448,1792]{2,1,0:T(8,128)(2,1)} custom-call(bf16[2,448,1792]{2,1,0:T(8,128)(2,1)} %bitcast.21, bf16[2,448,1792]{2,1,0:T(8,128)(2,1)} %bitcast.29, bf16[2,448,1792]{2,1,0:T(8,128)(2,1)} %refs_3_.7), custom_call_target="tpu_custom_call" | custom-call | tf_op jit(solution)/shard_map/pack/pallas_call | solution.py:178
  149.2 147.1 %pack.3 = bf16[3,448,1792]{2,1,0:T(8,128)(2,1)} custom-call(bf16[2,448,1792]{2,1,0:T(8,128)(2,1)} %bitcast.22, bf16[2,448,1792]{2,1,0:T(8,128)(2,1)} %bitcast.30, bf16[2,448,1792]{2,1,0:T(8,128)(2,1)} %refs_3_.7), custom_call_target="tpu_custom_call" | custom-call | tf_op jit(solution)/shard_map/pack/pallas_call | solution.py:178
  298.2 27.7 %all_to_all.20.qkv_ref = bf16[8,3,4,8,896]{4,3,2,1,0:T(8,128)(2,1)} all-to-all(bf16[8,3,4,8,896]{4,3,2,1,0:T(8,128)(2,1)S(1)} %bitcast.37), channel_id=1, replica_groups=mesh['ep'=8,'tp'=16] {'ep'}, dimensions={0} | all-to-all | bytes 2752512 | tf_op jit(solution)/shard_map/all_to_all | solution.py:228
  326.0 4.3 attend.1
  330.3 4.1 all-to-all-start.1
  335.8 7.3 %all-to-all-done.1.att_ref = bf16[8,4,8,896]{3,2,1,0:T(8,128)(2,1)S(1)} async-done(((bf16[8,4,8,896]{3,2,1,0:T(8,128)(2,1)}), bf16[8,4,8,896]{3,2,1,0:T(8,128)(2,1)S(1)}, u32[]{:S(2)}, u32[]{:S(2)}) %all-to-all-start.1) | async-done | bytes 458784 | tf_op jit(solution)/shard_map/all_to_all | solution.py:234
  343.9 2.7 route.1
  346.6 18.1 %all_to_all.21 = bf16[8,2,16,1792]{3,2,1,0:T(8,128)(2,1)S(1)} all-to-all(bf16[8,2,16,1792]{3,2,1,0:T(8,128)(2,1)} %bitcast.46), channel_id=1, replica_groups=mesh['ep'=8,'tp'=16] {'ep'}, dimensions={0} | all-to-all | bytes 1835008 | tf_op jit(solution)/shard_map/all_to_all | solution.py:265
  366.1 11.5 %collective-permute-done = bf16[128,1792]{1,0:T(8,128)(2,1)S(1)} collective-permute-done((bf16[128,1792]{1,0:T(8,128)(2,1)S(1)}, bf16[128,1792]{1,0:T(8,128)(2,1)S(1)}, u32[]{:S(2)}, u32[]{:S(2)}) %collective-permute-start) | collective-permute-done | bytes 458784 | tf_op jit(solution)/shard_map/ppermute | solution.py:245
  377.8 2.7 collective-permute-start.6
  383.3 8.6 %mlp.6 = bf16[256,1792]{1,0:T(8,128)(2,1)} custom-call(bf16[256,1792]{1,0:T(8,128)(2,1)} %copy-done.1, bf16[2,448,1792]{2,1,0:T(8,128)(2,1)} %bitcast.23, bf16[2,448,1792]{2,1,0:T(8,128)(2,1)} %bitcast.31, bf16[2,448,1792]{2,1,0:T(8,128)(2,1)} %refs_3_.7, bf16[3,448,1792]{2,1,0:T(8,128)(2,1)} %collective-permute-done.1.refs_4_.refs_5_), custom_call_target="tpu_custom_call" | custom-call | tf_op jit(solution)/shard_map/mlp/pallas_call | solution.py:144
  391.9 8.6 %mlp.7 = bf16[256,1792]{1,0:T(8,128)(2,1)} custom-call(bf16[256,1792]{1,0:T(8,128)(2,1)} %copy-done.2, bf16[2,448,1792]{2,1,0:T(8,128)(2,1)} %bitcast.24, bf16[2,448,1792]{2,1,0:T(8,128)(2,1)} %bitcast.32, bf16[2,448,1792]{2,1,0:T(8,128)(2,1)} %refs_3_.7, bf16[3,448,1792]{2,1,0:T(8,128)(2,1)} %collective-permute-done.3.refs_4_.refs_5_), custom_call_target="tpu_custom_call" | custom-call | tf_op jit(solution)/shard_map/mlp/pallas_call | solution.py:144
  411.0 12.3 %mlp.8 = (bf16[256,1792]{1,0:T(8,128)(2,1)}, bf16[256,1792]{1,0:T(8,128)(2,1)}) custom-call(bf16[256,1792]{1,0:T(8,128)(2,1)} %copy-done.5, bf16[256,1792]{1,0:T(8,128)(2,1)} %collective-permute-done.6.refs_1_, bf16[2,448,1792]{2,1,0:T(8,128)(2,1)} %bitcast.25, bf16[2,448,1792]{2,1,0:T(8,128)(2,1)} %bitcast.33, bf16[2,448,1792]{2,1,0:T(8,128)(2,1)} %refs_3_.7, ...), custom_call_target="tpu_custom_call" | custom-call | tf_op jit(solution)/shard_map/mlp/pallas_call | solution.py:144
  423.3 12.3 %mlp.9 = (bf16[256,1792]{1,0:T(8,128)(2,1)}, bf16[256,1792]{1,0:T(8,128)(2,1)}) custom-call(bf16[256,1792]{1,0:T(8,128)(2,1)} %collective-permute-done.5.refs_0_, bf16[256,1792]{1,0:T(8,128)(2,1)} %collective-permute-done.7.refs_1_, bf16[2,448,1792]{2,1,0:T(8,128)(2,1)} %bitcast.26, bf16[2,448,1792]{2,1,0:T(8,128)(2,1)} %bitcast.34, ...), custom_call_target="tpu_custom_call" | custom-call | tf_op jit(solution)/shard_map/mlp/pallas_call | solution.py:144
  435.7 3.0 collective-permute-start.14
  440.7 8.6 %mlp.10 = bf16[256,1792]{1,0:T(8,128)(2,1)} custom-call(bf16[256,1792]{1,0:T(8,128)(2,1)} %pad_maximum_fusion.2.refs_0_, bf16[2,448,1792]{2,1,0:T(8,128)(2,1)} %bitcast.27, bf16[2,448,1792]{2,1,0:T(8,128)(2,1)} %bitcast.35, bf16[2,448,1792]{2,1,0:T(8,128)(2,1)} %refs_3_.7, bf16[3,448,1792]{2,1,0:T(8,128)(2,1)} %collective-permute-done.1.refs_4_.refs_5_), custom_call_target="tpu_custom_call" | custom-call | tf_op jit(solution)/shard_map/mlp/pallas_call | solution.py:144
  450.4 8.7 %mlp.11 = bf16[256,1792]{1,0:T(8,128)(2,1)} custom-call(bf16[256,1792]{1,0:T(8,128)(2,1)} %pad_maximum_fusion.3.refs_0_, bf16[2,448,1792]{2,1,0:T(8,128)(2,1)} %bitcast.28, bf16[2,448,1792]{2,1,0:T(8,128)(2,1)} %bitcast.36, bf16[2,448,1792]{2,1,0:T(8,128)(2,1)} %refs_3_.7, bf16[3,448,1792]{2,1,0:T(8,128)(2,1)} %collective-permute-done.3.refs_4_.refs_5_), custom_call_target="tpu_custom_call" | custom-call | tf_op jit(solution)/shard_map/mlp/pallas_call | solution.py:144
  460.1 2.7 collective-permute-start.8
  462.7 15.3 %collective-permute-done.18 = bf16[256,1792]{1,0:T(8,128)(2,1)S(1)} collective-permute-done((bf16[256,1792]{1,0:T(8,128)(2,1)}, bf16[256,1792]{1,0:T(8,128)(2,1)S(1)}, u32[]{:S(2)}, u32[]{:S(2)}) %collective-permute-start.18) | collective-permute-done | bytes 917536 | tf_op jit(solution)/shard_map/ppermute | solution.py:245
  478.9 19.3 %collective-permute-done.12 = bf16[256,1792]{1,0:T(8,128)(2,1)S(1)} collective-permute-done((bf16[256,1792]{1,0:T(8,128)(2,1)}, bf16[256,1792]{1,0:T(8,128)(2,1)S(1)}, u32[]{:S(2)}, u32[]{:S(2)}) %collective-permute-start.12) | collective-permute-done | bytes 917536 | tf_op jit(solution)/shard_map/ppermute | solution.py:245
  500.6 7.4 %collective-permute-done.19 = bf16[128,1792]{1,0:T(8,128)(2,1)S(1)} collective-permute-done((bf16[128,1792]{1,0:T(8,128)(2,1)S(1)}, bf16[128,1792]{1,0:T(8,128)(2,1)S(1)}, u32[]{:S(2)}, u32[]{:S(2)}) %collective-permute-start.19) | collective-permute-done | bytes 458784 | tf_op jit(solution)/shard_map/ppermute | solution.py:245
  509.7 18.5 %all-to-all-start.3 = ((bf16[8,2,16,1792]{3,2,1,0:T(8,128)(2,1)}), bf16[8,2,16,1792]{3,2,1,0:T(8,128)(2,1)S(1)}, u32[]{:S(2)}, u32[]{:S(2)}) async-start(bf16[8,2,16,1792]{3,2,1,0:T(8,128)(2,1)} %pad_maximum_fusion.4), calls=%async_computation.3 | async-start | bytes 1835008 | tf_op jit(solution)/shard_map/all_to_all | solution.py:318
  528.9 12.9 %all-to-all-done.3 = bf16[8,2,16,1792]{3,2,1,0:T(8,128)(2,1)S(1)} async-done(((bf16[8,2,16,1792]{3,2,1,0:T(8,128)(2,1)}), bf16[8,2,16,1792]{3,2,1,0:T(8,128)(2,1)S(1)}, u32[]{:S(2)}, u32[]{:S(2)}) %all-to-all-start.3) | async-done | bytes 917536 | tf_op jit(solution)/shard_map/all_to_all | solution.py:318
  542.7 2.7 combine.1
  (79 shorter events, 31.7 us)
Async XLA Ops:
  147.1 151.0 %copy-start.7 = (bf16[4,32,3,1792]{3,1,2,0:T(8,128)(2,1)S(1)}, bf16[4,32,3,1792]{3,1,2,0:T(8,128)(2,1)}, u32[]{:S(2)}) copy-start(bf16[4,32,3,1792]{3,1,2,0:T(8,128)(2,1)} %param.9) | copy-start | bytes 4128772
  147.1 233.4 %collective-permute-start.1 = (bf16[3,448,1792]{2,1,0:T(8,128)(2,1)}, bf16[3,448,1792]{2,1,0:T(8,128)(2,1)}, u32[]{:S(2)}, u32[]{:S(2)}) collective-permute-start(bf16[3,448,1792]{2,1,0:T(8,128)(2,1)} %pack.2), channel_id=1, source_target_pairs={{0,3},{1,0},{2,1},{3,2},{4,7},{5,4},{6,5},{7,6},{8,11},{9,8},{10,9... | collective-permute-start | bytes 14450696 | tf_op jit(solution)/shard_map/ppermute | solution.py:245
  296.4 95.5 %collective-permute-start.3 = (bf16[3,448,1792]{2,1,0:T(8,128)(2,1)}, bf16[3,448,1792]{2,1,0:T(8,128)(2,1)}, u32[]{:S(2)}, u32[]{:S(2)}) collective-permute-start(bf16[3,448,1792]{2,1,0:T(8,128)(2,1)} %pack.3), channel_id=1, source_target_pairs={{0,12},{1,13},{2,14},{3,15},{4,0},{5,1},{6,2},{7,3},{8,4},{9,5},{1... | collective-permute-start | bytes 14450696 | tf_op jit(solution)/shard_map/ppermute | solution.py:245
  330.3 12.8 %all-to-all-start.1 = ((bf16[8,4,8,896]{3,2,1,0:T(8,128)(2,1)}), bf16[8,4,8,896]{3,2,1,0:T(8,128)(2,1)S(1)}, u32[]{:S(2)}, u32[]{:S(2)}) async-start(bf16[8,4,8,896]{3,2,1,0:T(8,128)(2,1)} %attend.1), calls=%async_computation.1 | async-start | bytes 917504 | tf_op jit(solution)/shard_map/all_to_all | solution.py:234
  364.8 12.8 %collective-permute-start = (bf16[128,1792]{1,0:T(8,128)(2,1)S(1)}, bf16[128,1792]{1,0:T(8,128)(2,1)S(1)}, u32[]{:S(2)}, u32[]{:S(2)}) collective-permute-start(bf16[128,1792]{1,0:T(8,128)(2,1)S(1)} %bitcast.41), channel_id=1, source_target_pairs={{0,2},{1,3},{2,0},{3,1},{4,6},{5,7},{6,4},{7,5},{8,10},{9,11},{10,... | collective-permute-start | bytes 1376264 | tf_op jit(solution)/shard_map/ppermute | solution.py:245
  365.4 15.0 %collective-permute-start.2 = (bf16[128,1792]{1,0:T(8,128)(2,1)S(1)}, bf16[128,1792]{1,0:T(8,128)(2,1)S(1)}, u32[]{:S(2)}, u32[]{:S(2)}) collective-permute-start(bf16[128,1792]{1,0:T(8,128)(2,1)S(1)} %bitcast.39), channel_id=1, source_target_pairs={{0,8},{1,9},{2,10},{3,11},{4,12},{5,13},{6,14},{7,15},{8,0},{9,1},... | collective-permute-start | bytes 1376264 | tf_op jit(solution)/shard_map/ppermute | solution.py:245
  377.7 22.8 %collective-permute-start.4 = (bf16[256,1792]{1,0:T(8,128)(2,1)S(1)}, bf16[256,1792]{1,0:T(8,128)(2,1)S(1)}, u32[]{:S(2)}, u32[]{:S(2)}) collective-permute-start(bf16[256,1792]{1,0:T(8,128)(2,1)S(1)} %pad_maximum_fusion.refs_0_), channel_id=1, source_target_pairs={{0,4},{1,5},{2,6},{3,7},{4,8},{5,9},{6,10},{7,11},{8,12},{9,13},{1... | collective-permute-start | bytes 2752520 | tf_op jit(solution)/shard_map/ppermute | solution.py:245
  377.8 23.8 %collective-permute-start.6 = (bf16[256,1792]{1,0:T(8,128)(2,1)S(1)}, bf16[256,1792]{1,0:T(8,128)(2,1)}, u32[]{:S(2)}, u32[]{:S(2)}) collective-permute-start(bf16[256,1792]{1,0:T(8,128)(2,1)S(1)} %pad_maximum_fusion.refs_0_), channel_id=1, source_target_pairs={{0,12},{1,13},{2,14},{3,15},{4,0},{5,1},{6,2},{7,3},{8,4},{9,5},{1... | collective-permute-start | bytes 2752520 | tf_op jit(solution)/shard_map/ppermute | solution.py:245
  380.5 21.0 %collective-permute-start.5 = (bf16[256,1792]{1,0:T(8,128)(2,1)S(1)}, bf16[256,1792]{1,0:T(8,128)(2,1)}, u32[]{:S(2)}, u32[]{:S(2)}) collective-permute-start(bf16[256,1792]{1,0:T(8,128)(2,1)S(1)} %pad_maximum_fusion.1.refs_0_), channel_id=1, source_target_pairs={{0,1},{1,2},{2,3},{3,0},{4,5},{5,6},{6,7},{7,4},{8,9},{9,10},{10,1... | collective-permute-start | bytes 2752520 | tf_op jit(solution)/shard_map/ppermute | solution.py:245
  380.6 20.9 %collective-permute-start.7 = (bf16[256,1792]{1,0:T(8,128)(2,1)S(1)}, bf16[256,1792]{1,0:T(8,128)(2,1)}, u32[]{:S(2)}, u32[]{:S(2)}) collective-permute-start(bf16[256,1792]{1,0:T(8,128)(2,1)S(1)} %pad_maximum_fusion.1.refs_0_), channel_id=1, source_target_pairs={{0,3},{1,0},{2,1},{3,2},{4,7},{5,4},{6,5},{7,6},{8,11},{9,8},{10,9... | collective-permute-start | bytes 2752520 | tf_op jit(solution)/shard_map/ppermute | solution.py:245
  402.6 33.1 %collective-permute-start.11 = (bf16[128,1792]{1,0:T(8,128)(2,1)S(1)}, bf16[128,1792]{1,0:T(8,128)(2,1)S(1)}, u32[]{:S(2)}, u32[]{:S(2)}) collective-permute-start(bf16[128,1792]{1,0:T(8,128)(2,1)S(1)} %slice.72), channel_id=1, source_target_pairs={{0,12},{1,13},{2,14},{3,15},{4,0},{5,1},{6,2},{7,3},{8,4},{9,5},{1... | collective-permute-start | bytes 1376264 | tf_op jit(solution)/shard_map/ppermute | solution.py:245
  403.7 35.0 %collective-permute-start.10 = (bf16[128,1792]{1,0:T(8,128)(2,1)}, bf16[128,1792]{1,0:T(8,128)(2,1)}, u32[]{:S(2)}, u32[]{:S(2)}) collective-permute-start(bf16[128,1792]{1,0:T(8,128)(2,1)} %slice.71), channel_id=1, source_target_pairs={{0,4},{1,5},{2,6},{3,7},{4,8},{5,9},{6,10},{7,11},{8,12},{9,13},{1... | collective-permute-start | bytes 1376264 | tf_op jit(solution)/shard_map/ppermute | solution.py:245
  406.7 42.6 %collective-permute-start.17 = (bf16[128,1792]{1,0:T(8,128)(2,1)}, bf16[128,1792]{1,0:T(8,128)(2,1)S(1)}, u32[]{:S(2)}, u32[]{:S(2)}) collective-permute-start(bf16[128,1792]{1,0:T(8,128)(2,1)} %slice.82), channel_id=1, source_target_pairs={{0,3},{1,0},{2,1},{3,2},{4,7},{5,4},{6,5},{7,6},{8,11},{9,8},{10,9... | collective-permute-start | bytes 1376264 | tf_op jit(solution)/shard_map/ppermute | solution.py:245
  411.0 38.4 %collective-permute-start.16 = (bf16[128,1792]{1,0:T(8,128)(2,1)}, bf16[128,1792]{1,0:T(8,128)(2,1)S(1)}, u32[]{:S(2)}, u32[]{:S(2)}) collective-permute-start(bf16[128,1792]{1,0:T(8,128)(2,1)} %slice.81), channel_id=1, source_target_pairs={{0,1},{1,2},{2,3},{3,0},{4,5},{5,6},{6,7},{7,4},{8,9},{9,10},{10,1... | collective-permute-start | bytes 1376264 | tf_op jit(solution)/shard_map/ppermute | solution.py:245
  435.6 27.1 %collective-permute-start.15 = (bf16[256,1792]{1,0:T(8,128)(2,1)}, bf16[256,1792]{1,0:T(8,128)(2,1)S(1)}, u32[]{:S(2)}, u32[]{:S(2)}) collective-permute-start(bf16[256,1792]{1,0:T(8,128)(2,1)} %get-tuple-element.38), channel_id=1, source_target_pairs={{0,1},{1,2},{2,3},{3,0},{4,5},{5,6},{6,7},{7,4},{8,9},{9,10},{10,1... | collective-permute-start | bytes 2752520 | tf_op jit(solution)/shard_map/ppermute | solution.py:245
  435.7 27.0 %collective-permute-start.14 = (bf16[256,1792]{1,0:T(8,128)(2,1)}, bf16[256,1792]{1,0:T(8,128)(2,1)S(1)}, u32[]{:S(2)}, u32[]{:S(2)}) collective-permute-start(bf16[256,1792]{1,0:T(8,128)(2,1)} %get-tuple-element.37), channel_id=1, source_target_pairs={{0,3},{1,0},{2,1},{3,2},{4,7},{5,4},{6,5},{7,6},{8,11},{9,8},{10,9... | collective-permute-start | bytes 2752520 | tf_op jit(solution)/shard_map/ppermute | solution.py:245
  459.1 39.1 %copy-start.3 = (bf16[256,1792]{1,0:T(8,128)(2,1)S(1)}, bf16[256,1792]{1,0:T(8,128)(2,1)}, u32[]{:S(2)}) copy-start(bf16[256,1792]{1,0:T(8,128)(2,1)} %mlp.6) | copy-start | bytes 2752516
  459.1 18.9 %collective-permute-start.18 = (bf16[256,1792]{1,0:T(8,128)(2,1)}, bf16[256,1792]{1,0:T(8,128)(2,1)S(1)}, u32[]{:S(2)}, u32[]{:S(2)}) collective-permute-start(bf16[256,1792]{1,0:T(8,128)(2,1)} %mlp.11), channel_id=1, source_target_pairs={{0,2},{1,3},{2,0},{3,1},{4,6},{5,7},{6,4},{7,5},{8,10},{9,11},{10,... | collective-permute-start | bytes 2752520 | tf_op jit(solution)/shard_map/ppermute | solution.py:245
  460.0 18.9 %collective-permute-start.9 = (bf16[256,1792]{1,0:T(8,128)(2,1)}, bf16[256,1792]{1,0:T(8,128)(2,1)S(1)}, u32[]{:S(2)}, u32[]{:S(2)}) collective-permute-start(bf16[256,1792]{1,0:T(8,128)(2,1)} %get-tuple-element.32), channel_id=1, source_target_pairs={{0,4},{1,5},{2,6},{3,7},{4,8},{5,9},{6,10},{7,11},{8,12},{9,13},{1... | collective-permute-start | bytes 2752520 | tf_op jit(solution)/shard_map/ppermute | solution.py:245
  460.1 18.9 %collective-permute-start.8 = (bf16[256,1792]{1,0:T(8,128)(2,1)}, bf16[256,1792]{1,0:T(8,128)(2,1)S(1)}, u32[]{:S(2)}, u32[]{:S(2)}) collective-permute-start(bf16[256,1792]{1,0:T(8,128)(2,1)} %get-tuple-element.31), channel_id=1, source_target_pairs={{0,12},{1,13},{2,14},{3,15},{4,0},{5,1},{6,2},{7,3},{8,4},{9,5},{1... | collective-permute-start | bytes 2752520 | tf_op jit(solution)/shard_map/ppermute | solution.py:245
  462.7 35.5 %collective-permute-start.12 = (bf16[256,1792]{1,0:T(8,128)(2,1)}, bf16[256,1792]{1,0:T(8,128)(2,1)S(1)}, u32[]{:S(2)}, u32[]{:S(2)}) collective-permute-start(bf16[256,1792]{1,0:T(8,128)(2,1)} %mlp.10), channel_id=1, source_target_pairs={{0,8},{1,9},{2,10},{3,11},{4,12},{5,13},{6,14},{7,15},{8,0},{9,1},... | collective-permute-start | bytes 2752520 | tf_op jit(solution)/shard_map/ppermute | solution.py:245
  478.3 29.8 %collective-permute-start.19 = (bf16[128,1792]{1,0:T(8,128)(2,1)S(1)}, bf16[128,1792]{1,0:T(8,128)(2,1)S(1)}, u32[]{:S(2)}, u32[]{:S(2)}) collective-permute-start(bf16[128,1792]{1,0:T(8,128)(2,1)S(1)} %add_convert_fusion.1), channel_id=1, source_target_pairs={{0,8},{1,9},{2,10},{3,11},{4,12},{5,13},{6,14},{7,15},{8,0},{9,1},... | collective-permute-start | bytes 1376264 | tf_op jit(solution)/shard_map/ppermute | solution.py:245
  498.4 9.9 %collective-permute-start.13 = (bf16[128,1792]{1,0:T(8,128)(2,1)S(1)}, bf16[128,1792]{1,0:T(8,128)(2,1)S(1)}, u32[]{:S(2)}, u32[]{:S(2)}) collective-permute-start(bf16[128,1792]{1,0:T(8,128)(2,1)S(1)} %add_convert_fusion.3), channel_id=1, source_target_pairs={{0,2},{1,3},{2,0},{3,1},{4,6},{5,7},{6,4},{7,5},{8,10},{9,11},{10,... | collective-permute-start | bytes 1376264 | tf_op jit(solution)/shard_map/ppermute | solution.py:245
  509.7 32.0 %all-to-all-start.3 = ((bf16[8,2,16,1792]{3,2,1,0:T(8,128)(2,1)}), bf16[8,2,16,1792]{3,2,1,0:T(8,128)(2,1)S(1)}, u32[]{:S(2)}, u32[]{:S(2)}) async-start(bf16[8,2,16,1792]{3,2,1,0:T(8,128)(2,1)} %pad_maximum_fusion.4), calls=%async_computation.3 | async-start | bytes 1835008 | tf_op jit(solution)/shard_map/all_to_all | solution.py:318
  (11 other events, 132.5 us)
where the time goes:
time: 546 us; the launch traced here: 545 us
  Pallas kernels  363 us (66%)
  waiting for transfers between devices  74.6 us (14%)
  starting transfers between devices  46.7 us (9%)
  blocking collectives  45.9 us (8%)
  local copies, waits for them, and re-layouts  9.59 us (2%)
    pallas_call x2, Pallas kernels, pack(): pl.pallas_call(lambda *refs: pack_kernel(index, *refs), in_specs=[anywher...  294 us
    pallas_call x6, Pallas kernels, mlp(): pl.pallas_call(lambda *refs: mlp_kernel(index, len(pieces), *refs), in_sp...  59.1 us
    ppermute x20, waiting for transfers between devices, send(): return lax.ppermute(value, ('ep', 'tp'), pairs)  54.4 us
    all_to_all x1, blocking collectives, block(): lax.all_to_all(spread, 'ep', split_axis=0, concat_axis=0, tiled=True)  27.7 us
    ppermute x20, starting transfers between devices, send(): return lax.ppermute(value, ('ep', 'tp'), pairs)  24.1 us
    all_to_all x1, starting transfers between devices, block(): back = lax.all_to_all(ready, 'ep', split_axis=0, concat_axis=0, tiled=True)  18.5 us
    all_to_all x1, blocking collectives, block(): lax.all_to_all(rows.reshape(groups, experts_local, capacity, model_width)...  18.1 us
    all_to_all x1, waiting for transfers between devices, block(): back = lax.all_to_all(ready, 'ep', split_axis=0, concat_axis=0, tiled=True)  12.9 us
  transfers between devices with their start and end apart: 22, of which 7 were waited for; matrix products, arithmetic and copies ran while one was open for 2% of the time, Pallas kernels for 39%

commit v1 on v0

--- a/solution.py
+++ b/solution.py
@@ -91,98 +91,80 @@
 
 
 def mlp_kernel(index, pieces, *refs):
-    rows_in = refs[:pieces]
     gate, up, down, near = refs[pieces : pieces + 4]
-    outs = refs[pieces + 4 : 2 * pieces + 4]
-    rows_buf, weight_buf, row_sem, weight_sem = refs[2 * pieces + 4 :]
-    count = outs[0].shape[0]
-    row_copies = [
-        pltpu.make_async_copy(
-            rows_in[i], rows_buf.at[pl.ds(i * count, count)], row_sem.at[i]
-        )
-        for i in range(pieces)
-    ]
-    sources = (
-        gate.at[index],
-        up.at[index],
-        near.at[0],
-        near.at[1],
-        down.at[index],
-        near.at[2],
-    )
-    weight_copies = [
-        pltpu.make_async_copy(source, weight_buf.at[i], weight_sem.at[i])
-        for i, source in enumerate(sources)
-    ]
-    for copy in row_copies + weight_copies:
-        copy.start()
-    for copy in row_copies:
-        copy.wait()
-    rows = rows_buf[...]
-    actives = []
-    for slice_index in range(2):
-        weight_copies[2 * slice_index].wait()
-        gate_val = nt_dot(rows, weight_buf[2 * slice_index])
-        weight_copies[2 * slice_index + 1].wait()
-        up_val = nt_dot(rows, weight_buf[2 * slice_index + 1])
-        actives.append(
-            (gate_val / (1.0 + jnp.exp(-gate_val)) * up_val).astype(jnp.bfloat16)
-        )
-    weight_copies[4].wait()
-    total = jnp.dot(actives[0], weight_buf[4], preferred_element_type=jnp.float32)
-    weight_copies[5].wait()
-    total = total + jnp.dot(actives[1], weight_buf[5], preferred_element_type=jnp.float32)
-    for i in range(pieces):
-        outs[i][...] = total[i * count : (i + 1) * count].astype(outs[i].dtype)
+    out = refs[pieces + 4]
+    rows = [ref[...] for ref in refs[:pieces]]
+    rows = rows[0] if pieces == 1 else jnp.concatenate(rows, axis=0)
+    total = None
+    for gate_w, up_w, down_w in (
+        (gate.at[index], up.at[index], down.at[index]),
+        (near.at[0], near.at[1], near.at[2]),
+    ):
+        gate_val = nt_dot(rows, gate_w[...])
+        up_val = nt_dot(rows, up_w[...])
+        active = (gate_val / (1.0 + jnp.exp(-gate_val)) * up_val).astype(jnp.bfloat16)
+        part = jnp.dot(active, down_w[...], preferred_element_type=jnp.float32)
+        total = part if total is None else total + part
+    out[...] = total.astype(out.dtype)
+
+
+def on_chip(count):
+    return [pl.BlockSpec(memory_space=pltpu.VMEM)] * count
+
+
+def grant(mebibytes):
+    return pltpu.CompilerParams(vmem_limit_bytes=mebibytes << 20)
 
 
 def mlp(pieces, index, gate, up, down, near):
-    count, width = pieces[0].shape
-    hidden_units = gate.shape[1]
-    anywhere = pl.BlockSpec(memory_space=pl.ANY)
-    out = jax.ShapeDtypeStruct((count, width), jnp.bfloat16)
+    count = sum(piece.shape[0] for piece in pieces)
     return pl.pallas_call(
         lambda *refs: mlp_kernel(index, len(pieces), *refs),
-        in_specs=[anywhere] * (len(pieces) + 4),
-        out_shape=tuple(out for _ in pieces),
-        scratch_shapes=[
-            pltpu.VMEM((len(pieces) * count, width), jnp.bfloat16),
-            pltpu.VMEM((6, hidden_units, width), jnp.bfloat16),
-            pltpu.SemaphoreType.DMA((len(pieces),)),
-            pltpu.SemaphoreType.DMA((6,)),
-        ],
+        in_specs=on_chip(len(pieces) + 4),
+        out_specs=on_chip(1)[0],
+        out_shape=jax.ShapeDtypeStruct((count, pieces[0].shape[1]), jnp.bfloat16),
+        compiler_params=grant(24),
         name="mlp",
     )(*pieces, gate, up, down, near)
 
 
-def pack_kernel(index, gate, up, down, out_ref, sem):
-    parts = 4
-    block = gate.shape[1] // parts
-    copies = []
+def pack_kernel(index, gate, up, down, out_ref):
     for i, source in enumerate((gate, up, down)):
-        for j in range(parts):
-            cut = pl.ds(j * block, block)
-            copies.append(
-                pltpu.make_async_copy(
-                    source.at[index, cut], out_ref.at[i, cut], sem.at[i * parts + j]
-                )
-            )
+        out_ref[i] = source[index]
+
+
+def pack(index, gate, up, down):
+    return pl.pallas_call(
+        lambda *refs: pack_kernel(index, *refs),
+        in_specs=on_chip(3),
+        out_specs=on_chip(1)[0],
+        out_shape=jax.ShapeDtypeStruct((3, *gate.shape[1:]), gate.dtype),
+        compiler_params=grant(18),
+        name="pack",
+    )(gate, up, down)
+
+
+def land_kernel(source, out_ref, sem):
+    copies = [
+        pltpu.make_async_copy(source.at[i], out_ref.at[i], sem.at[i])
+        for i in range(source.shape[0])
+    ]
     for copy in copies:
         copy.start()
     for copy in copies:
         copy.wait()
 
 
-def pack(index, gate, up, down):
-    anywhere = pl.BlockSpec(memory_space=pl.ANY)
+def land(value):
     return pl.pallas_call(
-        lambda *refs: pack_kernel(index, *refs),
-        in_specs=[anywhere] * 3,
-        out_specs=anywhere,
-        out_shape=jax.ShapeDtypeStruct((3, *gate.shape[1:]), gate.dtype),
-        scratch_shapes=[pltpu.SemaphoreType.DMA((12,))],
-        name="pack",
-    )(gate, up, down)
+        land_kernel,
+        in_specs=[pl.BlockSpec(memory_space=pl.ANY)],
+        out_specs=on_chip(1)[0],
+        out_shape=pltpu.VMEM(value.shape, value.dtype),
+        scratch_shapes=[pltpu.SemaphoreType.DMA((value.shape[0],))],
+        compiler_params=grant(1),
+        name="land",
+    )(value)
 
 
 def hop(sizes, move):
@@ -229,6 +211,9 @@
     mixed = pl.pallas_call(
         attend_kernel,
         out_shape=jax.ShapeDtypeStruct((groups, frames_local, SITE_GROUP, half), bf16),
+        in_specs=on_chip(1),
+        out_specs=on_chip(1)[0],
+        compiler_params=grant(16),
         name="attend",
     )(together)
     attended = lax.all_to_all(mixed, "ep", split_axis=0, concat_axis=0, tiled=True)
@@ -248,7 +233,9 @@
     packed_b = pack(1, gate, up, w_down)
     near_a = send(packed_a, hop(sizes, lambda y, c, z, x: (y, c, z, x - 1 + 2 * c)))
     near_b = send(packed_b, hop(sizes, lambda y, c, z, x: (y, c, z - 1 + 2 * c, x)))
-    near = [near_a, near_b]
+    near = []
+    for value in (near_a, near_b):
+        near.append(land(value))
 
     target = jnp.where(slot_index >= 0, expert_ids * capacity + slot_index, -1)
     target = target.reshape(tokens, 2)
@@ -260,6 +247,9 @@
             jax.ShapeDtypeStruct((tokens, model_width), jnp.float32),
             jax.ShapeDtypeStruct((slots, model_width), bf16),
         ),
+        in_specs=on_chip(4),
+        out_specs=tuple(on_chip(2)),
+        compiler_params=grant(12),
         name="route",
     )(attended, residual, norm_gain.reshape(1, model_width), target.T)
     arrived = lax.all_to_all(
@@ -288,21 +278,22 @@
 
     ahead = send_all(here, 1)
     behind = send_all(here, -1)
-    parts = [list(run(e, [here[e]])) for e in range(2)]
-    parts, ahead, behind = lax.optimization_barrier((parts, ahead, behind))
-    from_ahead = send_all([rows_in[:part_rows] for rows_in in ahead], 1)
-    from_behind = send_all([rows_in[part_rows:] for rows_in in behind], -1)
-    across = [jnp.concatenate([from_ahead[e], from_behind[e]]) for e in range(2)]
-    done = parts
+    done = [run(e, [here[e]]) for e in range(2)]
+    parts = [[part] for part in done]
+    from_ahead, from_behind = [None, None], [None, None]
+    for arrived_rows, relayed, cut, steps in (
+        (ahead, from_ahead, slice(0, part_rows), 1),
+        (behind, from_behind, slice(part_rows, 2 * part_rows), -1),
+    ):
+        for e in range(2):
+            rows_in, done = lax.optimization_barrier((arrived_rows[e], done))
+            relayed[e] = send(rows_in[cut], ring[e](steps))
+            done = run(e, [rows_in])
+            parts[e].append(send(done, ring[e](-steps)))
     for e in range(2):
-        rows_in, done = lax.optimization_barrier(([ahead[e], behind[e]], done))
+        rows_in, done = lax.optimization_barrier(([from_ahead[e], from_behind[e]], done))
         done = run(e, rows_in)
-        for part, steps in ((done[0], -1), (done[1], 1)):
-            parts[e].append(send(part, ring[e](steps)))
-    for e in range(2):
-        rows_in, done = lax.optimization_barrier((across[e], done))
-        done = run(e, [rows_in])
-        parts[e].append(send(done[0], ring[e](2)))
+        parts[e].append(send(done, ring[e](2)))
 
     def add(pieces):
         total = pieces[0].astype(jnp.float32)
@@ -319,6 +310,9 @@
     combined = pl.pallas_call(
         combine_kernel,
         out_shape=jax.ShapeDtypeStruct((tokens, model_width), bf16),
+        in_specs=on_chip(4),
+        out_specs=on_chip(1)[0],
+        compiler_params=grant(12),
         name="combine",
     )(hidden, back.reshape(slots, model_width), target, gates)
     return combined.reshape(frames_local, sites_local, model_width)

time: 546 us -> 222 us (0.41)
  Pallas kernels: 363 us -> 40.3 us
    pallas_call x2 -> x4, Pallas kernels: 294 us -> 9.88 us  [the longest x2 5.06 us: pack(): pl.pallas_call(lambda *refs: pack_kernel(index, *refs), in_specs=on_chip(...]
    pallas_call x6 -> x8, Pallas kernels: 59.1 us -> 25.6 us  [mlp(): pl.pallas_call(lambda *refs: mlp_kernel(index, len(pieces), *refs), in_sp...]
  transfers between devices with their start and end apart: 22 -> 22, of which waited for: 7 -> 11; matrix products, arithmetic and copies ran while one was open for 2% -> 1% of each run, Pallas kernels for 39% -> 17%
where the time goes in v1:
time: 222 us; the launch traced here: 221 us
  waiting for transfers between devices  79.4 us (36%)
  starting transfers between devices  47.9 us (22%)
  blocking collectives  44.8 us (20%)
  Pallas kernels  40.3 us (18%)
  local copies, waits for them, and re-layouts  6.38 us (3%)
    ppermute x20, waiting for transfers between devices, send(): return lax.ppermute(value, ('ep', 'tp'), pairs)  57.4 us
    all_to_all x1, blocking collectives, block(): lax.all_to_all(spread, 'ep', split_axis=0, concat_axis=0, tiled=True)  27.8 us
    pallas_call x8, Pallas kernels, mlp(): pl.pallas_call(lambda *refs: mlp_kernel(index, len(pieces), *refs), in_sp...  25.6 us
    all_to_all x1, starting transfers between devices, block(): back = lax.all_to_all(ready, 'ep', split_axis=0, concat_axis=0, tiled=True)  22.1 us
    ppermute x20, starting transfers between devices, send(): return lax.ppermute(value, ('ep', 'tp'), pairs)  21.6 us
    all_to_all x1, blocking collectives, block(): lax.all_to_all(rows.reshape(groups, experts_local, capacity, model_width)...  17.1 us
    all_to_all x1, waiting for transfers between devices, block(): back = lax.all_to_all(ready, 'ep', split_axis=0, concat_axis=0, tiled=True)  13.5 us
    all_to_all x1, waiting for transfers between devices, block(): lax.all_to_all(mixed, 'ep', split_axis=0, concat_axis=0, tiled=True)  8.47 us
  transfers between devices with their start and end apart: 22, of which 11 were waited for; matrix products, arithmetic and copies ran while one was open for 1% of the time, Pallas kernels for 17%

profile of v1, /device:TPU:1, one launch (start us, length us, event | category | flops | bytes accessed | tf_op | source)
XLA Modules:
  0.0 221.2 jit_solution(4405125666838256185)
XLA Ops:
  14.7 27.8 %all_to_all.20.qkv_ref = bf16[8,3,4,8,896]{4,3,2,1,0:T(8,128)(2,1)S(1)} all-to-all(bf16[8,3,4,8,896]{4,3,2,1,0:T(8,128)(2,1)S(1)} %bitcast.46), channel_id=1, replica_groups=mesh['ep'=8,'tp'=16] {'ep'}, dimensions={0} | all-to-all | bytes 2752512 | tf_op jit(solution)/shard_map/all_to_all | solution.py:210
  42.4 3.0 %attend.1 = bf16[8,4,8,896]{3,2,1,0:T(8,128)(2,1)} custom-call(bf16[8,3,4,8,896]{4,3,2,1,0:T(8,128)(2,1)S(1)} %all_to_all.20.qkv_ref), custom_call_target="tpu_custom_call" | custom-call | tf_op jit(solution)/shard_map/attend/pallas_call | solution.py:211
  45.4 4.1 %all-to-all-start.1 = ((bf16[8,4,8,896]{3,2,1,0:T(8,128)(2,1)}), bf16[8,4,8,896]{3,2,1,0:T(8,128)(2,1)S(1)}, u32[]{:S(2)}, u32[]{:S(2)}) async-start(bf16[8,4,8,896]{3,2,1,0:T(8,128)(2,1)} %attend.1), calls=%async_computation.1 | async-start | bytes 917504 | tf_op jit(solution)/shard_map/all_to_all | solution.py:219
  49.7 8.5 %all-to-all-done.1.att_ref = bf16[8,4,8,896]{3,2,1,0:T(8,128)(2,1)S(1)} async-done(((bf16[8,4,8,896]{3,2,1,0:T(8,128)(2,1)}), bf16[8,4,8,896]{3,2,1,0:T(8,128)(2,1)S(1)}, u32[]{:S(2)}, u32[]{:S(2)}) %all-to-all-start.1) | async-done | bytes 458784 | tf_op jit(solution)/shard_map/all_to_all | solution.py:219
  58.8 17.1 %all_to_all.21 = bf16[8,2,16,1792]{3,2,1,0:T(8,128)(2,1)S(1)} all-to-all(bf16[8,2,16,1792]{3,2,1,0:T(8,128)(2,1)S(1)} %bitcast.42), channel_id=1, replica_groups=mesh['ep'=8,'tp'=16] {'ep'}, dimensions={0} | all-to-all | bytes 1835008 | tf_op jit(solution)/shard_map/all_to_all | solution.py:255
  77.3 11.5 %collective-permute-done = bf16[128,1792]{1,0:T(8,128)(2,1)S(1)} collective-permute-done((bf16[128,1792]{1,0:T(8,128)(2,1)S(1)}, bf16[128,1792]{1,0:T(8,128)(2,1)S(1)}, u32[]{:S(2)}, u32[]{:S(2)}) %collective-permute-start) | collective-permute-done | bytes 458784 | tf_op jit(solution)/shard_map/ppermute | solution.py:230
  91.8 2.6 %collective-permute-start.11 = (bf16[256,1792]{1,0:T(8,128)(2,1)S(1)}, bf16[256,1792]{1,0:T(8,128)(2,1)S(1)}, u32[]{:S(2)}, u32[]{:S(2)}) collective-permute-start(bf16[256,1792]{1,0:T(8,128)(2,1)S(1)} %pad_maximum_fusion.1.refs_0_), channel_id=1, source_target_pairs={{0,3},{1,0},{2,1},{3,2},{4,7},{5,4},{6,5},{7,6},{8,11},{9,8},{10,9... | collective-permute-start | bytes 2752520 | tf_op jit(solution)/shard_map/ppermute | solution.py:230
  96.9 3.2 %mlp.8 = bf16[256,1792]{1,0:T(8,128)(2,1)S(1)} custom-call(bf16[256,1792]{1,0:T(8,128)(2,1)S(1)} %pad_maximum_fusion.refs_0_, bf16[2,448,1792]{2,1,0:T(8,128)(2,1)S(1)} %bitcast.23, bf16[2,448,1792]{2,1,0:T(8,128)(2,1)S(1)} %bitcast.33, bf16[2,448,1792]{2,1,0:T(8,128)(2,1)S(1)} %copy-done.5, bf16[3,448,1792]{2,1,0:T(8,128)(2,1)S(1)} %land.2.refs_4_.refs_5_), custom_call_target="tpu_custom_call" | custom-call | tf_op jit(solution)/shard_map/mlp/pallas_call | solution.py:121
  102.5 3.2 %mlp.9 = bf16[256,1792]{1,0:T(8,128)(2,1)S(1)} custom-call(bf16[256,1792]{1,0:T(8,128)(2,1)S(1)} %pad_maximum_fusion.1.refs_0_, bf16[2,448,1792]{2,1,0:T(8,128)(2,1)S(1)} %bitcast.24, bf16[2,448,1792]{2,1,0:T(8,128)(2,1)S(1)} %bitcast.34, bf16[2,448,1792]{2,1,0:T(8,128)(2,1)S(1)} %copy-done.5, bf16[3,448,1792]{2,1,0:T(8,128)(2,1)S(1)} %land.3.refs_4_.refs_5_), custom_call_target="tpu_custom_call" | custom-call | tf_op jit(solution)/shard_map/mlp/pallas_call | solution.py:121
  105.6 4.6 %collective-permute-done.2.refs_0_ = bf16[256,1792]{1,0:T(8,128)(2,1)S(1)} collective-permute-done((bf16[256,1792]{1,0:T(8,128)(2,1)S(1)}, bf16[256,1792]{1,0:T(8,128)(2,1)S(1)}, u32[]{:S(2)}, u32[]{:S(2)}) %collective-permute-start.2) | collective-permute-done | bytes 917536 | tf_op jit(solution)/shard_map/ppermute | solution.py:230
  110.3 3.2 %mlp.10 = bf16[256,1792]{1,0:T(8,128)(2,1)S(1)} custom-call(bf16[256,1792]{1,0:T(8,128)(2,1)S(1)} %collective-permute-done.2.refs_0_, bf16[2,448,1792]{2,1,0:T(8,128)(2,1)S(1)} %bitcast.25, bf16[2,448,1792]{2,1,0:T(8,128)(2,1)S(1)} %bitcast.35, bf16[2,448,1792]{2,1,0:T(8,128)(2,1)S(1)} %copy-done.5, bf16[3,448,1792]{2,1,0:T(8,128)(2,1)S(1)} %land.2.refs_4_.refs_5_), custom_call_target="tpu_custom_call" | custom-call | tf_op jit(solution)/shard_map/mlp/pallas_call | solution.py:121
  113.5 3.2 %mlp.11 = bf16[256,1792]{1,0:T(8,128)(2,1)S(1)} custom-call(bf16[256,1792]{1,0:T(8,128)(2,1)S(1)} %collective-permute-done.7.refs_0_, bf16[2,448,1792]{2,1,0:T(8,128)(2,1)S(1)} %bitcast.26, bf16[2,448,1792]{2,1,0:T(8,128)(2,1)S(1)} %bitcast.36, bf16[2,448,1792]{2,1,0:T(8,128)(2,1)S(1)} %copy-done.5, bf16[3,448,1792]{2,1,0:T(8,128)(2,1)S(1)} %land.3.refs_4_.refs_5_), custom_call_target="tpu_custom_call" | custom-call | tf_op jit(solution)/shard_map/mlp/pallas_call | solution.py:121
  116.7 3.4 %mlp.12 = bf16[256,1792]{1,0:T(8,128)(2,1)S(1)} custom-call(bf16[256,1792]{1,0:T(8,128)(2,1)S(1)} %collective-permute-done.6.refs_0_, bf16[2,448,1792]{2,1,0:T(8,128)(2,1)S(1)} %bitcast.27, bf16[2,448,1792]{2,1,0:T(8,128)(2,1)S(1)} %bitcast.37, bf16[2,448,1792]{2,1,0:T(8,128)(2,1)S(1)} %copy-done.5, bf16[3,448,1792]{2,1,0:T(8,128)(2,1)S(1)} %land.2.refs_4_.refs_5_), custom_call_target="tpu_custom_call" | custom-call | tf_op jit(solution)/shard_map/mlp/pallas_call | solution.py:121
  120.3 2.7 %collective-permute-start.10 = (bf16[128,1792]{1,0:T(8,128)(2,1)S(1)}, bf16[128,1792]{1,0:T(8,128)(2,1)S(1)}, u32[]{:S(2)}, u32[]{:S(2)}) collective-permute-start(bf16[128,1792]{1,0:T(8,128)(2,1)S(1)} %slice.72), channel_id=1, source_target_pairs={{0,12},{1,13},{2,14},{3,15},{4,0},{5,1},{6,2},{7,3},{8,4},{9,5},{1... | collective-permute-start | bytes 1376264 | tf_op jit(solution)/shard_map/ppermute | solution.py:230
  123.0 2.7 %collective-permute-start.17 = (bf16[128,1792]{1,0:T(8,128)(2,1)S(1)}, bf16[128,1792]{1,0:T(8,128)(2,1)S(1)}, u32[]{:S(2)}, u32[]{:S(2)}) collective-permute-start(bf16[128,1792]{1,0:T(8,128)(2,1)S(1)} %slice.82), channel_id=1, source_target_pairs={{0,3},{1,0},{2,1},{3,2},{4,7},{5,4},{6,5},{7,6},{8,11},{9,8},{10,9... | collective-permute-start | bytes 1376264 | tf_op jit(solution)/shard_map/ppermute | solution.py:230
  125.8 3.2 %mlp.13 = bf16[256,1792]{1,0:T(8,128)(2,1)S(1)} custom-call(bf16[256,1792]{1,0:T(8,128)(2,1)S(1)} %collective-permute-done.11.refs_0_, bf16[2,448,1792]{2,1,0:T(8,128)(2,1)S(1)} %bitcast.28, bf16[2,448,1792]{2,1,0:T(8,128)(2,1)S(1)} %bitcast.38, bf16[2,448,1792]{2,1,0:T(8,128)(2,1)S(1)} %copy-done.5, bf16[3,448,1792]{2,1,0:T(8,128)(2,1)S(1)} %land.3.refs_4_.refs_5_), custom_call_target="tpu_custom_call" | custom-call | tf_op jit(solution)/shard_map/mlp/pallas_call | solution.py:121
  131.7 3.2 %mlp.14 = bf16[256,1792]{1,0:T(8,128)(2,1)S(1)} custom-call(bf16[128,1792]{1,0:T(8,128)(2,1)S(1)} %collective-permute-done.9.refs_0_, bf16[128,1792]{1,0:T(8,128)(2,1)S(1)} %collective-permute-done.10.refs_1_, bf16[2,448,1792]{2,1,0:T(8,128)(2,1)S(1)} %bitcast.29, bf16[2,448,1792]{2,1,0:T(8,128)(2,1)S(1)} %bitcast.39, bf16[2,448,1792]{2,1,0:T(8,128)(2,1)S(1)} %copy-done.5, ...), custom_call_target="tpu_custom_call" | custom-call | tf_op jit(solution)/shard_map/mlp/pallas_call | solution.py:121
  134.9 3.2 %mlp.15 = bf16[256,1792]{1,0:T(8,128)(2,1)S(1)} custom-call(bf16[128,1792]{1,0:T(8,128)(2,1)S(1)} %collective-permute-done.16.refs_0_, bf16[128,1792]{1,0:T(8,128)(2,1)S(1)} %collective-permute-done.17.refs_1_, bf16[2,448,1792]{2,1,0:T(8,128)(2,1)S(1)} %bitcast.30, bf16[2,448,1792]{2,1,0:T(8,128)(2,1)S(1)} %bitcast.40, bf16[2,448,1792]{2,1,0:T(8,128)(2,1)S(1)} %copy-done.5, ...), custom_call_target="tpu_custom_call" | custom-call | tf_op jit(solution)/shard_map/mlp/pallas_call | solution.py:121
  139.1 2.7 %collective-permute-start.5 = (bf16[256,1792]{1,0:T(8,128)(2,1)S(1)}, bf16[256,1792]{1,0:T(8,128)(2,1)S(1)}, u32[]{:S(2)}, u32[]{:S(2)}) collective-permute-start(bf16[256,1792]{1,0:T(8,128)(2,1)S(1)} %mlp.10), channel_id=1, source_target_pairs={{0,12},{1,13},{2,14},{3,15},{4,0},{5,1},{6,2},{7,3},{8,4},{9,5},{1... | collective-permute-start | bytes 2752520 | tf_op jit(solution)/shard_map/ppermute | solution.py:230
  141.8 11.9 %collective-permute-done.15 = bf16[256,1792]{1,0:T(8,128)(2,1)S(1)} collective-permute-done((bf16[256,1792]{1,0:T(8,128)(2,1)S(1)}, bf16[256,1792]{1,0:T(8,128)(2,1)S(1)}, u32[]{:S(2)}, u32[]{:S(2)}) %collective-permute-start.15) | collective-permute-done | bytes 917536 | tf_op jit(solution)/shard_map/ppermute | solution.py:230
  153.7 17.8 %collective-permute-done.18 = bf16[256,1792]{1,0:T(8,128)(2,1)S(1)} collective-permute-done((bf16[256,1792]{1,0:T(8,128)(2,1)S(1)}, bf16[256,1792]{1,0:T(8,128)(2,1)S(1)}, u32[]{:S(2)}, u32[]{:S(2)}) %collective-permute-start.18) | collective-permute-done | bytes 917536 | tf_op jit(solution)/shard_map/ppermute | solution.py:230
  174.8 5.9 %collective-permute-done.19 = bf16[128,1792]{1,0:T(8,128)(2,1)S(1)} collective-permute-done((bf16[128,1792]{1,0:T(8,128)(2,1)S(1)}, bf16[128,1792]{1,0:T(8,128)(2,1)S(1)}, u32[]{:S(2)}, u32[]{:S(2)}) %collective-permute-start.19) | collective-permute-done | bytes 458784 | tf_op jit(solution)/shard_map/ppermute | solution.py:230
  184.2 22.1 %all-to-all-start.3 = ((bf16[8,2,16,1792]{3,2,1,0:T(8,128)(2,1)}), bf16[8,2,16,1792]{3,2,1,0:T(8,128)(2,1)S(1)}, u32[]{:S(2)}, u32[]{:S(2)}) async-start(bf16[8,2,16,1792]{3,2,1,0:T(8,128)(2,1)} %pad_maximum_fusion.2), calls=%async_computation.3 | async-start | bytes 1835008 | tf_op jit(solution)/shard_map/all_to_all | solution.py:309
  206.5 13.5 %all-to-all-done.3 = bf16[8,2,16,1792]{3,2,1,0:T(8,128)(2,1)S(1)} async-done(((bf16[8,2,16,1792]{3,2,1,0:T(8,128)(2,1)}), bf16[8,2,16,1792]{3,2,1,0:T(8,128)(2,1)S(1)}, u32[]{:S(2)}, u32[]{:S(2)}) %all-to-all-start.3) | async-done | bytes 917536 | tf_op jit(solution)/shard_map/all_to_all | solution.py:309
  (79 shorter events, 36.7 us)
Async XLA Ops:
  8.3 83.5 %collective-permute-start.1 = (bf16[3,448,1792]{2,1,0:T(8,128)(2,1)}, bf16[3,448,1792]{2,1,0:T(8,128)(2,1)}, u32[]{:S(2)}, u32[]{:S(2)}) collective-permute-start(bf16[3,448,1792]{2,1,0:T(8,128)(2,1)} %pack.2), channel_id=1, source_target_pairs={{0,3},{1,0},{2,1},{3,2},{4,7},{5,4},{6,5},{7,6},{8,11},{9,8},{10,9... | collective-permute-start | bytes 14450696 | tf_op jit(solution)/shard_map/ppermute | solution.py:230
  12.8 87.2 %collective-permute-start.4 = (bf16[3,448,1792]{2,1,0:T(8,128)(2,1)}, bf16[3,448,1792]{2,1,0:T(8,128)(2,1)}, u32[]{:S(2)}, u32[]{:S(2)}) collective-permute-start(bf16[3,448,1792]{2,1,0:T(8,128)(2,1)} %pack.3), channel_id=1, source_target_pairs={{0,12},{1,13},{2,14},{3,15},{4,0},{5,1},{6,2},{7,3},{8,4},{9,5},{1... | collective-permute-start | bytes 14450696 | tf_op jit(solution)/shard_map/ppermute | solution.py:230
  14.6 34.9 %copy-start.8 = (f32[1792]{0:T(1024)S(1)}, f32[1792]{0:T(1024)}, u32[]{:S(2)}) copy-start(f32[1792]{0:T(1024)} %param.11) | copy-start | bytes 21508
  14.6 43.6 %copy-start.6 = (bf16[4,32,1792]{2,1,0:T(8,128)(2,1)S(1)}, bf16[4,32,1792]{2,1,0:T(8,128)(2,1)}, u32[]{:S(2)}) copy-start(bf16[4,32,1792]{2,1,0:T(8,128)(2,1)} %res_ref.1) | copy-start | bytes 1376260
  45.4 12.8 %all-to-all-start.1 = ((bf16[8,4,8,896]{3,2,1,0:T(8,128)(2,1)}), bf16[8,4,8,896]{3,2,1,0:T(8,128)(2,1)S(1)}, u32[]{:S(2)}, u32[]{:S(2)}) async-start(bf16[8,4,8,896]{3,2,1,0:T(8,128)(2,1)} %attend.1), calls=%async_computation.1 | async-start | bytes 917504 | tf_op jit(solution)/shard_map/all_to_all | solution.py:219
  76.0 12.8 %collective-permute-start = (bf16[128,1792]{1,0:T(8,128)(2,1)S(1)}, bf16[128,1792]{1,0:T(8,128)(2,1)S(1)}, u32[]{:S(2)}, u32[]{:S(2)}) collective-permute-start(bf16[128,1792]{1,0:T(8,128)(2,1)S(1)} %bitcast.49), channel_id=1, source_target_pairs={{0,2},{1,3},{2,0},{3,1},{4,6},{5,7},{6,4},{7,5},{8,10},{9,11},{10,... | collective-permute-start | bytes 1376264 | tf_op jit(solution)/shard_map/ppermute | solution.py:230
  76.6 12.4 %collective-permute-start.3 = (bf16[128,1792]{1,0:T(8,128)(2,1)S(1)}, bf16[128,1792]{1,0:T(8,128)(2,1)S(1)}, u32[]{:S(2)}, u32[]{:S(2)}) collective-permute-start(bf16[128,1792]{1,0:T(8,128)(2,1)S(1)} %bitcast.47), channel_id=1, source_target_pairs={{0,8},{1,9},{2,10},{3,11},{4,12},{5,13},{6,14},{7,15},{8,0},{9,1},... | collective-permute-start | bytes 1376264 | tf_op jit(solution)/shard_map/ppermute | solution.py:230
  88.8 21.5 %collective-permute-start.2 = (bf16[256,1792]{1,0:T(8,128)(2,1)S(1)}, bf16[256,1792]{1,0:T(8,128)(2,1)S(1)}, u32[]{:S(2)}, u32[]{:S(2)}) collective-permute-start(bf16[256,1792]{1,0:T(8,128)(2,1)S(1)} %pad_maximum_fusion.refs_0_), channel_id=1, source_target_pairs={{0,4},{1,5},{2,6},{3,7},{4,8},{5,9},{6,10},{7,11},{8,12},{9,13},{1... | collective-permute-start | bytes 2752520 | tf_op jit(solution)/shard_map/ppermute | solution.py:230
  89.1 24.3 %collective-permute-start.7 = (bf16[256,1792]{1,0:T(8,128)(2,1)S(1)}, bf16[256,1792]{1,0:T(8,128)(2,1)S(1)}, u32[]{:S(2)}, u32[]{:S(2)}) collective-permute-start(bf16[256,1792]{1,0:T(8,128)(2,1)S(1)} %pad_maximum_fusion.1.refs_0_), channel_id=1, source_target_pairs={{0,1},{1,2},{2,3},{3,0},{4,5},{5,6},{6,7},{7,4},{8,9},{9,10},{10,1... | collective-permute-start | bytes 2752520 | tf_op jit(solution)/shard_map/ppermute | solution.py:230
  89.8 26.9 %collective-permute-start.6 = (bf16[256,1792]{1,0:T(8,128)(2,1)S(1)}, bf16[256,1792]{1,0:T(8,128)(2,1)S(1)}, u32[]{:S(2)}, u32[]{:S(2)}) collective-permute-start(bf16[256,1792]{1,0:T(8,128)(2,1)S(1)} %pad_maximum_fusion.refs_0_), channel_id=1, source_target_pairs={{0,12},{1,13},{2,14},{3,15},{4,0},{5,1},{6,2},{7,3},{8,4},{9,5},{1... | collective-permute-start | bytes 2752520 | tf_op jit(solution)/shard_map/ppermute | solution.py:230
  91.8 31.2 %collective-permute-start.11 = (bf16[256,1792]{1,0:T(8,128)(2,1)S(1)}, bf16[256,1792]{1,0:T(8,128)(2,1)S(1)}, u32[]{:S(2)}, u32[]{:S(2)}) collective-permute-start(bf16[256,1792]{1,0:T(8,128)(2,1)S(1)} %pad_maximum_fusion.1.refs_0_), channel_id=1, source_target_pairs={{0,3},{1,0},{2,1},{3,2},{4,7},{5,4},{6,5},{7,6},{8,11},{9,8},{10,9... | collective-permute-start | bytes 2752520 | tf_op jit(solution)/shard_map/ppermute | solution.py:230
  120.1 10.8 %collective-permute-start.9 = (bf16[128,1792]{1,0:T(8,128)(2,1)S(1)}, bf16[128,1792]{1,0:T(8,128)(2,1)S(1)}, u32[]{:S(2)}, u32[]{:S(2)}) collective-permute-start(bf16[128,1792]{1,0:T(8,128)(2,1)S(1)} %slice.71), channel_id=1, source_target_pairs={{0,4},{1,5},{2,6},{3,7},{4,8},{5,9},{6,10},{7,11},{8,12},{9,13},{1... | collective-permute-start | bytes 1376264 | tf_op jit(solution)/shard_map/ppermute | solution.py:230
  120.3 11.4 %collective-permute-start.10 = (bf16[128,1792]{1,0:T(8,128)(2,1)S(1)}, bf16[128,1792]{1,0:T(8,128)(2,1)S(1)}, u32[]{:S(2)}, u32[]{:S(2)}) collective-permute-start(bf16[128,1792]{1,0:T(8,128)(2,1)S(1)} %slice.72), channel_id=1, source_target_pairs={{0,12},{1,13},{2,14},{3,15},{4,0},{5,1},{6,2},{7,3},{8,4},{9,5},{1... | collective-permute-start | bytes 1376264 | tf_op jit(solution)/shard_map/ppermute | solution.py:230
  123.0 11.9 %collective-permute-start.16 = (bf16[128,1792]{1,0:T(8,128)(2,1)S(1)}, bf16[128,1792]{1,0:T(8,128)(2,1)S(1)}, u32[]{:S(2)}, u32[]{:S(2)}) collective-permute-start(bf16[128,1792]{1,0:T(8,128)(2,1)S(1)} %slice.81), channel_id=1, source_target_pairs={{0,1},{1,2},{2,3},{3,0},{4,5},{5,6},{6,7},{7,4},{8,9},{9,10},{10,1... | collective-permute-start | bytes 1376264 | tf_op jit(solution)/shard_map/ppermute | solution.py:230
  123.0 11.8 %collective-permute-start.17 = (bf16[128,1792]{1,0:T(8,128)(2,1)S(1)}, bf16[128,1792]{1,0:T(8,128)(2,1)S(1)}, u32[]{:S(2)}, u32[]{:S(2)}) collective-permute-start(bf16[128,1792]{1,0:T(8,128)(2,1)S(1)} %slice.82), channel_id=1, source_target_pairs={{0,3},{1,0},{2,1},{3,2},{4,7},{5,4},{6,5},{7,6},{8,11},{9,8},{10,9... | collective-permute-start | bytes 1376264 | tf_op jit(solution)/shard_map/ppermute | solution.py:230
  128.9 24.8 %collective-permute-start.15 = (bf16[256,1792]{1,0:T(8,128)(2,1)S(1)}, bf16[256,1792]{1,0:T(8,128)(2,1)S(1)}, u32[]{:S(2)}, u32[]{:S(2)}) collective-permute-start(bf16[256,1792]{1,0:T(8,128)(2,1)S(1)} %mlp.13), channel_id=1, source_target_pairs={{0,1},{1,2},{2,3},{3,0},{4,5},{5,6},{6,7},{7,4},{8,9},{9,10},{10,1... | collective-permute-start | bytes 2752520 | tf_op jit(solution)/shard_map/ppermute | solution.py:230
  130.9 22.8 %collective-permute-start.14 = (bf16[256,1792]{1,0:T(8,128)(2,1)S(1)}, bf16[256,1792]{1,0:T(8,128)(2,1)S(1)}, u32[]{:S(2)}, u32[]{:S(2)}) collective-permute-start(bf16[256,1792]{1,0:T(8,128)(2,1)S(1)} %mlp.11), channel_id=1, source_target_pairs={{0,3},{1,0},{2,1},{3,2},{4,7},{5,4},{6,5},{7,6},{8,11},{9,8},{10,9... | collective-permute-start | bytes 2752520 | tf_op jit(solution)/shard_map/ppermute | solution.py:230
  138.0 33.5 %collective-permute-start.18 = (bf16[256,1792]{1,0:T(8,128)(2,1)S(1)}, bf16[256,1792]{1,0:T(8,128)(2,1)S(1)}, u32[]{:S(2)}, u32[]{:S(2)}) collective-permute-start(bf16[256,1792]{1,0:T(8,128)(2,1)S(1)} %mlp.15), channel_id=1, source_target_pairs={{0,2},{1,3},{2,0},{3,1},{4,6},{5,7},{6,4},{7,5},{8,10},{9,11},{10,... | collective-permute-start | bytes 2752520 | tf_op jit(solution)/shard_map/ppermute | solution.py:230
  139.1 32.8 %collective-permute-start.8 = (bf16[256,1792]{1,0:T(8,128)(2,1)S(1)}, bf16[256,1792]{1,0:T(8,128)(2,1)S(1)}, u32[]{:S(2)}, u32[]{:S(2)}) collective-permute-start(bf16[256,1792]{1,0:T(8,128)(2,1)S(1)} %mlp.12), channel_id=1, source_target_pairs={{0,4},{1,5},{2,6},{3,7},{4,8},{5,9},{6,10},{7,11},{8,12},{9,13},{1... | collective-permute-start | bytes 2752520 | tf_op jit(solution)/shard_map/ppermute | solution.py:230
  139.1 32.8 %collective-permute-start.5 = (bf16[256,1792]{1,0:T(8,128)(2,1)S(1)}, bf16[256,1792]{1,0:T(8,128)(2,1)S(1)}, u32[]{:S(2)}, u32[]{:S(2)}) collective-permute-start(bf16[256,1792]{1,0:T(8,128)(2,1)S(1)} %mlp.10), channel_id=1, source_target_pairs={{0,12},{1,13},{2,14},{3,15},{4,0},{5,1},{6,2},{7,3},{8,4},{9,5},{1... | collective-permute-start | bytes 2752520 | tf_op jit(solution)/shard_map/ppermute | solution.py:230
  153.7 19.8 %collective-permute-start.12 = (bf16[256,1792]{1,0:T(8,128)(2,1)S(1)}, bf16[256,1792]{1,0:T(8,128)(2,1)S(1)}, u32[]{:S(2)}, u32[]{:S(2)}) collective-permute-start(bf16[256,1792]{1,0:T(8,128)(2,1)S(1)} %mlp.14), channel_id=1, source_target_pairs={{0,8},{1,9},{2,10},{3,11},{4,12},{5,13},{6,14},{7,15},{8,0},{9,1},... | collective-permute-start | bytes 2752520 | tf_op jit(solution)/shard_map/ppermute | solution.py:230
  171.8 8.9 %collective-permute-start.19 = (bf16[128,1792]{1,0:T(8,128)(2,1)S(1)}, bf16[128,1792]{1,0:T(8,128)(2,1)S(1)}, u32[]{:S(2)}, u32[]{:S(2)}) collective-permute-start(bf16[128,1792]{1,0:T(8,128)(2,1)S(1)} %add_convert_fusion.1), channel_id=1, source_target_pairs={{0,8},{1,9},{2,10},{3,11},{4,12},{5,13},{6,14},{7,15},{8,0},{9,1},... | collective-permute-start | bytes 1376264 | tf_op jit(solution)/shard_map/ppermute | solution.py:230
  173.7 9.2 %collective-permute-start.13 = (bf16[128,1792]{1,0:T(8,128)(2,1)S(1)}, bf16[128,1792]{1,0:T(8,128)(2,1)S(1)}, u32[]{:S(2)}, u32[]{:S(2)}) collective-permute-start(bf16[128,1792]{1,0:T(8,128)(2,1)S(1)} %add_convert_fusion.3), channel_id=1, source_target_pairs={{0,2},{1,3},{2,0},{3,1},{4,6},{5,7},{6,4},{7,5},{8,10},{9,11},{10,... | collective-permute-start | bytes 1376264 | tf_op jit(solution)/shard_map/ppermute | solution.py:230
  184.2 35.7 %all-to-all-start.3 = ((bf16[8,2,16,1792]{3,2,1,0:T(8,128)(2,1)}), bf16[8,2,16,1792]{3,2,1,0:T(8,128)(2,1)S(1)}, u32[]{:S(2)}, u32[]{:S(2)}) async-start(bf16[8,2,16,1792]{3,2,1,0:T(8,128)(2,1)} %pad_maximum_fusion.2), calls=%async_computation.3 | async-start | bytes 1835008 | tf_op jit(solution)/shard_map/all_to_all | solution.py:309
  (10 other events, 130.4 us)

commit v2 on v1

--- a/solution.py
+++ b/solution.py
@@ -91,8 +91,7 @@
 
 
 def mlp_kernel(index, pieces, *refs):
-    gate, up, down, near = refs[pieces : pieces + 4]
-    out = refs[pieces + 4]
+    gate, up, down, near, out = refs[pieces:]
     rows = [ref[...] for ref in refs[:pieces]]
     rows = rows[0] if pieces == 1 else jnp.concatenate(rows, axis=0)
     total = None
@@ -128,18 +127,21 @@
     )(*pieces, gate, up, down, near)
 
 
-def pack_kernel(index, gate, up, down, out_ref):
+def pack_kernel(gate, up, down, out_ref):
     for i, source in enumerate((gate, up, down)):
-        out_ref[i] = source[index]
+        out_ref[i] = source[...]
 
 
 def pack(index, gate, up, down):
+    steps = 4
+    _, rows, width = gate.shape
     return pl.pallas_call(
-        lambda *refs: pack_kernel(index, *refs),
-        in_specs=on_chip(3),
-        out_specs=on_chip(1)[0],
-        out_shape=jax.ShapeDtypeStruct((3, *gate.shape[1:]), gate.dtype),
-        compiler_params=grant(18),
+        pack_kernel,
+        grid=(steps,),
+        in_specs=[pl.BlockSpec((None, rows // steps, width), lambda i: (index, i, 0))] * 3,
+        out_specs=pl.BlockSpec((3, rows // steps, width), lambda i: (0, i, 0)),
+        out_shape=jax.ShapeDtypeStruct((3, rows, width), gate.dtype),
+        compiler_params=grant(58),
         name="pack",
     )(gate, up, down)
 
@@ -158,11 +160,11 @@
 def land(value):
     return pl.pallas_call(
         land_kernel,
-        in_specs=[pl.BlockSpec(memory_space=pl.ANY)],
+        in_specs=[pl.BlockSpec(memory_space=pltpu.HBM)],
         out_specs=on_chip(1)[0],
         out_shape=pltpu.VMEM(value.shape, value.dtype),
         scratch_shapes=[pltpu.SemaphoreType.DMA((value.shape[0],))],
-        compiler_params=grant(1),
+        compiler_params=grant(6),
         name="land",
     )(value)
 
@@ -212,7 +214,6 @@
         attend_kernel,
         out_shape=jax.ShapeDtypeStruct((groups, frames_local, SITE_GROUP, half), bf16),
         in_specs=on_chip(1),
-        out_specs=on_chip(1)[0],
         compiler_params=grant(16),
         name="attend",
     )(together)
@@ -247,8 +248,8 @@
             jax.ShapeDtypeStruct((tokens, model_width), jnp.float32),
             jax.ShapeDtypeStruct((slots, model_width), bf16),
         ),
-        in_specs=on_chip(4),
-        out_specs=tuple(on_chip(2)),
+        in_specs=on_chip(1) + [pl.BlockSpec()] + on_chip(2),
+        out_specs=(pl.BlockSpec(), on_chip(1)[0]),
         compiler_params=grant(12),
         name="route",
     )(attended, residual, norm_gain.reshape(1, model_width), target.T)
@@ -263,37 +264,32 @@
     mine = [arrived[:, e].reshape(part_rows, model_width) for e in range(2)]
     far = (along_x, along_z)
     ring = (along_z, along_x)
-    here = []
-    for e in range(2):
-        here.append(jnp.concatenate([mine[e], send(mine[e], far[e](2))]))
-
-    def send_all(values, steps):
+
+    def send_all(values, moves, steps):
         out = []
         for e in range(2):
-            out.append(send(values[e], ring[e](steps)))
+            out.append(send(values[e], moves[e](steps)))
         return out
 
-    def run(e, pieces):
+    def run(e, pieces, after):
+        pieces, _ = lax.optimization_barrier((pieces, after))
         return mlp(pieces, e, gate, up, w_down, near[e])
 
-    ahead = send_all(here, 1)
-    behind = send_all(here, -1)
-    done = [run(e, [here[e]]) for e in range(2)]
-    parts = [[part] for part in done]
-    from_ahead, from_behind = [None, None], [None, None]
-    for arrived_rows, relayed, cut, steps in (
-        (ahead, from_ahead, slice(0, part_rows), 1),
-        (behind, from_behind, slice(part_rows, 2 * part_rows), -1),
-    ):
+    other = send_all(mine, far, 2)
+    ahead = [send_all(mine, ring, 1)]
+    behind = [send_all(mine, ring, -1)]
+    ahead.append(send_all(other, ring, 1))
+    behind.append(send_all(other, ring, -1))
+    across = [send_all(ahead[0], ring, 1), send_all(behind[1], ring, -1)]
+    done = ()
+    parts = []
+    for e in range(2):
+        done = run(e, [mine[e], other[e]], done)
+        parts.append([done])
+    for pieces, steps in ((ahead, -1), (behind, 1), (across, 2)):
         for e in range(2):
-            rows_in, done = lax.optimization_barrier((arrived_rows[e], done))
-            relayed[e] = send(rows_in[cut], ring[e](steps))
-            done = run(e, [rows_in])
-            parts[e].append(send(done, ring[e](-steps)))
-    for e in range(2):
-        rows_in, done = lax.optimization_barrier(([from_ahead[e], from_behind[e]], done))
-        done = run(e, rows_in)
-        parts[e].append(send(done, ring[e](2)))
+            done = run(e, [pieces[0][e], pieces[1][e]], done)
+            parts[e].append(send(done, ring[e](steps)))
 
     def add(pieces):
         total = pieces[0].astype(jnp.float32)
@@ -311,7 +307,6 @@
         combine_kernel,
         out_shape=jax.ShapeDtypeStruct((tokens, model_width), bf16),
         in_specs=on_chip(4),
-        out_specs=on_chip(1)[0],
         compiler_params=grant(12),
         name="combine",
     )(hidden, back.reshape(slots, model_width), target, gates)

time: 222 us -> 242 us (1.090)
  waiting for transfers between devices: 79.4 us -> 115 us
  starting transfers between devices: 47.9 us -> 32.8 us
  local copies, waits for them, and re-layouts: 6.38 us -> 0.53 us
  Pallas kernels: 40.3 us -> 45.4 us
    ppermute x20 -> x24, waiting for transfers between devices: 57.4 us -> 92.8 us  [send(): return lax.ppermute(value, ('ep', 'tp'), pairs)]
    all_to_all x1, starting transfers between devices: 22.1 us -> 8.04 us  [block(): back = lax.all_to_all(ready, 'ep', split_axis=0, concat_axis=0, tiled=True)]
    unnamed x25 -> x19, local copies, waits for them, and re-layouts: 5.88 us -> 0.14 us
    pallas_call x4, Pallas kernels: 9.88 us -> 14.9 us  [the longest x2 10.1 us: pack(): pl.pallas_call(pack_kernel, grid=(steps,), in_specs=[pl.BlockSpec((None,...]
    ppermute x20 -> x24, starting transfers between devices: 21.6 us -> 20.6 us  [send(): return lax.ppermute(value, ('ep', 'tp'), pairs)]
  transfers between devices with their start and end apart: 22 -> 26, of which waited for: 11 -> 13; matrix products, arithmetic and copies ran while one was open for 1% -> 1% of each run, Pallas kernels for 17% -> 15%
where the time goes in v2:
time: 242 us; the launch traced here: 240 us
  waiting for transfers between devices  115 us (48%)
  Pallas kernels  45.4 us (19%)
  blocking collectives  44.7 us (18%)
  starting transfers between devices  32.8 us (14%)
    ppermute x24, waiting for transfers between devices, send(): return lax.ppermute(value, ('ep', 'tp'), pairs)  92.8 us
    all_to_all x1, blocking collectives, block(): lax.all_to_all(spread, 'ep', split_axis=0, concat_axis=0, tiled=True)  27.6 us
    pallas_call x8, Pallas kernels, mlp(): pl.pallas_call(lambda *refs: mlp_kernel(index, len(pieces), *refs), in_sp...  25.6 us
    ppermute x24, starting transfers between devices, send(): return lax.ppermute(value, ('ep', 'tp'), pairs)  20.6 us
    all_to_all x1, blocking collectives, block(): lax.all_to_all(rows.reshape(groups, experts_local, capacity, model_width)...  17.1 us
    all_to_all x1, waiting for transfers between devices, block(): back = lax.all_to_all(ready, 'ep', split_axis=0, concat_axis=0, tiled=True)  13.5 us
    pallas_call x2, Pallas kernels, pack(): pl.pallas_call(pack_kernel, grid=(steps,), in_specs=[pl.BlockSpec((None,...  10.1 us
    all_to_all x1, waiting for transfers between devices, block(): lax.all_to_all(mixed, 'ep', split_axis=0, concat_axis=0, tiled=True)  8.45 us
  transfers between devices with their start and end apart: 26, of which 13 were waited for; matrix products, arithmetic and copies ran while one was open for 1% of the time, Pallas kernels for 15%

profile of v2, /device:TPU:1, one launch (start us, length us, event | category | flops | bytes accessed | tf_op | source)
XLA Modules:
  0.0 240.4 jit_solution(7413745157643210016)
XLA Ops:
  0.0 5.0 %pack.2 = bf16[3,448,1792]{2,1,0:T(8,128)(2,1)} custom-call(bf16[2,448,1792]{2,1,0:T(8,128)(2,1)} %bitcast.21, bf16[2,448,1792]{2,1,0:T(8,128)(2,1)} %bitcast.31, bf16[2,448,1792]{2,1,0:T(8,128)(2,1)} %refs_4_.15), custom_call_target="tpu_custom_call" | custom-call | tf_op jit(solution)/shard_map/pack/pallas_call | solution.py:138
  7.1 5.0 %pack.3 = bf16[3,448,1792]{2,1,0:T(8,128)(2,1)} custom-call(bf16[2,448,1792]{2,1,0:T(8,128)(2,1)} %bitcast.22, bf16[2,448,1792]{2,1,0:T(8,128)(2,1)} %bitcast.32, bf16[2,448,1792]{2,1,0:T(8,128)(2,1)} %refs_4_.15), custom_call_target="tpu_custom_call" | custom-call | tf_op jit(solution)/shard_map/pack/pallas_call | solution.py:138
  14.0 27.6 %all_to_all.20.qkv_ref = bf16[8,3,4,8,896]{4,3,2,1,0:T(8,128)(2,1)S(1)} all-to-all(bf16[8,3,4,8,896]{4,3,2,1,0:T(8,128)(2,1)S(1)} %bitcast.54), channel_id=1, replica_groups=mesh['ep'=8,'tp'=16] {'ep'}, dimensions={0} | all-to-all | bytes 2752512 | tf_op jit(solution)/shard_map/all_to_all | solution.py:212
  44.6 4.1 %all-to-all-start.1 = ((bf16[8,4,8,896]{3,2,1,0:T(8,128)(2,1)}), bf16[8,4,8,896]{3,2,1,0:T(8,128)(2,1)S(1)}, u32[]{:S(2)}, u32[]{:S(2)}) async-start(bf16[8,4,8,896]{3,2,1,0:T(8,128)(2,1)} %attend.1), calls=%async_computation.1 | async-start | bytes 917504 | tf_op jit(solution)/shard_map/all_to_all | solution.py:220
  49.0 8.5 %all-to-all-done.1.att_ref = bf16[8,4,8,896]{3,2,1,0:T(8,128)(2,1)S(1)} async-done(((bf16[8,4,8,896]{3,2,1,0:T(8,128)(2,1)}), bf16[8,4,8,896]{3,2,1,0:T(8,128)(2,1)S(1)}, u32[]{:S(2)}, u32[]{:S(2)}) %all-to-all-start.1) | async-done | bytes 458784 | tf_op jit(solution)/shard_map/all_to_all | solution.py:220
  58.1 17.1 %all_to_all.21 = bf16[8,2,16,1792]{3,2,1,0:T(8,128)(2,1)S(1)} all-to-all(bf16[8,2,16,1792]{3,2,1,0:T(8,128)(2,1)S(1)} %bitcast.50), channel_id=1, replica_groups=mesh['ep'=8,'tp'=16] {'ep'}, dimensions={0} | all-to-all | bytes 1835008 | tf_op jit(solution)/shard_map/all_to_all | solution.py:256
  76.5 11.5 %collective-permute-done.refs_1_ = bf16[128,1792]{1,0:T(8,128)(2,1)S(1)} collective-permute-done((bf16[128,1792]{1,0:T(8,128)(2,1)S(1)}, bf16[128,1792]{1,0:T(8,128)(2,1)S(1)}, u32[]{:S(2)}, u32[]{:S(2)}) %collective-permute-start) | collective-permute-done | bytes 458784 | tf_op jit(solution)/shard_map/ppermute | solution.py:231
  88.3 11.3 %collective-permute-done.2.refs_0_ = bf16[128,1792]{1,0:T(8,128)(2,1)S(1)} collective-permute-done((bf16[128,1792]{1,0:T(8,128)(2,1)S(1)}, bf16[128,1792]{1,0:T(8,128)(2,1)S(1)}, u32[]{:S(2)}, u32[]{:S(2)}) %collective-permute-start.2) | collective-permute-done | bytes 458784 | tf_op jit(solution)/shard_map/ppermute | solution.py:231
  99.8 9.7 %collective-permute-done.3.refs_1_ = bf16[128,1792]{1,0:T(8,128)(2,1)S(1)} collective-permute-done((bf16[128,1792]{1,0:T(8,128)(2,1)S(1)}, bf16[128,1792]{1,0:T(8,128)(2,1)S(1)}, u32[]{:S(2)}, u32[]{:S(2)}) %collective-permute-start.3) | collective-permute-done | bytes 458784 | tf_op jit(solution)/shard_map/ppermute | solution.py:231
  118.6 3.2 %mlp.8 = bf16[256,1792]{1,0:T(8,128)(2,1)S(1)} custom-call(bf16[128,1792]{1,0:T(8,128)(2,1)S(1)} %bitcast.49, bf16[128,1792]{1,0:T(8,128)(2,1)S(1)} %collective-permute-done.refs_1_, bf16[2,448,1792]{2,1,0:T(8,128)(2,1)S(1)} %bitcast.23, bf16[2,448,1792]{2,1,0:T(8,128)(2,1)S(1)} %bitcast.33, bf16[2,448,1792]{2,1,0:T(8,128)(2,1)S(1)} %copy-done.2, ...), custom_call_target="tpu_custom_call" | custom-call | tf_op jit(solution)/shard_map/mlp/pallas_call | solution.py:120
  124.2 3.2 %mlp.9 = bf16[256,1792]{1,0:T(8,128)(2,1)S(1)} custom-call(bf16[128,1792]{1,0:T(8,128)(2,1)S(1)} %bitcast.45, bf16[128,1792]{1,0:T(8,128)(2,1)S(1)} %collective-permute-done.4.refs_1_, bf16[2,448,1792]{2,1,0:T(8,128)(2,1)S(1)} %bitcast.24, bf16[2,448,1792]{2,1,0:T(8,128)(2,1)S(1)} %bitcast.34, bf16[2,448,1792]{2,1,0:T(8,128)(2,1)S(1)} %copy-done.2, ...), custom_call_target="tpu_custom_call" | custom-call | tf_op jit(solution)/shard_map/mlp/pallas_call | solution.py:120
  127.4 3.2 %mlp.10 = bf16[256,1792]{1,0:T(8,128)(2,1)S(1)} custom-call(bf16[128,1792]{1,0:T(8,128)(2,1)S(1)} %collective-permute-done.2.refs_0_, bf16[128,1792]{1,0:T(8,128)(2,1)S(1)} %collective-permute-done.3.refs_1_, bf16[2,448,1792]{2,1,0:T(8,128)(2,1)S(1)} %bitcast.25, bf16[2,448,1792]{2,1,0:T(8,128)(2,1)S(1)} %bitcast.35, bf16[2,448,1792]{2,1,0:T(8,128)(2,1)S(1)} %copy-done.2, ...), custom_call_target="tpu_custom_call" | custom-call | tf_op jit(solution)/shard_map/mlp/pallas_call | solution.py:120
  130.5 3.2 %mlp.11 = bf16[256,1792]{1,0:T(8,128)(2,1)S(1)} custom-call(bf16[128,1792]{1,0:T(8,128)(2,1)S(1)} %collective-permute-done.9.refs_0_, bf16[128,1792]{1,0:T(8,128)(2,1)S(1)} %collective-permute-done.10.refs_1_, bf16[2,448,1792]{2,1,0:T(8,128)(2,1)S(1)} %bitcast.26, bf16[2,448,1792]{2,1,0:T(8,128)(2,1)S(1)} %bitcast.36, bf16[2,448,1792]{2,1,0:T(8,128)(2,1)S(1)} %copy-done.2, ...), custom_call_target="tpu_custom_call" | custom-call | tf_op jit(solution)/shard_map/mlp/pallas_call | solution.py:120
  133.7 3.4 %mlp.12 = bf16[256,1792]{1,0:T(8,128)(2,1)S(1)} custom-call(bf16[128,1792]{1,0:T(8,128)(2,1)S(1)} %collective-permute-done.7.refs_0_, bf16[128,1792]{1,0:T(8,128)(2,1)S(1)} %collective-permute-done.8.refs_1_, bf16[2,448,1792]{2,1,0:T(8,128)(2,1)S(1)} %bitcast.27, bf16[2,448,1792]{2,1,0:T(8,128)(2,1)S(1)} %bitcast.37, bf16[2,448,1792]{2,1,0:T(8,128)(2,1)S(1)} %copy-done.2, ...), custom_call_target="tpu_custom_call" | custom-call | tf_op jit(solution)/shard_map/mlp/pallas_call | solution.py:120
  137.1 3.2 %mlp.13 = bf16[256,1792]{1,0:T(8,128)(2,1)S(1)} custom-call(bf16[128,1792]{1,0:T(8,128)(2,1)S(1)} %collective-permute-done.14.refs_0_, bf16[128,1792]{1,0:T(8,128)(2,1)S(1)} %collective-permute-done.15.refs_1_, bf16[2,448,1792]{2,1,0:T(8,128)(2,1)S(1)} %bitcast.28, bf16[2,448,1792]{2,1,0:T(8,128)(2,1)S(1)} %bitcast.38, bf16[2,448,1792]{2,1,0:T(8,128)(2,1)S(1)} %copy-done.2, ...), custom_call_target="tpu_custom_call" | custom-call | tf_op jit(solution)/shard_map/mlp/pallas_call | solution.py:120
  140.3 3.2 %mlp.14 = bf16[256,1792]{1,0:T(8,128)(2,1)S(1)} custom-call(bf16[128,1792]{1,0:T(8,128)(2,1)S(1)} %collective-permute-done.12.refs_0_, bf16[128,1792]{1,0:T(8,128)(2,1)S(1)} %collective-permute-done.13.refs_1_, bf16[2,448,1792]{2,1,0:T(8,128)(2,1)S(1)} %bitcast.29, bf16[2,448,1792]{2,1,0:T(8,128)(2,1)S(1)} %bitcast.39, bf16[2,448,1792]{2,1,0:T(8,128)(2,1)S(1)} %copy-done.2, ...), custom_call_target="tpu_custom_call" | custom-call | tf_op jit(solution)/shard_map/mlp/pallas_call | solution.py:120
  149.0 6.2 %collective-permute-done.20.refs_0_ = bf16[128,1792]{1,0:T(8,128)(2,1)S(1)} collective-permute-done((bf16[128,1792]{1,0:T(8,128)(2,1)S(1)}, bf16[128,1792]{1,0:T(8,128)(2,1)S(1)}, u32[]{:S(2)}, u32[]{:S(2)}) %collective-permute-start.20) | collective-permute-done | bytes 458784 | tf_op jit(solution)/shard_map/ppermute | solution.py:231
  155.2 3.2 %mlp.15 = bf16[256,1792]{1,0:T(8,128)(2,1)S(1)} custom-call(bf16[128,1792]{1,0:T(8,128)(2,1)S(1)} %collective-permute-done.20.refs_0_, bf16[128,1792]{1,0:T(8,128)(2,1)S(1)} %collective-permute-done.21.refs_1_, bf16[2,448,1792]{2,1,0:T(8,128)(2,1)S(1)} %bitcast.30, bf16[2,448,1792]{2,1,0:T(8,128)(2,1)S(1)} %bitcast.40, bf16[2,448,1792]{2,1,0:T(8,128)(2,1)S(1)} %copy-done.2, ...), custom_call_target="tpu_custom_call" | custom-call | tf_op jit(solution)/shard_map/mlp/pallas_call | solution.py:120
  163.5 23.1 %collective-permute-done.11 = bf16[256,1792]{1,0:T(8,128)(2,1)S(1)} collective-permute-done((bf16[256,1792]{1,0:T(8,128)(2,1)S(1)}, bf16[256,1792]{1,0:T(8,128)(2,1)S(1)}, u32[]{:S(2)}, u32[]{:S(2)}) %collective-permute-start.11) | collective-permute-done | bytes 917536 | tf_op jit(solution)/shard_map/ppermute | solution.py:231
  189.0 5.2 %collective-permute-done.22 = bf16[256,1792]{1,0:T(8,128)(2,1)S(1)} collective-permute-done((bf16[256,1792]{1,0:T(8,128)(2,1)S(1)}, bf16[256,1792]{1,0:T(8,128)(2,1)S(1)}, u32[]{:S(2)}, u32[]{:S(2)}) %collective-permute-start.22) | collective-permute-done | bytes 917536 | tf_op jit(solution)/shard_map/ppermute | solution.py:231
  194.2 11.9 %collective-permute-done.18 = bf16[256,1792]{1,0:T(8,128)(2,1)S(1)} collective-permute-done((bf16[256,1792]{1,0:T(8,128)(2,1)S(1)}, bf16[256,1792]{1,0:T(8,128)(2,1)S(1)}, u32[]{:S(2)}, u32[]{:S(2)}) %collective-permute-start.18) | collective-permute-done | bytes 917536 | tf_op jit(solution)/shard_map/ppermute | solution.py:231
  208.2 8.0 %collective-permute-done.23 = bf16[128,1792]{1,0:T(8,128)(2,1)S(1)} collective-permute-done((bf16[128,1792]{1,0:T(8,128)(2,1)S(1)}, bf16[128,1792]{1,0:T(8,128)(2,1)S(1)}, u32[]{:S(2)}, u32[]{:S(2)}) %collective-permute-start.23) | collective-permute-done | bytes 458784 | tf_op jit(solution)/shard_map/ppermute | solution.py:231
  217.5 8.0 %all-to-all-start.3 = ((bf16[8,2,16,1792]{3,2,1,0:T(8,128)(2,1)}), bf16[8,2,16,1792]{3,2,1,0:T(8,128)(2,1)S(1)}, u32[]{:S(2)}, u32[]{:S(2)}) async-start(bf16[8,2,16,1792]{3,2,1,0:T(8,128)(2,1)} %pad_maximum_fusion), calls=%async_computation.3 | async-start | bytes 1835008 | tf_op jit(solution)/shard_map/all_to_all | solution.py:305
  225.7 13.5 %all-to-all-done.3 = bf16[8,2,16,1792]{3,2,1,0:T(8,128)(2,1)S(1)} async-done(((bf16[8,2,16,1792]{3,2,1,0:T(8,128)(2,1)}), bf16[8,2,16,1792]{3,2,1,0:T(8,128)(2,1)S(1)}, u32[]{:S(2)}, u32[]{:S(2)}) %all-to-all-start.3) | async-done | bytes 917536 | tf_op jit(solution)/shard_map/all_to_all | solution.py:305
  (75 shorter events, 38.9 us)
Async XLA Ops:
  5.1 108.4 %collective-permute-start.1 = (bf16[3,448,1792]{2,1,0:T(8,128)(2,1)}, bf16[3,448,1792]{2,1,0:T(8,128)(2,1)}, u32[]{:S(2)}, u32[]{:S(2)}) collective-permute-start(bf16[3,448,1792]{2,1,0:T(8,128)(2,1)} %pack.2), channel_id=1, source_target_pairs={{0,3},{1,0},{2,1},{3,2},{4,7},{5,4},{6,5},{7,6},{8,11},{9,8},{10,9... | collective-permute-start | bytes 14450696 | tf_op jit(solution)/shard_map/ppermute | solution.py:231
  12.1 101.3 %collective-permute-start.5 = (bf16[3,448,1792]{2,1,0:T(8,128)(2,1)}, bf16[3,448,1792]{2,1,0:T(8,128)(2,1)}, u32[]{:S(2)}, u32[]{:S(2)}) collective-permute-start(bf16[3,448,1792]{2,1,0:T(8,128)(2,1)} %pack.3), channel_id=1, source_target_pairs={{0,12},{1,13},{2,14},{3,15},{4,0},{5,1},{6,2},{7,3},{8,4},{9,5},{1... | collective-permute-start | bytes 14450696 | tf_op jit(solution)/shard_map/ppermute | solution.py:231
  44.6 12.8 %all-to-all-start.1 = ((bf16[8,4,8,896]{3,2,1,0:T(8,128)(2,1)}), bf16[8,4,8,896]{3,2,1,0:T(8,128)(2,1)S(1)}, u32[]{:S(2)}, u32[]{:S(2)}) async-start(bf16[8,4,8,896]{3,2,1,0:T(8,128)(2,1)} %attend.1), calls=%async_computation.1 | async-start | bytes 917504 | tf_op jit(solution)/shard_map/all_to_all | solution.py:220
  75.2 12.8 %collective-permute-start = (bf16[128,1792]{1,0:T(8,128)(2,1)S(1)}, bf16[128,1792]{1,0:T(8,128)(2,1)S(1)}, u32[]{:S(2)}, u32[]{:S(2)}) collective-permute-start(bf16[128,1792]{1,0:T(8,128)(2,1)S(1)} %bitcast.46), channel_id=1, source_target_pairs={{0,2},{1,3},{2,0},{3,1},{4,6},{5,7},{6,4},{7,5},{8,10},{9,11},{10,... | collective-permute-start | bytes 1376264 | tf_op jit(solution)/shard_map/ppermute | solution.py:231
  75.8 12.5 %collective-permute-start.4 = (bf16[128,1792]{1,0:T(8,128)(2,1)S(1)}, bf16[128,1792]{1,0:T(8,128)(2,1)S(1)}, u32[]{:S(2)}, u32[]{:S(2)}) collective-permute-start(bf16[128,1792]{1,0:T(8,128)(2,1)S(1)} %bitcast.42), channel_id=1, source_target_pairs={{0,8},{1,9},{2,10},{3,11},{4,12},{5,13},{6,14},{7,15},{8,0},{9,1},... | collective-permute-start | bytes 1376264 | tf_op jit(solution)/shard_map/ppermute | solution.py:231
  76.5 23.1 %collective-permute-start.2 = (bf16[128,1792]{1,0:T(8,128)(2,1)S(1)}, bf16[128,1792]{1,0:T(8,128)(2,1)S(1)}, u32[]{:S(2)}, u32[]{:S(2)}) collective-permute-start(bf16[128,1792]{1,0:T(8,128)(2,1)S(1)} %bitcast.47), channel_id=1, source_target_pairs={{0,4},{1,5},{2,6},{3,7},{4,8},{5,9},{6,10},{7,11},{8,12},{9,13},{1... | collective-permute-start | bytes 1376264 | tf_op jit(solution)/shard_map/ppermute | solution.py:231
  88.0 11.8 %collective-permute-start.9 = (bf16[128,1792]{1,0:T(8,128)(2,1)S(1)}, bf16[128,1792]{1,0:T(8,128)(2,1)S(1)}, u32[]{:S(2)}, u32[]{:S(2)}) collective-permute-start(bf16[128,1792]{1,0:T(8,128)(2,1)S(1)} %bitcast.43), channel_id=1, source_target_pairs={{0,1},{1,2},{2,3},{3,0},{4,5},{5,6},{6,7},{7,4},{8,9},{9,10},{10,1... | collective-permute-start | bytes 1376264 | tf_op jit(solution)/shard_map/ppermute | solution.py:231
  88.3 21.1 %collective-permute-start.3 = (bf16[128,1792]{1,0:T(8,128)(2,1)S(1)}, bf16[128,1792]{1,0:T(8,128)(2,1)S(1)}, u32[]{:S(2)}, u32[]{:S(2)}) collective-permute-start(bf16[128,1792]{1,0:T(8,128)(2,1)S(1)} %collective-permute-done.refs_1_), channel_id=1, source_target_pairs={{0,4},{1,5},{2,6},{3,7},{4,8},{5,9},{6,10},{7,11},{8,12},{9,13},{1... | collective-permute-start | bytes 1376264 | tf_op jit(solution)/shard_map/ppermute | solution.py:231
  99.6 12.7 %collective-permute-start.10 = (bf16[128,1792]{1,0:T(8,128)(2,1)S(1)}, bf16[128,1792]{1,0:T(8,128)(2,1)S(1)}, u32[]{:S(2)}, u32[]{:S(2)}) collective-permute-start(bf16[128,1792]{1,0:T(8,128)(2,1)S(1)} %collective-permute-done.4.refs_1_), channel_id=1, source_target_pairs={{0,1},{1,2},{2,3},{3,0},{4,5},{5,6},{6,7},{7,4},{8,9},{9,10},{10,1... | collective-permute-start | bytes 1376264 | tf_op jit(solution)/shard_map/ppermute | solution.py:231
  99.7 12.5 %collective-permute-start.8 = (bf16[128,1792]{1,0:T(8,128)(2,1)S(1)}, bf16[128,1792]{1,0:T(8,128)(2,1)S(1)}, u32[]{:S(2)}, u32[]{:S(2)}) collective-permute-start(bf16[128,1792]{1,0:T(8,128)(2,1)S(1)} %collective-permute-done.refs_1_), channel_id=1, source_target_pairs={{0,12},{1,13},{2,14},{3,15},{4,0},{5,1},{6,2},{7,3},{8,4},{9,5},{1... | collective-permute-start | bytes 1376264 | tf_op jit(solution)/shard_map/ppermute | solution.py:231
  109.4 24.3 %collective-permute-start.7 = (bf16[128,1792]{1,0:T(8,128)(2,1)S(1)}, bf16[128,1792]{1,0:T(8,128)(2,1)S(1)}, u32[]{:S(2)}, u32[]{:S(2)}) collective-permute-start(bf16[128,1792]{1,0:T(8,128)(2,1)S(1)} %bitcast.48), channel_id=1, source_target_pairs={{0,12},{1,13},{2,14},{3,15},{4,0},{5,1},{6,2},{7,3},{8,4},{9,5},{1... | collective-permute-start | bytes 1376264 | tf_op jit(solution)/shard_map/ppermute | solution.py:231
  112.3 24.9 %collective-permute-start.14 = (bf16[128,1792]{1,0:T(8,128)(2,1)S(1)}, bf16[128,1792]{1,0:T(8,128)(2,1)S(1)}, u32[]{:S(2)}, u32[]{:S(2)}) collective-permute-start(bf16[128,1792]{1,0:T(8,128)(2,1)S(1)} %bitcast.44), channel_id=1, source_target_pairs={{0,3},{1,0},{2,1},{3,2},{4,7},{5,4},{6,5},{7,6},{8,11},{9,8},{10,9... | collective-permute-start | bytes 1376264 | tf_op jit(solution)/shard_map/ppermute | solution.py:231
  112.3 24.9 %collective-permute-start.15 = (bf16[128,1792]{1,0:T(8,128)(2,1)S(1)}, bf16[128,1792]{1,0:T(8,128)(2,1)S(1)}, u32[]{:S(2)}, u32[]{:S(2)}) collective-permute-start(bf16[128,1792]{1,0:T(8,128)(2,1)S(1)} %collective-permute-done.4.refs_1_), channel_id=1, source_target_pairs={{0,3},{1,0},{2,1},{3,2},{4,7},{5,4},{6,5},{7,6},{8,11},{9,8},{10,9... | collective-permute-start | bytes 1376264 | tf_op jit(solution)/shard_map/ppermute | solution.py:231
  113.5 26.8 %collective-permute-start.12 = (bf16[128,1792]{1,0:T(8,128)(2,1)S(1)}, bf16[128,1792]{1,0:T(8,128)(2,1)S(1)}, u32[]{:S(2)}, u32[]{:S(2)}) collective-permute-start(bf16[128,1792]{1,0:T(8,128)(2,1)S(1)} %collective-permute-done.2.refs_0_), channel_id=1, source_target_pairs={{0,4},{1,5},{2,6},{3,7},{4,8},{5,9},{6,10},{7,11},{8,12},{9,13},{1... | collective-permute-start | bytes 1376264 | tf_op jit(solution)/shard_map/ppermute | solution.py:231
  113.5 26.8 %collective-permute-start.13 = (bf16[128,1792]{1,0:T(8,128)(2,1)S(1)}, bf16[128,1792]{1,0:T(8,128)(2,1)S(1)}, u32[]{:S(2)}, u32[]{:S(2)}) collective-permute-start(bf16[128,1792]{1,0:T(8,128)(2,1)S(1)} %collective-permute-done.8.refs_1_), channel_id=1, source_target_pairs={{0,12},{1,13},{2,14},{3,15},{4,0},{5,1},{6,2},{7,3},{8,4},{9,5},{1... | collective-permute-start | bytes 1376264 | tf_op jit(solution)/shard_map/ppermute | solution.py:231
  143.5 19.7 %collective-permute-start.16 = (bf16[256,1792]{1,0:T(8,128)(2,1)S(1)}, bf16[256,1792]{1,0:T(8,128)(2,1)S(1)}, u32[]{:S(2)}, u32[]{:S(2)}) collective-permute-start(bf16[256,1792]{1,0:T(8,128)(2,1)S(1)} %mlp.14), channel_id=1, source_target_pairs={{0,8},{1,9},{2,10},{3,11},{4,12},{5,13},{6,14},{7,15},{8,0},{9,1},... | collective-permute-start | bytes 2752520 | tf_op jit(solution)/shard_map/ppermute | solution.py:231
  143.6 43.0 %collective-permute-start.11 = (bf16[256,1792]{1,0:T(8,128)(2,1)S(1)}, bf16[256,1792]{1,0:T(8,128)(2,1)S(1)}, u32[]{:S(2)}, u32[]{:S(2)}) collective-permute-start(bf16[256,1792]{1,0:T(8,128)(2,1)S(1)} %mlp.12), channel_id=1, source_target_pairs={{0,4},{1,5},{2,6},{3,7},{4,8},{5,9},{6,10},{7,11},{8,12},{9,13},{1... | collective-permute-start | bytes 2752520 | tf_op jit(solution)/shard_map/ppermute | solution.py:231
  144.2 42.4 %collective-permute-start.6 = (bf16[256,1792]{1,0:T(8,128)(2,1)S(1)}, bf16[256,1792]{1,0:T(8,128)(2,1)S(1)}, u32[]{:S(2)}, u32[]{:S(2)}) collective-permute-start(bf16[256,1792]{1,0:T(8,128)(2,1)S(1)} %mlp.10), channel_id=1, source_target_pairs={{0,12},{1,13},{2,14},{3,15},{4,0},{5,1},{6,2},{7,3},{8,4},{9,5},{1... | collective-permute-start | bytes 2752520 | tf_op jit(solution)/shard_map/ppermute | solution.py:231
  155.2 39.0 %collective-permute-start.19 = (bf16[256,1792]{1,0:T(8,128)(2,1)S(1)}, bf16[256,1792]{1,0:T(8,128)(2,1)S(1)}, u32[]{:S(2)}, u32[]{:S(2)}) collective-permute-start(bf16[256,1792]{1,0:T(8,128)(2,1)S(1)} %mlp.13), channel_id=1, source_target_pairs={{0,1},{1,2},{2,3},{3,0},{4,5},{5,6},{6,7},{7,4},{8,9},{9,10},{10,1... | collective-permute-start | bytes 2752520 | tf_op jit(solution)/shard_map/ppermute | solution.py:231
  158.4 35.8 %collective-permute-start.22 = (bf16[256,1792]{1,0:T(8,128)(2,1)S(1)}, bf16[256,1792]{1,0:T(8,128)(2,1)S(1)}, u32[]{:S(2)}, u32[]{:S(2)}) collective-permute-start(bf16[256,1792]{1,0:T(8,128)(2,1)S(1)} %mlp.15), channel_id=1, source_target_pairs={{0,2},{1,3},{2,0},{3,1},{4,6},{5,7},{6,4},{7,5},{8,10},{9,11},{10,... | collective-permute-start | bytes 2752520 | tf_op jit(solution)/shard_map/ppermute | solution.py:231
  163.2 42.8 %collective-permute-start.18 = (bf16[256,1792]{1,0:T(8,128)(2,1)S(1)}, bf16[256,1792]{1,0:T(8,128)(2,1)S(1)}, u32[]{:S(2)}, u32[]{:S(2)}) collective-permute-start(bf16[256,1792]{1,0:T(8,128)(2,1)S(1)} %mlp.11), channel_id=1, source_target_pairs={{0,3},{1,0},{2,1},{3,2},{4,7},{5,4},{6,5},{7,6},{8,11},{9,8},{10,9... | collective-permute-start | bytes 2752520 | tf_op jit(solution)/shard_map/ppermute | solution.py:231
  186.8 21.1 %collective-permute-start.17 = (bf16[128,1792]{1,0:T(8,128)(2,1)S(1)}, bf16[128,1792]{1,0:T(8,128)(2,1)S(1)}, u32[]{:S(2)}, u32[]{:S(2)}) collective-permute-start(bf16[128,1792]{1,0:T(8,128)(2,1)S(1)} %add_convert_fusion.3), channel_id=1, source_target_pairs={{0,2},{1,3},{2,0},{3,1},{4,6},{5,7},{6,4},{7,5},{8,10},{9,11},{10,... | collective-permute-start | bytes 1376264 | tf_op jit(solution)/shard_map/ppermute | solution.py:231
  206.3 9.9 %collective-permute-start.23 = (bf16[128,1792]{1,0:T(8,128)(2,1)S(1)}, bf16[128,1792]{1,0:T(8,128)(2,1)S(1)}, u32[]{:S(2)}, u32[]{:S(2)}) collective-permute-start(bf16[128,1792]{1,0:T(8,128)(2,1)S(1)} %add_convert_fusion.1), channel_id=1, source_target_pairs={{0,8},{1,9},{2,10},{3,11},{4,12},{5,13},{6,14},{7,15},{8,0},{9,1},... | collective-permute-start | bytes 1376264 | tf_op jit(solution)/shard_map/ppermute | solution.py:231
  217.5 21.6 %all-to-all-start.3 = ((bf16[8,2,16,1792]{3,2,1,0:T(8,128)(2,1)}), bf16[8,2,16,1792]{3,2,1,0:T(8,128)(2,1)S(1)}, u32[]{:S(2)}, u32[]{:S(2)}) async-start(bf16[8,2,16,1792]{3,2,1,0:T(8,128)(2,1)} %pad_maximum_fusion), calls=%async_computation.3 | async-start | bytes 1835008 | tf_op jit(solution)/shard_map/all_to_all | solution.py:305
  (11 other events, 329.2 us)

commit v3 on v2

--- a/solution.py
+++ b/solution.py
@@ -27,8 +27,10 @@
     col_site = lax.broadcasted_iota(jnp.int32, (2 * rows, rows), 1) % sites
     same_site = row_site == col_site
     low_head = lax.broadcasted_iota(jnp.int32, (rows, LANES), 1) < HD
-    for pair in range(width // LANES):
-        cols = pl.ds(pair * LANES, LANES)
+
+    @pl.loop(0, width // LANES)
+    def _(pair):
+        cols = pl.ds(pl.multiple_of(pair * LANES, LANES), LANES)
         query = qkv_ref[:, 0, :, :, cols].reshape(rows, LANES)
         key = qkv_ref[:, 1, :, :, cols].reshape(rows, LANES)
         value = qkv_ref[:, 2, :, :, cols].reshape(rows, LANES)
@@ -90,21 +92,23 @@
     out_ref[...] = (hidden_ref[...] + moved).astype(out_ref.dtype)
 
 
-def mlp_kernel(index, pieces, *refs):
-    gate, up, down, near, out = refs[pieces:]
-    rows = [ref[...] for ref in refs[:pieces]]
-    rows = rows[0] if pieces == 1 else jnp.concatenate(rows, axis=0)
-    total = None
-    for gate_w, up_w, down_w in (
-        (gate.at[index], up.at[index], down.at[index]),
-        (near.at[0], near.at[1], near.at[2]),
-    ):
-        gate_val = nt_dot(rows, gate_w[...])
-        up_val = nt_dot(rows, up_w[...])
+def mlp_kernel(pieces, *refs):
+    weights = refs[pieces]
+    outs = refs[pieces + 1 : -1]
+    total = refs[-1]
+    rows = jnp.concatenate([ref[...] for ref in refs[:pieces]], axis=0)
+    total[...] = jnp.zeros(total.shape, total.dtype)
+
+    @pl.loop(0, weights.shape[0])
+    def _(i):
+        gate_val = nt_dot(rows, weights[i, 0])
+        up_val = nt_dot(rows, weights[i, 1])
         active = (gate_val / (1.0 + jnp.exp(-gate_val)) * up_val).astype(jnp.bfloat16)
-        part = jnp.dot(active, down_w[...], preferred_element_type=jnp.float32)
-        total = part if total is None else total + part
-    out[...] = total.astype(out.dtype)
+        total[...] += jnp.dot(active, weights[i, 2], preferred_element_type=jnp.float32)
+
+    count = total.shape[0] // pieces
+    for i, out in enumerate(outs):
+        out[...] = total[i * count : (i + 1) * count].astype(out.dtype)
 
 
 def on_chip(count):
@@ -115,16 +119,17 @@
     return pltpu.CompilerParams(vmem_limit_bytes=mebibytes << 20)
 
 
-def mlp(pieces, index, gate, up, down, near):
-    count = sum(piece.shape[0] for piece in pieces)
+def mlp(pieces, dtype, weights):
+    rows = sum(piece.shape[0] for piece in pieces)
     return pl.pallas_call(
-        lambda *refs: mlp_kernel(index, len(pieces), *refs),
-        in_specs=on_chip(len(pieces) + 4),
-        out_specs=on_chip(1)[0],
-        out_shape=jax.ShapeDtypeStruct((count, pieces[0].shape[1]), jnp.bfloat16),
-        compiler_params=grant(24),
+        lambda *refs: mlp_kernel(len(pieces), *refs),
+        in_specs=on_chip(len(pieces) + 1),
+        out_specs=tuple(on_chip(len(pieces))),
+        out_shape=tuple(jax.ShapeDtypeStruct(piece.shape, dtype) for piece in pieces),
+        scratch_shapes=[pltpu.VMEM((rows, pieces[0].shape[1]), jnp.float32)],
+        compiler_params=grant(18),
         name="mlp",
-    )(*pieces, gate, up, down, near)
+    )(*pieces, weights)
 
 
 def pack_kernel(gate, up, down, out_ref):
@@ -146,27 +151,28 @@
     )(gate, up, down)
 
 
-def land_kernel(source, out_ref, sem):
+def land_kernel(own, near, out_ref, sem):
     copies = [
-        pltpu.make_async_copy(source.at[i], out_ref.at[i], sem.at[i])
-        for i in range(source.shape[0])
+        pltpu.make_async_copy(near.at[i], out_ref.at[1, i], sem.at[i])
+        for i in range(near.shape[0])
     ]
     for copy in copies:
         copy.start()
+    out_ref[0] = own[...]
     for copy in copies:
         copy.wait()
 
 
-def land(value):
+def land(own, near):
     return pl.pallas_call(
         land_kernel,
-        in_specs=[pl.BlockSpec(memory_space=pltpu.HBM)],
+        in_specs=on_chip(1) + [pl.BlockSpec(memory_space=pltpu.HBM)],
         out_specs=on_chip(1)[0],
-        out_shape=pltpu.VMEM(value.shape, value.dtype),
-        scratch_shapes=[pltpu.SemaphoreType.DMA((value.shape[0],))],
-        compiler_params=grant(6),
+        out_shape=pltpu.VMEM((2, *own.shape), own.dtype),
+        scratch_shapes=[pltpu.SemaphoreType.DMA((own.shape[0],))],
+        compiler_params=grant(16),
         name="land",
-    )(value)
+    )(own, near)
 
 
 def hop(sizes, move):
@@ -234,9 +240,9 @@
     packed_b = pack(1, gate, up, w_down)
     near_a = send(packed_a, hop(sizes, lambda y, c, z, x: (y, c, z, x - 1 + 2 * c)))
     near_b = send(packed_b, hop(sizes, lambda y, c, z, x: (y, c, z - 1 + 2 * c, x)))
-    near = []
-    for value in (near_a, near_b):
-        near.append(land(value))
+    weights = []
+    for own_part, near_part in ((packed_a, near_a), (packed_b, near_b)):
+        weights.append(land(own_part, near_part))
 
     target = jnp.where(slot_index >= 0, expert_ids * capacity + slot_index, -1)
     target = target.reshape(tokens, 2)
@@ -271,36 +277,42 @@
             out.append(send(values[e], moves[e](steps)))
         return out
 
-    def run(e, pieces, after):
-        pieces, _ = lax.optimization_barrier((pieces, after))
-        return mlp(pieces, e, gate, up, w_down, near[e])
+    done = ()
+
+    def run(e, pieces, dtype=bf16):
+        nonlocal done
+        pieces, _ = lax.optimization_barrier((pieces, done))
+        done = mlp(pieces, dtype, weights[e])
+        return done
 
     other = send_all(mine, far, 2)
-    ahead = [send_all(mine, ring, 1)]
-    behind = [send_all(mine, ring, -1)]
-    ahead.append(send_all(other, ring, 1))
-    behind.append(send_all(other, ring, -1))
-    across = [send_all(ahead[0], ring, 1), send_all(behind[1], ring, -1)]
-    done = ()
-    parts = []
-    for e in range(2):
-        done = run(e, [mine[e], other[e]], done)
-        parts.append([done])
-    for pieces, steps in ((ahead, -1), (behind, 1), (across, 2)):
-        for e in range(2):
-            done = run(e, [pieces[0][e], pieces[1][e]], done)
-            parts[e].append(send(done, ring[e](steps)))
-
-    def add(pieces):
+    ahead_mine = send_all(mine, ring, 1)
+    behind_mine = send_all(mine, ring, -1)
+    ahead_other = send_all(other, ring, 1)
+    behind_other = send_all(other, ring, -1)
+    cross_mine = send_all(ahead_mine, ring, 1)
+    cross_other = send_all(behind_other, ring, -1)
+    own = [run(e, [mine[e], other[e]]) for e in range(2)]
+    first = [run(e, [ahead_mine[e], behind_other[e]]) for e in range(2)]
+    first_mine = send_all([out[0] for out in first], ring, -1)
+    first_other = send_all([out[1] for out in first], ring, 1)
+    cross = [run(e, [cross_mine[e], cross_other[e]]) for e in range(2)]
+    pass_mine = send_all([out[0] for out in cross], ring, 1)
+    pass_other = send_all([out[1] for out in cross], ring, -1)
+    late = [run(e, [ahead_other[e], behind_mine[e]], jnp.float32) for e in range(2)]
+
+    def add(*pieces):
         total = pieces[0].astype(jnp.float32)
         for piece in pieces[1:]:
             total = total + piece.astype(jnp.float32)
         return total.astype(bf16)
 
-    summed = []
-    for e in range(2):
-        opposite = add([part[part_rows:] for part in parts[e]])
-        summed.append(add([part[:part_rows] for part in parts[e]] + [send(opposite, far[e](2))]))
+    last_other = send_all([add(late[e][0], pass_other[e]) for e in range(2)], ring, -1)
+    last_mine = send_all([add(late[e][1], pass_mine[e]) for e in range(2)], ring, 1)
+    swapped = send_all([add(own[e][1], first_other[e], last_other[e]) for e in range(2)], far, 2)
+    summed = [
+        add(own[e][0], first_mine[e], last_mine[e], swapped[e]) for e in range(2)
+    ]
     ready = jnp.stack([part.reshape(groups, capacity, model_width) for part in summed], axis=1)
     back = lax.all_to_all(ready, "ep", split_axis=0, concat_axis=0, tiled=True)
     combined = pl.pallas_call(

time: 242 us -> 235 us (0.971)
  waiting for transfers between devices: 115 us -> 84.6 us
  starting transfers between devices: 32.8 us -> 46.8 us
  Pallas kernels: 45.4 us -> 51.3 us
    ppermute x24 -> x30, waiting for transfers between devices: 92.8 us -> 62.7 us  [send(): return lax.ppermute(value, ('ep', 'tp'), pairs)]
    ppermute x24 -> x30, starting transfers between devices: 20.6 us -> 27.8 us  [send(): return lax.ppermute(value, ('ep', 'tp'), pairs)]
    all_to_all x1, starting transfers between devices: 8.04 us -> 14.9 us  [block(): back = lax.all_to_all(ready, 'ep', split_axis=0, concat_axis=0, tiled=True)]
    pallas_call x10, Pallas kernels: 30.4 us -> 34 us  [the longest x8 29.2 us: mlp(): pl.pallas_call(lambda *refs: mlp_kernel(len(pieces), *refs), in_specs=on_...]
  transfers between devices with their start and end apart: 26 -> 32, of which waited for: 13 -> 11; matrix products, arithmetic and copies ran while one was open for 1% -> 1% of each run, Pallas kernels for 15% -> 19%
where the time goes in v3:
time: 235 us; the launch traced here: 233 us
  waiting for transfers between devices  84.6 us (36%)
  Pallas kernels  51.3 us (22%)
  starting transfers between devices  46.8 us (20%)
  blocking collectives  44.7 us (19%)
  local copies, waits for them, and re-layouts  2.89 us (1%)
    ppermute x30, waiting for transfers between devices, send(): return lax.ppermute(value, ('ep', 'tp'), pairs)  62.7 us
    pallas_call x8, Pallas kernels, mlp(): pl.pallas_call(lambda *refs: mlp_kernel(len(pieces), *refs), in_specs=on_...  29.2 us
    ppermute x30, starting transfers between devices, send(): return lax.ppermute(value, ('ep', 'tp'), pairs)  27.8 us
    all_to_all x1, blocking collectives, block(): lax.all_to_all(spread, 'ep', split_axis=0, concat_axis=0, tiled=True)  27.6 us
    all_to_all x1, blocking collectives, block(): lax.all_to_all(rows.reshape(groups, experts_local, capacity, model_width)...  17.1 us
    all_to_all x1, starting transfers between devices, block(): back = lax.all_to_all(ready, 'ep', split_axis=0, concat_axis=0, tiled=True)  14.9 us
    all_to_all x1, waiting for transfers between devices, block(): back = lax.all_to_all(ready, 'ep', split_axis=0, concat_axis=0, tiled=True)  13.5 us
    pallas_call x2, Pallas kernels, pack(): pl.pallas_call(pack_kernel, grid=(steps,), in_specs=[pl.BlockSpec((None,...  10.1 us
  transfers between devices with their start and end apart: 32, of which 11 were waited for; matrix products, arithmetic and copies ran while one was open for 1% of the time, Pallas kernels for 19%

profile of v3, /device:TPU:1, one launch (start us, length us, event | category | flops | bytes accessed | tf_op | source)
XLA Modules:
  0.0 232.9 jit_solution(12814044371351181415)
XLA Ops:
  0.0 5.0 %pack.2.own = bf16[3,448,1792]{2,1,0:T(8,128)(2,1)} custom-call(bf16[2,448,1792]{2,1,0:T(8,128)(2,1)} %bitcast.36, bf16[2,448,1792]{2,1,0:T(8,128)(2,1)} %bitcast.38, bf16[2,448,1792]{2,1,0:T(8,128)(2,1)} %down.3), custom_call_target="tpu_custom_call" | custom-call | tf_op jit(solution)/shard_map/pack/pallas_call | solution.py:143
  7.1 5.1 %pack.3.own = bf16[3,448,1792]{2,1,0:T(8,128)(2,1)} custom-call(bf16[2,448,1792]{2,1,0:T(8,128)(2,1)} %bitcast.37, bf16[2,448,1792]{2,1,0:T(8,128)(2,1)} %bitcast.39, bf16[2,448,1792]{2,1,0:T(8,128)(2,1)} %down.3), custom_call_target="tpu_custom_call" | custom-call | tf_op jit(solution)/shard_map/pack/pallas_call | solution.py:143
  14.0 27.6 %all_to_all.20.qkv_ref = bf16[8,3,4,8,896]{4,3,2,1,0:T(8,128)(2,1)S(1)} all-to-all(bf16[8,3,4,8,896]{4,3,2,1,0:T(8,128)(2,1)S(1)} %bitcast.40), channel_id=1, replica_groups=mesh['ep'=8,'tp'=16] {'ep'}, dimensions={0} | all-to-all | bytes 2752512 | tf_op jit(solution)/shard_map/all_to_all | solution.py:218
  41.6 5.4 %attend.1 = bf16[8,4,8,896]{3,2,1,0:T(8,128)(2,1)} custom-call(bf16[8,3,4,8,896]{4,3,2,1,0:T(8,128)(2,1)S(1)} %all_to_all.20.qkv_ref), custom_call_target="tpu_custom_call" | custom-call | tf_op jit(solution)/shard_map/attend/pallas_call | solution.py:219
  47.0 4.1 %all-to-all-start.1 = ((bf16[8,4,8,896]{3,2,1,0:T(8,128)(2,1)}), bf16[8,4,8,896]{3,2,1,0:T(8,128)(2,1)S(1)}, u32[]{:S(2)}, u32[]{:S(2)}) async-start(bf16[8,4,8,896]{3,2,1,0:T(8,128)(2,1)} %attend.1), calls=%async_computation.1 | async-start | bytes 917504 | tf_op jit(solution)/shard_map/all_to_all | solution.py:226
  51.3 8.5 %all-to-all-done.1.att_ref = bf16[8,4,8,896]{3,2,1,0:T(8,128)(2,1)S(1)} async-done(((bf16[8,4,8,896]{3,2,1,0:T(8,128)(2,1)}), bf16[8,4,8,896]{3,2,1,0:T(8,128)(2,1)S(1)}, u32[]{:S(2)}, u32[]{:S(2)}) %all-to-all-start.1) | async-done | bytes 458784 | tf_op jit(solution)/shard_map/all_to_all | solution.py:226
  60.4 17.1 %all_to_all.21 = bf16[8,2,16,1792]{3,2,1,0:T(8,128)(2,1)S(1)} all-to-all(bf16[8,2,16,1792]{3,2,1,0:T(8,128)(2,1)S(1)} %bitcast.32), channel_id=1, replica_groups=mesh['ep'=8,'tp'=16] {'ep'}, dimensions={0} | all-to-all | bytes 1835008 | tf_op jit(solution)/shard_map/all_to_all | solution.py:262
  78.9 11.5 %collective-permute-done.refs_1_ = bf16[128,1792]{1,0:T(8,128)(2,1)S(1)} collective-permute-done((bf16[128,1792]{1,0:T(8,128)(2,1)S(1)}, bf16[128,1792]{1,0:T(8,128)(2,1)S(1)}, u32[]{:S(2)}, u32[]{:S(2)}) %collective-permute-start) | collective-permute-done | bytes 458784 | tf_op jit(solution)/shard_map/ppermute | solution.py:237
  90.7 11.2 %collective-permute-done.2.refs_0_ = bf16[128,1792]{1,0:T(8,128)(2,1)S(1)} collective-permute-done((bf16[128,1792]{1,0:T(8,128)(2,1)S(1)}, bf16[128,1792]{1,0:T(8,128)(2,1)S(1)}, u32[]{:S(2)}, u32[]{:S(2)}) %collective-permute-start.2) | collective-permute-done | bytes 458784 | tf_op jit(solution)/shard_map/ppermute | solution.py:237
  103.5 10.0 %collective-permute-done.11.refs_1_ = bf16[128,1792]{1,0:T(8,128)(2,1)S(1)} collective-permute-done((bf16[128,1792]{1,0:T(8,128)(2,1)S(1)}, bf16[128,1792]{1,0:T(8,128)(2,1)S(1)}, u32[]{:S(2)}, u32[]{:S(2)}) %collective-permute-start.11) | collective-permute-done | bytes 458784 | tf_op jit(solution)/shard_map/ppermute | solution.py:237
  120.4 3.6 %mlp.8 = (bf16[128,1792]{1,0:T(8,128)(2,1)S(1)}, bf16[128,1792]{1,0:T(8,128)(2,1)S(1)}) custom-call(bf16[128,1792]{1,0:T(8,128)(2,1)S(1)} %bitcast.30, bf16[128,1792]{1,0:T(8,128)(2,1)S(1)} %collective-permute-done.refs_1_, bf16[2,3,448,1792]{3,2,1,0:T(8,128)(2,1)S(1)} %land.2.refs_2_), custom_call_target="tpu_custom_call" | custom-call | tf_op jit(solution)/shard_map/mlp/pallas_call | solution.py:124
  128.0 3.6 %mlp.9 = (bf16[128,1792]{1,0:T(8,128)(2,1)S(1)}, bf16[128,1792]{1,0:T(8,128)(2,1)S(1)}) custom-call(bf16[128,1792]{1,0:T(8,128)(2,1)S(1)} %bitcast.26, bf16[128,1792]{1,0:T(8,128)(2,1)S(1)} %collective-permute-done.4.refs_1_, bf16[2,3,448,1792]{3,2,1,0:T(8,128)(2,1)S(1)} %land.3.refs_2_), custom_call_target="tpu_custom_call" | custom-call | tf_op jit(solution)/shard_map/mlp/pallas_call | solution.py:124
  131.7 3.6 %mlp.10 = (bf16[128,1792]{1,0:T(8,128)(2,1)S(1)}, bf16[128,1792]{1,0:T(8,128)(2,1)S(1)}) custom-call(bf16[128,1792]{1,0:T(8,128)(2,1)S(1)} %collective-permute-done.2.refs_0_, bf16[128,1792]{1,0:T(8,128)(2,1)S(1)} %collective-permute-done.3.refs_1_, bf16[2,3,448,1792]{3,2,1,0:T(8,128)(2,1)S(1)} %land.2.refs_2_), custom_call_target="tpu_custom_call" | custom-call | tf_op jit(solution)/shard_map/mlp/pallas_call | solution.py:124
  135.6 3.6 %mlp.11 = (bf16[128,1792]{1,0:T(8,128)(2,1)S(1)}, bf16[128,1792]{1,0:T(8,128)(2,1)S(1)}) custom-call(bf16[128,1792]{1,0:T(8,128)(2,1)S(1)} %collective-permute-done.9.refs_0_, bf16[128,1792]{1,0:T(8,128)(2,1)S(1)} %collective-permute-done.11.refs_1_, bf16[2,3,448,1792]{3,2,1,0:T(8,128)(2,1)S(1)} %land.3.refs_2_), custom_call_target="tpu_custom_call" | custom-call | tf_op jit(solution)/shard_map/mlp/pallas_call | solution.py:124
  140.8 3.6 %mlp.12 = (bf16[128,1792]{1,0:T(8,128)(2,1)S(1)}, bf16[128,1792]{1,0:T(8,128)(2,1)S(1)}) custom-call(bf16[128,1792]{1,0:T(8,128)(2,1)S(1)} %collective-permute-done.13.refs_0_, bf16[128,1792]{1,0:T(8,128)(2,1)S(1)} %collective-permute-done.14.refs_1_, bf16[2,3,448,1792]{3,2,1,0:T(8,128)(2,1)S(1)} %land.2.refs_2_), custom_call_target="tpu_custom_call" | custom-call | tf_op jit(solution)/shard_map/mlp/pallas_call | solution.py:124
  146.0 3.6 %mlp.13 = (bf16[128,1792]{1,0:T(8,128)(2,1)S(1)}, bf16[128,1792]{1,0:T(8,128)(2,1)S(1)}) custom-call(bf16[128,1792]{1,0:T(8,128)(2,1)S(1)} %collective-permute-done.10.refs_0_, bf16[128,1792]{1,0:T(8,128)(2,1)S(1)} %collective-permute-done.12.refs_1_, bf16[2,3,448,1792]{3,2,1,0:T(8,128)(2,1)S(1)} %land.3.refs_2_), custom_call_target="tpu_custom_call" | custom-call | tf_op jit(solution)/shard_map/mlp/pallas_call | solution.py:124
  151.2 3.7 %mlp.14 = (f32[128,1792]{1,0:T(8,128)S(1)}, f32[128,1792]{1,0:T(8,128)S(1)}) custom-call(bf16[128,1792]{1,0:T(8,128)(2,1)S(1)} %collective-permute-done.7.refs_0_, bf16[128,1792]{1,0:T(8,128)(2,1)S(1)} %collective-permute-done.8.refs_1_, bf16[2,3,448,1792]{3,2,1,0:T(8,128)(2,1)S(1)} %land.2.refs_2_), custom_call_target="tpu_custom_call" | custom-call | tf_op jit(solution)/shard_map/mlp/pallas_call | solution.py:124
  157.4 3.7 %mlp.15 = (f32[128,1792]{1,0:T(8,128)S(1)}, f32[128,1792]{1,0:T(8,128)S(1)}) custom-call(bf16[128,1792]{1,0:T(8,128)(2,1)S(1)} %collective-permute-done.22.refs_0_, bf16[128,1792]{1,0:T(8,128)(2,1)S(1)} %collective-permute-done.23.refs_1_, bf16[2,3,448,1792]{3,2,1,0:T(8,128)(2,1)S(1)} %land.3.refs_2_), custom_call_target="tpu_custom_call" | custom-call | tf_op jit(solution)/shard_map/mlp/pallas_call | solution.py:124
  171.2 6.0 %collective-permute-done.19 = bf16[128,1792]{1,0:T(8,128)(2,1)S(1)} collective-permute-done((bf16[128,1792]{1,0:T(8,128)(2,1)S(1)}, bf16[128,1792]{1,0:T(8,128)(2,1)S(1)}, u32[]{:S(2)}, u32[]{:S(2)}) %collective-permute-start.19) | collective-permute-done | bytes 458784 | tf_op jit(solution)/shard_map/ppermute | solution.py:237
  177.2 3.4 %collective-permute-start.28 = (bf16[128,1792]{1,0:T(8,128)(2,1)S(1)}, bf16[128,1792]{1,0:T(8,128)(2,1)S(1)}, u32[]{:S(2)}, u32[]{:S(2)}) collective-permute-start(bf16[128,1792]{1,0:T(8,128)(2,1)S(1)} %add_convert_fusion.2), channel_id=1, source_target_pairs={{0,3},{1,0},{2,1},{3,2},{4,7},{5,4},{6,5},{7,6},{8,11},{9,8},{10,9... | collective-permute-start | bytes 1376264 | tf_op jit(solution)/shard_map/ppermute | solution.py:237
  180.9 8.0 %collective-permute-done.28 = bf16[128,1792]{1,0:T(8,128)(2,1)S(1)} collective-permute-done((bf16[128,1792]{1,0:T(8,128)(2,1)S(1)}, bf16[128,1792]{1,0:T(8,128)(2,1)S(1)}, u32[]{:S(2)}, u32[]{:S(2)}) %collective-permute-start.28) | collective-permute-done | bytes 458784 | tf_op jit(solution)/shard_map/ppermute | solution.py:237
  191.3 10.3 %collective-permute-done.20 = bf16[128,1792]{1,0:T(8,128)(2,1)S(1)} collective-permute-done((bf16[128,1792]{1,0:T(8,128)(2,1)S(1)}, bf16[128,1792]{1,0:T(8,128)(2,1)S(1)}, u32[]{:S(2)}, u32[]{:S(2)}) %collective-permute-start.20) | collective-permute-done | bytes 458784 | tf_op jit(solution)/shard_map/ppermute | solution.py:237
  203.2 14.9 %all-to-all-start.3 = ((bf16[8,2,16,1792]{3,2,1,0:T(8,128)(2,1)}), bf16[8,2,16,1792]{3,2,1,0:T(8,128)(2,1)S(1)}, u32[]{:S(2)}, u32[]{:S(2)}) async-start(bf16[8,2,16,1792]{3,2,1,0:T(8,128)(2,1)} %pad_maximum_fusion), calls=%async_computation.3 | async-start | bytes 1835008 | tf_op jit(solution)/shard_map/all_to_all | solution.py:317
  218.2 13.5 %all-to-all-done.3 = bf16[8,2,16,1792]{3,2,1,0:T(8,128)(2,1)S(1)} async-done(((bf16[8,2,16,1792]{3,2,1,0:T(8,128)(2,1)}), bf16[8,2,16,1792]{3,2,1,0:T(8,128)(2,1)S(1)}, u32[]{:S(2)}, u32[]{:S(2)}) %all-to-all-start.3) | async-done | bytes 917536 | tf_op jit(solution)/shard_map/all_to_all | solution.py:317
  (92 shorter events, 41.7 us)
Async XLA Ops:
  5.0 108.5 %collective-permute-start.1 = (bf16[3,448,1792]{2,1,0:T(8,128)(2,1)}, bf16[3,448,1792]{2,1,0:T(8,128)(2,1)}, u32[]{:S(2)}, u32[]{:S(2)}) collective-permute-start(bf16[3,448,1792]{2,1,0:T(8,128)(2,1)} %pack.2.own), channel_id=1, source_target_pairs={{0,3},{1,0},{2,1},{3,2},{4,7},{5,4},{6,5},{7,6},{8,11},{9,8},{10,9... | collective-permute-start | bytes 14450696 | tf_op jit(solution)/shard_map/ppermute | solution.py:237
  12.2 111.9 %collective-permute-start.5 = (bf16[3,448,1792]{2,1,0:T(8,128)(2,1)}, bf16[3,448,1792]{2,1,0:T(8,128)(2,1)}, u32[]{:S(2)}, u32[]{:S(2)}) collective-permute-start(bf16[3,448,1792]{2,1,0:T(8,128)(2,1)} %pack.3.own), channel_id=1, source_target_pairs={{0,12},{1,13},{2,14},{3,15},{4,0},{5,1},{6,2},{7,3},{8,4},{9,5},{1... | collective-permute-start | bytes 14450696 | tf_op jit(solution)/shard_map/ppermute | solution.py:237
  47.0 12.8 %all-to-all-start.1 = ((bf16[8,4,8,896]{3,2,1,0:T(8,128)(2,1)}), bf16[8,4,8,896]{3,2,1,0:T(8,128)(2,1)S(1)}, u32[]{:S(2)}, u32[]{:S(2)}) async-start(bf16[8,4,8,896]{3,2,1,0:T(8,128)(2,1)} %attend.1), calls=%async_computation.1 | async-start | bytes 917504 | tf_op jit(solution)/shard_map/all_to_all | solution.py:226
  77.6 12.8 %collective-permute-start = (bf16[128,1792]{1,0:T(8,128)(2,1)S(1)}, bf16[128,1792]{1,0:T(8,128)(2,1)S(1)}, u32[]{:S(2)}, u32[]{:S(2)}) collective-permute-start(bf16[128,1792]{1,0:T(8,128)(2,1)S(1)} %bitcast.28), channel_id=1, source_target_pairs={{0,2},{1,3},{2,0},{3,1},{4,6},{5,7},{6,4},{7,5},{8,10},{9,11},{10,... | collective-permute-start | bytes 1376264 | tf_op jit(solution)/shard_map/ppermute | solution.py:237
  78.2 12.5 %collective-permute-start.4 = (bf16[128,1792]{1,0:T(8,128)(2,1)S(1)}, bf16[128,1792]{1,0:T(8,128)(2,1)S(1)}, u32[]{:S(2)}, u32[]{:S(2)}) collective-permute-start(bf16[128,1792]{1,0:T(8,128)(2,1)S(1)} %bitcast.24), channel_id=1, source_target_pairs={{0,8},{1,9},{2,10},{3,11},{4,12},{5,13},{6,14},{7,15},{8,0},{9,1},... | collective-permute-start | bytes 1376264 | tf_op jit(solution)/shard_map/ppermute | solution.py:237
  78.9 23.0 %collective-permute-start.2 = (bf16[128,1792]{1,0:T(8,128)(2,1)S(1)}, bf16[128,1792]{1,0:T(8,128)(2,1)S(1)}, u32[]{:S(2)}, u32[]{:S(2)}) collective-permute-start(bf16[128,1792]{1,0:T(8,128)(2,1)S(1)} %bitcast.29), channel_id=1, source_target_pairs={{0,4},{1,5},{2,6},{3,7},{4,8},{5,9},{6,10},{7,11},{8,12},{9,13},{1... | collective-permute-start | bytes 1376264 | tf_op jit(solution)/shard_map/ppermute | solution.py:237
  102.8 32.5 %collective-permute-start.13 = (bf16[128,1792]{1,0:T(8,128)(2,1)S(1)}, bf16[128,1792]{1,0:T(8,128)(2,1)S(1)}, u32[]{:S(2)}, u32[]{:S(2)}) collective-permute-start(bf16[128,1792]{1,0:T(8,128)(2,1)S(1)} %collective-permute-done.2.refs_0_), channel_id=1, source_target_pairs={{0,4},{1,5},{2,6},{3,7},{4,8},{5,9},{6,10},{7,11},{8,12},{9,13},{1... | collective-permute-start | bytes 1376264 | tf_op jit(solution)/shard_map/ppermute | solution.py:237
  102.8 36.5 %collective-permute-start.10 = (bf16[128,1792]{1,0:T(8,128)(2,1)S(1)}, bf16[128,1792]{1,0:T(8,128)(2,1)S(1)}, u32[]{:S(2)}, u32[]{:S(2)}) collective-permute-start(bf16[128,1792]{1,0:T(8,128)(2,1)S(1)} %collective-permute-done.9.refs_0_), channel_id=1, source_target_pairs={{0,1},{1,2},{2,3},{3,0},{4,5},{5,6},{6,7},{7,4},{8,9},{9,10},{10,1... | collective-permute-start | bytes 1376264 | tf_op jit(solution)/shard_map/ppermute | solution.py:237
  113.5 25.8 %collective-permute-start.14 = (bf16[128,1792]{1,0:T(8,128)(2,1)S(1)}, bf16[128,1792]{1,0:T(8,128)(2,1)S(1)}, u32[]{:S(2)}, u32[]{:S(2)}) collective-permute-start(bf16[128,1792]{1,0:T(8,128)(2,1)S(1)} %collective-permute-done.3.refs_1_), channel_id=1, source_target_pairs={{0,12},{1,13},{2,14},{3,15},{4,0},{5,1},{6,2},{7,3},{8,4},{9,5},{1... | collective-permute-start | bytes 1376264 | tf_op jit(solution)/shard_map/ppermute | solution.py:237
  113.5 31.0 %collective-permute-start.12 = (bf16[128,1792]{1,0:T(8,128)(2,1)S(1)}, bf16[128,1792]{1,0:T(8,128)(2,1)S(1)}, u32[]{:S(2)}, u32[]{:S(2)}) collective-permute-start(bf16[128,1792]{1,0:T(8,128)(2,1)S(1)} %collective-permute-done.11.refs_1_), channel_id=1, source_target_pairs={{0,3},{1,0},{2,1},{3,2},{4,7},{5,4},{6,5},{7,6},{8,11},{9,8},{10,9... | collective-permute-start | bytes 1376264 | tf_op jit(solution)/shard_map/ppermute | solution.py:237
  124.0 25.6 %collective-permute-start.8 = (bf16[128,1792]{1,0:T(8,128)(2,1)S(1)}, bf16[128,1792]{1,0:T(8,128)(2,1)S(1)}, u32[]{:S(2)}, u32[]{:S(2)}) collective-permute-start(bf16[128,1792]{1,0:T(8,128)(2,1)S(1)} %bitcast.31), channel_id=1, source_target_pairs={{0,12},{1,13},{2,14},{3,15},{4,0},{5,1},{6,2},{7,3},{8,4},{9,5},{1... | collective-permute-start | bytes 1376264 | tf_op jit(solution)/shard_map/ppermute | solution.py:237
  135.3 15.6 %collective-permute-start.7 = (bf16[128,1792]{1,0:T(8,128)(2,1)S(1)}, bf16[128,1792]{1,0:T(8,128)(2,1)S(1)}, u32[]{:S(2)}, u32[]{:S(2)}) collective-permute-start(bf16[128,1792]{1,0:T(8,128)(2,1)S(1)} %collective-permute-done.refs_1_), channel_id=1, source_target_pairs={{0,4},{1,5},{2,6},{3,7},{4,8},{5,9},{6,10},{7,11},{8,12},{9,13},{1... | collective-permute-start | bytes 1376264 | tf_op jit(solution)/shard_map/ppermute | solution.py:237
  139.3 15.6 %collective-permute-start.23 = (bf16[128,1792]{1,0:T(8,128)(2,1)S(1)}, bf16[128,1792]{1,0:T(8,128)(2,1)S(1)}, u32[]{:S(2)}, u32[]{:S(2)}) collective-permute-start(bf16[128,1792]{1,0:T(8,128)(2,1)S(1)} %bitcast.27), channel_id=1, source_target_pairs={{0,3},{1,0},{2,1},{3,2},{4,7},{5,4},{6,5},{7,6},{8,11},{9,8},{10,9... | collective-permute-start | bytes 1376264 | tf_op jit(solution)/shard_map/ppermute | solution.py:237
  139.4 18.0 %collective-permute-start.22 = (bf16[128,1792]{1,0:T(8,128)(2,1)S(1)}, bf16[128,1792]{1,0:T(8,128)(2,1)S(1)}, u32[]{:S(2)}, u32[]{:S(2)}) collective-permute-start(bf16[128,1792]{1,0:T(8,128)(2,1)S(1)} %collective-permute-done.4.refs_1_), channel_id=1, source_target_pairs={{0,1},{1,2},{2,3},{3,0},{4,5},{5,6},{6,7},{7,4},{8,9},{9,10},{10,1... | collective-permute-start | bytes 1376264 | tf_op jit(solution)/shard_map/ppermute | solution.py:237
  144.5 16.6 %collective-permute-start.15 = (bf16[128,1792]{1,0:T(8,128)(2,1)S(1)}, bf16[128,1792]{1,0:T(8,128)(2,1)S(1)}, u32[]{:S(2)}, u32[]{:S(2)}) collective-permute-start(bf16[128,1792]{1,0:T(8,128)(2,1)S(1)} %get-tuple-element.59), channel_id=1, source_target_pairs={{0,4},{1,5},{2,6},{3,7},{4,8},{5,9},{6,10},{7,11},{8,12},{9,13},{1... | collective-permute-start | bytes 1376264 | tf_op jit(solution)/shard_map/ppermute | solution.py:237
  149.6 14.3 %collective-permute-start.18 = (bf16[128,1792]{1,0:T(8,128)(2,1)S(1)}, bf16[128,1792]{1,0:T(8,128)(2,1)S(1)}, u32[]{:S(2)}, u32[]{:S(2)}) collective-permute-start(bf16[128,1792]{1,0:T(8,128)(2,1)S(1)} %get-tuple-element.60), channel_id=1, source_target_pairs={{0,12},{1,13},{2,14},{3,15},{4,0},{5,1},{6,2},{7,3},{8,4},{9,5},{1... | collective-permute-start | bytes 1376264 | tf_op jit(solution)/shard_map/ppermute | solution.py:237
  151.0 19.0 %collective-permute-start.17 = (bf16[128,1792]{1,0:T(8,128)(2,1)S(1)}, bf16[128,1792]{1,0:T(8,128)(2,1)S(1)}, u32[]{:S(2)}, u32[]{:S(2)}) collective-permute-start(bf16[128,1792]{1,0:T(8,128)(2,1)S(1)} %get-tuple-element.52), channel_id=1, source_target_pairs={{0,4},{1,5},{2,6},{3,7},{4,8},{5,9},{6,10},{7,11},{8,12},{9,13},{1... | collective-permute-start | bytes 1376264 | tf_op jit(solution)/shard_map/ppermute | solution.py:237
  154.9 36.2 %collective-permute-start.6 = (bf16[128,1792]{1,0:T(8,128)(2,1)S(1)}, bf16[128,1792]{1,0:T(8,128)(2,1)S(1)}, u32[]{:S(2)}, u32[]{:S(2)}) collective-permute-start(bf16[128,1792]{1,0:T(8,128)(2,1)S(1)} %get-tuple-element.51), channel_id=1, source_target_pairs={{0,12},{1,13},{2,14},{3,15},{4,0},{5,1},{6,2},{7,3},{8,4},{9,5},{1... | collective-permute-start | bytes 1376264 | tf_op jit(solution)/shard_map/ppermute | solution.py:237
  163.9 16.9 %collective-permute-start.26 = (bf16[128,1792]{1,0:T(8,128)(2,1)S(1)}, bf16[128,1792]{1,0:T(8,128)(2,1)S(1)}, u32[]{:S(2)}, u32[]{:S(2)}) collective-permute-start(bf16[128,1792]{1,0:T(8,128)(2,1)S(1)} %get-tuple-element.56), channel_id=1, source_target_pairs={{0,1},{1,2},{2,3},{3,0},{4,5},{5,6},{6,7},{7,4},{8,9},{9,10},{10,1... | collective-permute-start | bytes 1376264 | tf_op jit(solution)/shard_map/ppermute | solution.py:237
  166.8 35.0 %collective-permute-start.21 = (bf16[128,1792]{1,0:T(8,128)(2,1)S(1)}, bf16[128,1792]{1,0:T(8,128)(2,1)S(1)}, u32[]{:S(2)}, u32[]{:S(2)}) collective-permute-start(bf16[128,1792]{1,0:T(8,128)(2,1)S(1)} %get-tuple-element.55), channel_id=1, source_target_pairs={{0,3},{1,0},{2,1},{3,2},{4,7},{5,4},{6,5},{7,6},{8,11},{9,8},{10,9... | collective-permute-start | bytes 1376264 | tf_op jit(solution)/shard_map/ppermute | solution.py:237
  170.0 21.3 %collective-permute-start.16 = (bf16[128,1792]{1,0:T(8,128)(2,1)S(1)}, bf16[128,1792]{1,0:T(8,128)(2,1)S(1)}, u32[]{:S(2)}, u32[]{:S(2)}) collective-permute-start(bf16[128,1792]{1,0:T(8,128)(2,1)S(1)} %add_convert_fusion.7), channel_id=1, source_target_pairs={{0,4},{1,5},{2,6},{3,7},{4,8},{5,9},{6,10},{7,11},{8,12},{9,13},{1... | collective-permute-start | bytes 1376264 | tf_op jit(solution)/shard_map/ppermute | solution.py:237
  180.8 21.0 %collective-permute-start.25 = (bf16[128,1792]{1,0:T(8,128)(2,1)S(1)}, bf16[128,1792]{1,0:T(8,128)(2,1)S(1)}, u32[]{:S(2)}, u32[]{:S(2)}) collective-permute-start(bf16[128,1792]{1,0:T(8,128)(2,1)S(1)} %add_convert_fusion.3), channel_id=1, source_target_pairs={{0,1},{1,2},{2,3},{3,0},{4,5},{5,6},{6,7},{7,4},{8,9},{9,10},{10,1... | collective-permute-start | bytes 1376264 | tf_op jit(solution)/shard_map/ppermute | solution.py:237
  188.9 12.7 %collective-permute-start.20 = (bf16[128,1792]{1,0:T(8,128)(2,1)S(1)}, bf16[128,1792]{1,0:T(8,128)(2,1)S(1)}, u32[]{:S(2)}, u32[]{:S(2)}) collective-permute-start(bf16[128,1792]{1,0:T(8,128)(2,1)S(1)} %add_convert_fusion.5), channel_id=1, source_target_pairs={{0,2},{1,3},{2,0},{3,1},{4,6},{5,7},{6,4},{7,5},{8,10},{9,11},{10,... | collective-permute-start | bytes 1376264 | tf_op jit(solution)/shard_map/ppermute | solution.py:237
  203.2 28.5 %all-to-all-start.3 = ((bf16[8,2,16,1792]{3,2,1,0:T(8,128)(2,1)}), bf16[8,2,16,1792]{3,2,1,0:T(8,128)(2,1)S(1)}, u32[]{:S(2)}, u32[]{:S(2)}) async-start(bf16[8,2,16,1792]{3,2,1,0:T(8,128)(2,1)} %pad_maximum_fusion), calls=%async_computation.3 | async-start | bytes 1835008 | tf_op jit(solution)/shard_map/all_to_all | solution.py:317
  (17 other events, 393.0 us)

commit v4 on v3

--- a/solution.py
+++ b/solution.py
@@ -27,10 +27,8 @@
     col_site = lax.broadcasted_iota(jnp.int32, (2 * rows, rows), 1) % sites
     same_site = row_site == col_site
     low_head = lax.broadcasted_iota(jnp.int32, (rows, LANES), 1) < HD
-
-    @pl.loop(0, width // LANES)
-    def _(pair):
-        cols = pl.ds(pl.multiple_of(pair * LANES, LANES), LANES)
+    for pair in range(width // LANES):
+        cols = pl.ds(pair * LANES, LANES)
         query = qkv_ref[:, 0, :, :, cols].reshape(rows, LANES)
         key = qkv_ref[:, 1, :, :, cols].reshape(rows, LANES)
         value = qkv_ref[:, 2, :, :, cols].reshape(rows, LANES)
@@ -79,11 +77,27 @@
     )
 
 
-def combine_kernel(hidden_ref, rows_ref, target_ref, gate_ref, out_ref):
-    tokens = hidden_ref.shape[0]
-    returned = rows_ref[...]
+def settle_kernel(position, *refs):
+    own, moved, outs = refs[:2], refs[2:8], refs[8:]
+    count = outs[0].shape[1]
+    for k, out in enumerate(outs):
+        start = pl.multiple_of((position[0] ^ k) * count, count)
+        cut = pl.ds(start, count)
+        for e in range(2):
+            total = own[e][cut].astype(jnp.float32)
+            for part in moved[3 * e : 3 * e + 3]:
+                total = total + part[cut].astype(jnp.float32)
+            out[e] = total.astype(out.dtype)
+
+
+def combine_kernel(hidden_ref, target_ref, gate_ref, *refs):
+    pieces, out_ref = refs[:-1], refs[-1]
+    tokens, width = hidden_ref.shape
+    returned = jnp.concatenate(
+        [piece[e] for piece in pieces for e in range(piece.shape[0])], axis=0
+    )
     col = lax.broadcasted_iota(jnp.int32, (tokens, returned.shape[0]), 1)
-    moved = jnp.zeros(hidden_ref.shape, jnp.float32)
+    moved = jnp.zeros((tokens, width), jnp.float32)
     for choice in range(2):
         target = target_ref[:, choice : choice + 1]
         picker = jnp.where(col == target, 1.0, 0.0).astype(jnp.bfloat16)
@@ -132,47 +146,54 @@
     )(*pieces, weights)
 
 
-def pack_kernel(gate, up, down, out_ref):
-    for i, source in enumerate((gate, up, down)):
-        out_ref[i] = source[...]
-
-
-def pack(index, gate, up, down):
+def pack_kernel(*refs):
+    for i, source in enumerate(refs[:-1]):
+        refs[-1][i] = source[...]
+
+
+def pack(index, *sources):
     steps = 4
-    _, rows, width = gate.shape
+    _, rows, width = sources[0].shape
+    count = len(sources)
     return pl.pallas_call(
         pack_kernel,
         grid=(steps,),
-        in_specs=[pl.BlockSpec((None, rows // steps, width), lambda i: (index, i, 0))] * 3,
-        out_specs=pl.BlockSpec((3, rows // steps, width), lambda i: (0, i, 0)),
-        out_shape=jax.ShapeDtypeStruct((3, rows, width), gate.dtype),
+        in_specs=[pl.BlockSpec((None, rows // steps, width), lambda i: (index, i, 0))] * count,
+        out_specs=pl.BlockSpec((count, rows // steps, width), lambda i: (0, i, 0)),
+        out_shape=jax.ShapeDtypeStruct((count, rows, width), sources[0].dtype),
         compiler_params=grant(58),
         name="pack",
-    )(gate, up, down)
-
-
-def land_kernel(own, near, out_ref, sem):
+    )(*sources)
+
+
+def land_kernel(index, gate, up, down, near_gate, near_rest, out_ref, sem):
+    sources = (
+        (gate.at[index], up.at[index], down.at[index]),
+        (near_gate.at[0], near_rest.at[0], near_rest.at[1]),
+    )
     copies = [
-        pltpu.make_async_copy(near.at[i], out_ref.at[1, i], sem.at[i])
-        for i in range(near.shape[0])
+        pltpu.make_async_copy(source, out_ref.at[i, j], sem.at[i, j])
+        for i, group in enumerate(sources)
+        for j, source in enumerate(group)
     ]
     for copy in copies:
         copy.start()
-    out_ref[0] = own[...]
     for copy in copies:
         copy.wait()
 
 
-def land(own, near):
+def land(index, *sources):
+    held = [pltpu.with_memory_space_constraint(source, pltpu.HBM) for source in sources]
+    _, rows, width = sources[0].shape
     return pl.pallas_call(
-        land_kernel,
-        in_specs=on_chip(1) + [pl.BlockSpec(memory_space=pltpu.HBM)],
+        lambda *refs: land_kernel(index, *refs),
+        in_specs=[pl.BlockSpec(memory_space=pltpu.HBM)] * len(held),
         out_specs=on_chip(1)[0],
-        out_shape=pltpu.VMEM((2, *own.shape), own.dtype),
-        scratch_shapes=[pltpu.SemaphoreType.DMA((own.shape[0],))],
-        compiler_params=grant(16),
+        out_shape=pltpu.VMEM((2, 3, rows, width), sources[0].dtype),
+        scratch_shapes=[pltpu.SemaphoreType.DMA((2, 3))],
+        compiler_params=grant(11),
         name="land",
-    )(own, near)
+    )(*held)
 
 
 def hop(sizes, move):
@@ -236,13 +257,18 @@
     def send(value, pairs):
         return lax.ppermute(value, ("ep", "tp"), pairs)
 
-    packed_a = pack(0, gate, up, w_down)
-    packed_b = pack(1, gate, up, w_down)
-    near_a = send(packed_a, hop(sizes, lambda y, c, z, x: (y, c, z, x - 1 + 2 * c)))
-    near_b = send(packed_b, hop(sizes, lambda y, c, z, x: (y, c, z - 1 + 2 * c, x)))
+    beside = (
+        hop(sizes, lambda y, c, z, x: (y, c, z, x - 1 + 2 * c)),
+        hop(sizes, lambda y, c, z, x: (y, c, z - 1 + 2 * c, x)),
+    )
+    near = [[], []]
+    for sources in ((gate,), (up, w_down)):
+        for e in range(2):
+            packed = pack(e, *sources)
+            near[e].append(send(packed, beside[e]))
     weights = []
-    for own_part, near_part in ((packed_a, near_a), (packed_b, near_b)):
-        weights.append(land(own_part, near_part))
+    for e in range(2):
+        weights.append(land(e, gate, up, w_down, *near[e]))
 
     target = jnp.where(slot_index >= 0, expert_ids * capacity + slot_index, -1)
     target = target.reshape(tokens, 2)
@@ -309,19 +335,51 @@
 
     last_other = send_all([add(late[e][0], pass_other[e]) for e in range(2)], ring, -1)
     last_mine = send_all([add(late[e][1], pass_mine[e]) for e in range(2)], ring, 1)
-    swapped = send_all([add(own[e][1], first_other[e], last_other[e]) for e in range(2)], far, 2)
-    summed = [
-        add(own[e][0], first_mine[e], last_mine[e], swapped[e]) for e in range(2)
-    ]
-    ready = jnp.stack([part.reshape(groups, capacity, model_width) for part in summed], axis=1)
-    back = lax.all_to_all(ready, "ep", split_axis=0, concat_axis=0, tiled=True)
+    swapped = send_all(
+        [add(own[e][1], first_other[e], last_other[e]) for e in range(2)], far, 2
+    )
+    position = lax.axis_index("ep")
+    pieces = pl.pallas_call(
+        settle_kernel,
+        in_specs=[pl.BlockSpec(memory_space=pltpu.SMEM)] + on_chip(8),
+        out_specs=tuple(on_chip(groups)),
+        out_shape=tuple(
+            jax.ShapeDtypeStruct((experts_local, capacity, model_width), bf16)
+            for _ in range(groups)
+        ),
+        compiler_params=grant(12),
+        name="settle",
+    )(
+        position.astype(jnp.int32).reshape(1),
+        own[0][0],
+        own[1][0],
+        first_mine[0],
+        last_mine[0],
+        swapped[0],
+        first_mine[1],
+        last_mine[1],
+        swapped[1],
+    )
+
+    def toggle(mask):
+        def move(y, c, z, x):
+            place = (2 * y + c) ^ mask
+            return (place // 2, place % 2, z, x)
+
+        return hop(sizes, move)
+
+    back = list(pieces)
+    for k in (4, 5, 2, 3, 6, 7, 1):
+        back[k] = send(pieces[k], toggle(k))
+    place = ((expert_ids // experts_local) ^ position) * experts_local
+    place = (place + expert_ids % experts_local) * capacity + slot_index
     combined = pl.pallas_call(
         combine_kernel,
         out_shape=jax.ShapeDtypeStruct((tokens, model_width), bf16),
-        in_specs=on_chip(4),
+        in_specs=on_chip(3 + groups),
         compiler_params=grant(12),
         name="combine",
-    )(hidden, back.reshape(slots, model_width), target, gates)
+    )(hidden, jnp.where(slot_index >= 0, place, -1).reshape(tokens, 2), gates, *back)
     return combined.reshape(frames_local, sites_local, model_width)
 
 

time: 235 us -> 246 us (1.047)
  starting transfers between devices: 46.8 us -> 77 us
  blocking collectives: 44.7 us -> 22.3 us
  Pallas kernels: 51.3 us -> 57.9 us
    ppermute x30 -> x39, starting transfers between devices: 27.8 us -> 66.7 us  [send(): return lax.ppermute(value, ('ep', 'tp'), pairs)]
    all_to_all x1 -> x0, blocking collectives: 27.6 us -> none  [block(): lax.all_to_all(spread, 'ep', split_axis=0, concat_axis=0, tiled=True)]
    ppermute x30 -> x39, waiting for transfers between devices: 62.7 us -> 76.8 us  [send(): return lax.ppermute(value, ('ep', 'tp'), pairs)]
    all_to_all x1, starting transfers between devices: 14.9 us -> 5.96 us  [block(): lax.all_to_all(spread, 'ep', split_axis=0, concat_axis=0, tiled=True)]
    all_to_all x1, waiting for transfers between devices: 8.45 us -> 0.01 us  [block(): lax.all_to_all(mixed, 'ep', split_axis=0, concat_axis=0, tiled=True)]
    all_to_all x1, waiting for transfers between devices: 13.5 us -> 7.19 us  [block(): lax.all_to_all(spread, 'ep', split_axis=0, concat_axis=0, tiled=True)]
    pallas_call x2 -> x4, Pallas kernels: 10.1 us -> 15.7 us  [pack(): pl.pallas_call(pack_kernel, grid=(steps,), in_specs=[pl.BlockSpec((None,...]
    all_to_all x1, blocking collectives: 17.1 us -> 22.3 us  [block(): lax.all_to_all(rows.reshape(groups, experts_local, capacity, model_width)...]
  transfers between devices with their start and end apart: 32 -> 41, of which waited for: 11 -> 18; matrix products, arithmetic and copies ran while one was open for 1% -> 0% of each run, Pallas kernels for 19% -> 23%
where the time goes in v4:
time: 246 us; the launch traced here: 245 us
  waiting for transfers between devices  84 us (34%)
  starting transfers between devices  77 us (31%)
  Pallas kernels  57.9 us (24%)
  blocking collectives  22.3 us (9%)
  local copies, waits for them, and re-layouts  2.95 us (1%)
    ppermute x39, waiting for transfers between devices, send(): return lax.ppermute(value, ('ep', 'tp'), pairs)  76.8 us
    ppermute x39, starting transfers between devices, send(): return lax.ppermute(value, ('ep', 'tp'), pairs)  66.7 us
    pallas_call x8, Pallas kernels, mlp(): pl.pallas_call(lambda *refs: mlp_kernel(len(pieces), *refs), in_specs=on_...  29.2 us
    all_to_all x1, blocking collectives, block(): lax.all_to_all(rows.reshape(groups, experts_local, capacity, model_width)...  22.3 us
    pallas_call x4, Pallas kernels, pack(): pl.pallas_call(pack_kernel, grid=(steps,), in_specs=[pl.BlockSpec((None,...  15.7 us
    pallas_call x2, Pallas kernels, land(): pl.pallas_call(lambda *refs: land_kernel(index, *refs), in_specs=[pl.Bloc...  7.68 us
    all_to_all x1, waiting for transfers between devices, block(): lax.all_to_all(spread, 'ep', split_axis=0, concat_axis=0, tiled=True)  7.19 us
    all_to_all x1, starting transfers between devices, block(): lax.all_to_all(spread, 'ep', split_axis=0, concat_axis=0, tiled=True)  5.96 us
  transfers between devices with their start and end apart: 41, of which 18 were waited for; matrix products, arithmetic and copies ran while one was open for 0% of the time, Pallas kernels for 23%

profile of v4, /device:TPU:1, one launch (start us, length us, event | category | flops | bytes accessed | tf_op | source)
XLA Modules:
  0.0 245.0 jit_solution(11348798821480155551)
XLA Ops:
  2.6 6.0 %all-to-all-start = ((bf16[8,3,4,8,896]{4,3,2,1,0:T(8,128)(2,1)}), bf16[8,3,4,8,896]{4,3,2,1,0:T(8,128)(2,1)S(1)}, u32[]{:S(2)}, u32[]{:S(2)}) async-start(bf16[8,3,4,8,896]{4,3,2,1,0:T(8,128)(2,1)} %bitcast.2), calls=%async_computation | async-start | bytes 2752512 | tf_op jit(solution)/shard_map/all_to_all | solution.py:239
  8.5 4.2 %pack.5 = bf16[2,448,1792]{2,1,0:T(8,128)(2,1)} custom-call(bf16[2,448,1792]{2,1,0:T(8,128)(2,1)} %bitcast.32, bf16[2,448,1792]{2,1,0:T(8,128)(2,1)} %refs_2_.3), custom_call_target="tpu_custom_call" | custom-call | tf_op jit(solution)/shard_map/pack/pallas_call | solution.py:158
  14.0 4.2 %pack.7 = bf16[2,448,1792]{2,1,0:T(8,128)(2,1)} custom-call(bf16[2,448,1792]{2,1,0:T(8,128)(2,1)} %bitcast.33, bf16[2,448,1792]{2,1,0:T(8,128)(2,1)} %refs_2_.3), custom_call_target="tpu_custom_call" | custom-call | tf_op jit(solution)/shard_map/pack/pallas_call | solution.py:158
  19.8 7.2 %all-to-all-done.qkv_ref = bf16[8,3,4,8,896]{4,3,2,1,0:T(8,128)(2,1)S(1)} async-done(((bf16[8,3,4,8,896]{4,3,2,1,0:T(8,128)(2,1)}), bf16[8,3,4,8,896]{4,3,2,1,0:T(8,128)(2,1)S(1)}, u32[]{:S(2)}, u32[]{:S(2)}) %all-to-all-start) | async-done | bytes 1376288 | tf_op jit(solution)/shard_map/all_to_all | solution.py:239
  30.0 4.3 %all-to-all-start.1 = ((bf16[8,4,8,896]{3,2,1,0:T(8,128)(2,1)}), bf16[8,4,8,896]{3,2,1,0:T(8,128)(2,1)S(1)}, u32[]{:S(2)}, u32[]{:S(2)}) async-start(bf16[8,4,8,896]{3,2,1,0:T(8,128)(2,1)} %attend.1), calls=%async_computation.1 | async-start | bytes 917504 | tf_op jit(solution)/shard_map/all_to_all | solution.py:247
  45.3 22.3 %all_to_all.15 = bf16[8,2,16,1792]{3,2,1,0:T(8,128)(2,1)S(1)} all-to-all(bf16[8,2,16,1792]{3,2,1,0:T(8,128)(2,1)S(1)} %bitcast.24), channel_id=1, replica_groups=mesh['ep'=8,'tp'=16] {'ep'}, dimensions={0} | all-to-all | bytes 1835008 | tf_op jit(solution)/shard_map/all_to_all | solution.py:288
  75.0 5.4 %collective-permute-done.refs_1_ = bf16[128,1792]{1,0:T(8,128)(2,1)S(1)} collective-permute-done((bf16[128,1792]{1,0:T(8,128)(2,1)S(1)}, bf16[128,1792]{1,0:T(8,128)(2,1)S(1)}, u32[]{:S(2)}, u32[]{:S(2)}) %collective-permute-start) | collective-permute-done | bytes 458784 | tf_op jit(solution)/shard_map/ppermute | solution.py:258
  80.4 4.7 %collective-permute-start.11 = (bf16[128,1792]{1,0:T(8,128)(2,1)S(1)}, bf16[128,1792]{1,0:T(8,128)(2,1)S(1)}, u32[]{:S(2)}, u32[]{:S(2)}) collective-permute-start(bf16[128,1792]{1,0:T(8,128)(2,1)S(1)} %bitcast.17), channel_id=1, source_target_pairs={{0,1},{1,2},{2,3},{3,0},{4,5},{5,6},{6,7},{7,4},{8,9},{9,10},{10,1... | collective-permute-start | bytes 1376264 | tf_op jit(solution)/shard_map/ppermute | solution.py:258
  85.2 5.4 %collective-permute-done.6.refs_0_ = bf16[128,1792]{1,0:T(8,128)(2,1)S(1)} collective-permute-done((bf16[128,1792]{1,0:T(8,128)(2,1)S(1)}, bf16[128,1792]{1,0:T(8,128)(2,1)S(1)}, u32[]{:S(2)}, u32[]{:S(2)}) %collective-permute-start.6) | collective-permute-done | bytes 458784 | tf_op jit(solution)/shard_map/ppermute | solution.py:258
  90.6 3.9 %collective-permute-done.11.refs_0_ = bf16[128,1792]{1,0:T(8,128)(2,1)S(1)} collective-permute-done((bf16[128,1792]{1,0:T(8,128)(2,1)S(1)}, bf16[128,1792]{1,0:T(8,128)(2,1)S(1)}, u32[]{:S(2)}, u32[]{:S(2)}) %collective-permute-start.11) | collective-permute-done | bytes 458784 | tf_op jit(solution)/shard_map/ppermute | solution.py:258
  103.0 3.8 %land.2.refs_2_ = bf16[2,3,448,1792]{3,2,1,0:T(8,128)(2,1)S(1)} custom-call(bf16[2,448,1792]{2,1,0:T(8,128)(2,1)} %bitcast.30, bf16[2,448,1792]{2,1,0:T(8,128)(2,1)} %bitcast.34, bf16[2,448,1792]{2,1,0:T(8,128)(2,1)} %refs_2_.3, bf16[1,448,1792]{2,1,0:T(8,128)(2,1)} %collective-permute-done.1.refs_3_, bf16[2,448,1792]{2,1,0:T(8,128)(2,1)} %collective-permute-done.2.refs_4_), custom_call_target="tpu_custom_call" | custom-call | tf_op jit(solution)/shard_map/land/pallas_call | solution.py:188
  111.6 3.8 %land.3.refs_2_ = bf16[2,3,448,1792]{3,2,1,0:T(8,128)(2,1)S(1)} custom-call(bf16[2,448,1792]{2,1,0:T(8,128)(2,1)} %bitcast.31, bf16[2,448,1792]{2,1,0:T(8,128)(2,1)} %bitcast.35, bf16[2,448,1792]{2,1,0:T(8,128)(2,1)} %refs_2_.3, bf16[1,448,1792]{2,1,0:T(8,128)(2,1)} %copy-done.1, bf16[2,448,1792]{2,1,0:T(8,128)(2,1)} %collective-permute-done.5.refs_4_), custom_call_target="tpu_custom_call" | custom-call | tf_op jit(solution)/shard_map/land/pallas_call | solution.py:188
  115.4 3.6 %mlp.9 = (bf16[128,1792]{1,0:T(8,128)(2,1)S(1)}, bf16[128,1792]{1,0:T(8,128)(2,1)S(1)}) custom-call(bf16[128,1792]{1,0:T(8,128)(2,1)S(1)} %bitcast.18, bf16[128,1792]{1,0:T(8,128)(2,1)S(1)} %collective-permute-done.3.refs_1_, bf16[2,3,448,1792]{3,2,1,0:T(8,128)(2,1)S(1)} %land.3.refs_2_), custom_call_target="tpu_custom_call" | custom-call | tf_op jit(solution)/shard_map/mlp/pallas_call | solution.py:138
  131.8 3.6 %mlp.12 = (bf16[128,1792]{1,0:T(8,128)(2,1)S(1)}, bf16[128,1792]{1,0:T(8,128)(2,1)S(1)}) custom-call(bf16[128,1792]{1,0:T(8,128)(2,1)S(1)} %collective-permute-done.15.refs_0_, bf16[128,1792]{1,0:T(8,128)(2,1)S(1)} %collective-permute-done.16.refs_1_, bf16[2,3,448,1792]{3,2,1,0:T(8,128)(2,1)S(1)} %land.2.refs_2_), custom_call_target="tpu_custom_call" | custom-call | tf_op jit(solution)/shard_map/mlp/pallas_call | solution.py:138
  141.3 3.7 %mlp.14 = (f32[128,1792]{1,0:T(8,128)S(1)}, f32[128,1792]{1,0:T(8,128)S(1)}) custom-call(bf16[128,1792]{1,0:T(8,128)(2,1)S(1)} %collective-permute-done.9.refs_0_, bf16[128,1792]{1,0:T(8,128)(2,1)S(1)} %collective-permute-done.10.refs_1_, bf16[2,3,448,1792]{3,2,1,0:T(8,128)(2,1)S(1)} %land.2.refs_2_), custom_call_target="tpu_custom_call" | custom-call | tf_op jit(solution)/shard_map/mlp/pallas_call | solution.py:138
  149.3 3.7 %mlp.15 = (f32[128,1792]{1,0:T(8,128)S(1)}, f32[128,1792]{1,0:T(8,128)S(1)}) custom-call(bf16[128,1792]{1,0:T(8,128)(2,1)S(1)} %collective-permute-done.24.refs_0_, bf16[128,1792]{1,0:T(8,128)(2,1)S(1)} %collective-permute-done.25.refs_1_, bf16[2,3,448,1792]{3,2,1,0:T(8,128)(2,1)S(1)} %land.3.refs_2_), custom_call_target="tpu_custom_call" | custom-call | tf_op jit(solution)/shard_map/mlp/pallas_call | solution.py:138
  153.1 9.2 %collective-permute-done.17 = bf16[128,1792]{1,0:T(8,128)(2,1)S(1)} collective-permute-done((bf16[128,1792]{1,0:T(8,128)(2,1)S(1)}, bf16[128,1792]{1,0:T(8,128)(2,1)S(1)}, u32[]{:S(2)}, u32[]{:S(2)}) %collective-permute-start.17) | collective-permute-done | bytes 458784 | tf_op jit(solution)/shard_map/ppermute | solution.py:258
  165.3 5.3 %collective-permute-done.29 = bf16[128,1792]{1,0:T(8,128)(2,1)S(1)} collective-permute-done((bf16[128,1792]{1,0:T(8,128)(2,1)S(1)}, bf16[128,1792]{1,0:T(8,128)(2,1)S(1)}, u32[]{:S(2)}, u32[]{:S(2)}) %collective-permute-start.29) | collective-permute-done | bytes 458784 | tf_op jit(solution)/shard_map/ppermute | solution.py:258
  170.7 8.9 %collective-permute-done.26 = bf16[128,1792]{1,0:T(8,128)(2,1)S(1)} collective-permute-done((bf16[128,1792]{1,0:T(8,128)(2,1)S(1)}, bf16[128,1792]{1,0:T(8,128)(2,1)S(1)}, u32[]{:S(2)}, u32[]{:S(2)}) %collective-permute-start.26) | collective-permute-done | bytes 458784 | tf_op jit(solution)/shard_map/ppermute | solution.py:258
  181.5 5.7 %collective-permute-done.30 = bf16[128,1792]{1,0:T(8,128)(2,1)S(1)} collective-permute-done((bf16[128,1792]{1,0:T(8,128)(2,1)S(1)}, bf16[128,1792]{1,0:T(8,128)(2,1)S(1)}, u32[]{:S(2)}, u32[]{:S(2)}) %collective-permute-start.30) | collective-permute-done | bytes 458784 | tf_op jit(solution)/shard_map/ppermute | solution.py:258
  189.0 5.6 %collective-permute-done.21 = bf16[128,1792]{1,0:T(8,128)(2,1)S(1)} collective-permute-done((bf16[128,1792]{1,0:T(8,128)(2,1)S(1)}, bf16[128,1792]{1,0:T(8,128)(2,1)S(1)}, u32[]{:S(2)}, u32[]{:S(2)}) %collective-permute-start.21) | collective-permute-done | bytes 458784 | tf_op jit(solution)/shard_map/ppermute | solution.py:258
  196.3 7.1 %collective-permute-done.31.refs_7_ = bf16[128,1792]{1,0:T(8,128)(2,1)S(1)} collective-permute-done((bf16[128,1792]{1,0:T(8,128)(2,1)S(1)}, bf16[128,1792]{1,0:T(8,128)(2,1)S(1)}, u32[]{:S(2)}, u32[]{:S(2)}) %collective-permute-start.31) | collective-permute-done | bytes 458784 | tf_op jit(solution)/shard_map/ppermute | solution.py:258
  203.4 3.7 %collective-permute-done.22.refs_4_ = bf16[128,1792]{1,0:T(8,128)(2,1)S(1)} collective-permute-done((bf16[128,1792]{1,0:T(8,128)(2,1)S(1)}, bf16[128,1792]{1,0:T(8,128)(2,1)S(1)}, u32[]{:S(2)}, u32[]{:S(2)}) %collective-permute-start.22) | collective-permute-done | bytes 458784 | tf_op jit(solution)/shard_map/ppermute | solution.py:258
  207.6 18.1 %collective-permute-start.32 = (bf16[2,16,1792]{2,1,0:T(8,128)(2,1)S(1)}, bf16[2,16,1792]{2,1,0:T(8,128)(2,1)S(1)}, u32[]{:S(2)}, u32[]{:S(2)}) collective-permute-start(bf16[2,16,1792]{2,1,0:T(8,128)(2,1)S(1)} %get-tuple-element.82), channel_id=1, source_target_pairs={{0,16},{1,17},{2,18},{3,19},{4,20},{5,21},{6,22},{7,23},{8,24},{9,... | collective-permute-start | bytes 344072 | tf_op jit(solution)/shard_map/ppermute | solution.py:258
  (103 shorter events, 91.0 us)
Async XLA Ops:
  2.6 24.4 %all-to-all-start = ((bf16[8,3,4,8,896]{4,3,2,1,0:T(8,128)(2,1)}), bf16[8,3,4,8,896]{4,3,2,1,0:T(8,128)(2,1)S(1)}, u32[]{:S(2)}, u32[]{:S(2)}) async-start(bf16[8,3,4,8,896]{4,3,2,1,0:T(8,128)(2,1)} %bitcast.2), calls=%async_computation | async-start | bytes 2752512 | tf_op jit(solution)/shard_map/all_to_all | solution.py:239
  12.8 81.8 %collective-permute-start.2 = (bf16[2,448,1792]{2,1,0:T(8,128)(2,1)}, bf16[2,448,1792]{2,1,0:T(8,128)(2,1)}, u32[]{:S(2)}, u32[]{:S(2)}) collective-permute-start(bf16[2,448,1792]{2,1,0:T(8,128)(2,1)} %pack.5), channel_id=1, source_target_pairs={{0,3},{1,0},{2,1},{3,2},{4,7},{5,4},{6,5},{7,6},{8,11},{9,8},{10,9... | collective-permute-start | bytes 9633800 | tf_op jit(solution)/shard_map/ppermute | solution.py:258
  18.2 92.4 %collective-permute-start.5 = (bf16[2,448,1792]{2,1,0:T(8,128)(2,1)}, bf16[2,448,1792]{2,1,0:T(8,128)(2,1)}, u32[]{:S(2)}, u32[]{:S(2)}) collective-permute-start(bf16[2,448,1792]{2,1,0:T(8,128)(2,1)} %pack.7), channel_id=1, source_target_pairs={{0,12},{1,13},{2,14},{3,15},{4,0},{5,1},{6,2},{7,3},{8,4},{9,5},{1... | collective-permute-start | bytes 9633800 | tf_op jit(solution)/shard_map/ppermute | solution.py:258
  30.0 14.6 %all-to-all-start.1 = ((bf16[8,4,8,896]{3,2,1,0:T(8,128)(2,1)}), bf16[8,4,8,896]{3,2,1,0:T(8,128)(2,1)S(1)}, u32[]{:S(2)}, u32[]{:S(2)}) async-start(bf16[8,4,8,896]{3,2,1,0:T(8,128)(2,1)} %attend.1), calls=%async_computation.1 | async-start | bytes 917504 | tf_op jit(solution)/shard_map/all_to_all | solution.py:247
  38.0 30.3 %collective-permute-start.1 = (bf16[1,448,1792]{2,1,0:T(8,128)(2,1)}, bf16[1,448,1792]{2,1,0:T(8,128)(2,1)}, u32[]{:S(2)}, u32[]{:S(2)}) collective-permute-start(bf16[1,448,1792]{2,1,0:T(8,128)(2,1)} %pack.4), channel_id=1, source_target_pairs={{0,3},{1,0},{2,1},{3,2},{4,7},{5,4},{6,5},{7,6},{8,11},{9,8},{10,9... | collective-permute-start | bytes 4816904 | tf_op jit(solution)/shard_map/ppermute | solution.py:258
  42.9 32.2 %collective-permute-start.4 = (bf16[1,448,1792]{2,1,0:T(8,128)(2,1)}, bf16[1,448,1792]{2,1,0:T(8,128)(2,1)S(1)}, u32[]{:S(2)}, u32[]{:S(2)}) collective-permute-start(bf16[1,448,1792]{2,1,0:T(8,128)(2,1)} %pack.6), channel_id=1, source_target_pairs={{0,12},{1,13},{2,14},{3,15},{4,0},{5,1},{6,2},{7,3},{8,4},{9,5},{1... | collective-permute-start | bytes 4816904 | tf_op jit(solution)/shard_map/ppermute | solution.py:258
  68.3 16.8 %collective-permute-start.3 = (bf16[128,1792]{1,0:T(8,128)(2,1)S(1)}, bf16[128,1792]{1,0:T(8,128)(2,1)S(1)}, u32[]{:S(2)}, u32[]{:S(2)}) collective-permute-start(bf16[128,1792]{1,0:T(8,128)(2,1)S(1)} %bitcast.16), channel_id=1, source_target_pairs={{0,8},{1,9},{2,10},{3,11},{4,12},{5,13},{6,14},{7,15},{8,0},{9,1},... | collective-permute-start | bytes 1376264 | tf_op jit(solution)/shard_map/ppermute | solution.py:258
  75.0 15.6 %collective-permute-start.6 = (bf16[128,1792]{1,0:T(8,128)(2,1)S(1)}, bf16[128,1792]{1,0:T(8,128)(2,1)S(1)}, u32[]{:S(2)}, u32[]{:S(2)}) collective-permute-start(bf16[128,1792]{1,0:T(8,128)(2,1)S(1)} %bitcast.21), channel_id=1, source_target_pairs={{0,4},{1,5},{2,6},{3,7},{4,8},{5,9},{6,10},{7,11},{8,12},{9,13},{1... | collective-permute-start | bytes 1376264 | tf_op jit(solution)/shard_map/ppermute | solution.py:258
  80.4 14.1 %collective-permute-start.11 = (bf16[128,1792]{1,0:T(8,128)(2,1)S(1)}, bf16[128,1792]{1,0:T(8,128)(2,1)S(1)}, u32[]{:S(2)}, u32[]{:S(2)}) collective-permute-start(bf16[128,1792]{1,0:T(8,128)(2,1)S(1)} %bitcast.17), channel_id=1, source_target_pairs={{0,1},{1,2},{2,3},{3,0},{4,5},{5,6},{6,7},{7,4},{8,9},{9,10},{10,1... | collective-permute-start | bytes 1376264 | tf_op jit(solution)/shard_map/ppermute | solution.py:258
  94.5 28.2 %collective-permute-start.15 = (bf16[128,1792]{1,0:T(8,128)(2,1)S(1)}, bf16[128,1792]{1,0:T(8,128)(2,1)S(1)}, u32[]{:S(2)}, u32[]{:S(2)}) collective-permute-start(bf16[128,1792]{1,0:T(8,128)(2,1)S(1)} %collective-permute-done.6.refs_0_), channel_id=1, source_target_pairs={{0,4},{1,5},{2,6},{3,7},{4,8},{5,9},{6,10},{7,11},{8,12},{9,13},{1... | collective-permute-start | bytes 1376264 | tf_op jit(solution)/shard_map/ppermute | solution.py:258
  94.5 35.0 %collective-permute-start.12 = (bf16[128,1792]{1,0:T(8,128)(2,1)S(1)}, bf16[128,1792]{1,0:T(8,128)(2,1)S(1)}, u32[]{:S(2)}, u32[]{:S(2)}) collective-permute-start(bf16[128,1792]{1,0:T(8,128)(2,1)S(1)} %collective-permute-done.11.refs_0_), channel_id=1, source_target_pairs={{0,1},{1,2},{2,3},{3,0},{4,5},{5,6},{6,7},{7,4},{8,9},{9,10},{10,1... | collective-permute-start | bytes 1376264 | tf_op jit(solution)/shard_map/ppermute | solution.py:258
  97.1 34.7 %collective-permute-start.16 = (bf16[128,1792]{1,0:T(8,128)(2,1)S(1)}, bf16[128,1792]{1,0:T(8,128)(2,1)S(1)}, u32[]{:S(2)}, u32[]{:S(2)}) collective-permute-start(bf16[128,1792]{1,0:T(8,128)(2,1)S(1)} %collective-permute-done.7.refs_1_), channel_id=1, source_target_pairs={{0,12},{1,13},{2,14},{3,15},{4,0},{5,1},{6,2},{7,3},{8,4},{9,5},{1... | collective-permute-start | bytes 1376264 | tf_op jit(solution)/shard_map/ppermute | solution.py:258
  102.6 32.9 %collective-permute-start.14 = (bf16[128,1792]{1,0:T(8,128)(2,1)S(1)}, bf16[128,1792]{1,0:T(8,128)(2,1)S(1)}, u32[]{:S(2)}, u32[]{:S(2)}) collective-permute-start(bf16[128,1792]{1,0:T(8,128)(2,1)S(1)} %collective-permute-done.13.refs_1_), channel_id=1, source_target_pairs={{0,3},{1,0},{2,1},{3,2},{4,7},{5,4},{6,5},{7,6},{8,11},{9,8},{10,9... | collective-permute-start | bytes 1376264 | tf_op jit(solution)/shard_map/ppermute | solution.py:258
  110.6 29.4 %collective-permute-start.10 = (bf16[128,1792]{1,0:T(8,128)(2,1)S(1)}, bf16[128,1792]{1,0:T(8,128)(2,1)S(1)}, u32[]{:S(2)}, u32[]{:S(2)}) collective-permute-start(bf16[128,1792]{1,0:T(8,128)(2,1)S(1)} %bitcast.23), channel_id=1, source_target_pairs={{0,12},{1,13},{2,14},{3,15},{4,0},{5,1},{6,2},{7,3},{8,4},{9,5},{1... | collective-permute-start | bytes 1376264 | tf_op jit(solution)/shard_map/ppermute | solution.py:258
  122.7 17.3 %collective-permute-start.9 = (bf16[128,1792]{1,0:T(8,128)(2,1)S(1)}, bf16[128,1792]{1,0:T(8,128)(2,1)S(1)}, u32[]{:S(2)}, u32[]{:S(2)}) collective-permute-start(bf16[128,1792]{1,0:T(8,128)(2,1)S(1)} %collective-permute-done.refs_1_), channel_id=1, source_target_pairs={{0,4},{1,5},{2,6},{3,7},{4,8},{5,9},{6,10},{7,11},{8,12},{9,13},{1... | collective-permute-start | bytes 1376264 | tf_op jit(solution)/shard_map/ppermute | solution.py:258
  129.5 15.5 %collective-permute-start.25 = (bf16[128,1792]{1,0:T(8,128)(2,1)S(1)}, bf16[128,1792]{1,0:T(8,128)(2,1)S(1)}, u32[]{:S(2)}, u32[]{:S(2)}) collective-permute-start(bf16[128,1792]{1,0:T(8,128)(2,1)S(1)} %bitcast.19), channel_id=1, source_target_pairs={{0,3},{1,0},{2,1},{3,2},{4,7},{5,4},{6,5},{7,6},{8,11},{9,8},{10,9... | collective-permute-start | bytes 1376264 | tf_op jit(solution)/shard_map/ppermute | solution.py:258
  131.8 15.5 %collective-permute-start.24 = (bf16[128,1792]{1,0:T(8,128)(2,1)S(1)}, bf16[128,1792]{1,0:T(8,128)(2,1)S(1)}, u32[]{:S(2)}, u32[]{:S(2)}) collective-permute-start(bf16[128,1792]{1,0:T(8,128)(2,1)S(1)} %collective-permute-done.3.refs_1_), channel_id=1, source_target_pairs={{0,1},{1,2},{2,3},{3,0},{4,5},{5,6},{6,7},{7,4},{8,9},{9,10},{10,1... | collective-permute-start | bytes 1376264 | tf_op jit(solution)/shard_map/ppermute | solution.py:258
  135.5 17.5 %collective-permute-start.20 = (bf16[128,1792]{1,0:T(8,128)(2,1)S(1)}, bf16[128,1792]{1,0:T(8,128)(2,1)S(1)}, u32[]{:S(2)}, u32[]{:S(2)}) collective-permute-start(bf16[128,1792]{1,0:T(8,128)(2,1)S(1)} %get-tuple-element.68), channel_id=1, source_target_pairs={{0,12},{1,13},{2,14},{3,15},{4,0},{5,1},{6,2},{7,3},{8,4},{9,5},{1... | collective-permute-start | bytes 1376264 | tf_op jit(solution)/shard_map/ppermute | solution.py:258
  140.0 41.5 %collective-permute-start.28 = (bf16[128,1792]{1,0:T(8,128)(2,1)S(1)}, bf16[128,1792]{1,0:T(8,128)(2,1)S(1)}, u32[]{:S(2)}, u32[]{:S(2)}) collective-permute-start(bf16[128,1792]{1,0:T(8,128)(2,1)S(1)} %get-tuple-element.64), channel_id=1, source_target_pairs={{0,1},{1,2},{2,3},{3,0},{4,5},{5,6},{6,7},{7,4},{8,9},{9,10},{10,1... | collective-permute-start | bytes 1376264 | tf_op jit(solution)/shard_map/ppermute | solution.py:258
  140.1 47.4 %collective-permute-start.19 = (bf16[128,1792]{1,0:T(8,128)(2,1)S(1)}, bf16[128,1792]{1,0:T(8,128)(2,1)S(1)}, u32[]{:S(2)}, u32[]{:S(2)}) collective-permute-start(bf16[128,1792]{1,0:T(8,128)(2,1)S(1)} %get-tuple-element.60), channel_id=1, source_target_pairs={{0,4},{1,5},{2,6},{3,7},{4,8},{5,9},{6,10},{7,11},{8,12},{9,13},{1... | collective-permute-start | bytes 1376264 | tf_op jit(solution)/shard_map/ppermute | solution.py:258
  145.0 49.7 %collective-permute-start.23 = (bf16[128,1792]{1,0:T(8,128)(2,1)S(1)}, bf16[128,1792]{1,0:T(8,128)(2,1)S(1)}, u32[]{:S(2)}, u32[]{:S(2)}) collective-permute-start(bf16[128,1792]{1,0:T(8,128)(2,1)S(1)} %get-tuple-element.63), channel_id=1, source_target_pairs={{0,3},{1,0},{2,1},{3,2},{4,7},{5,4},{6,5},{7,6},{8,11},{9,8},{10,9... | collective-permute-start | bytes 1376264 | tf_op jit(solution)/shard_map/ppermute | solution.py:258
  147.3 49.1 %collective-permute-start.8 = (bf16[128,1792]{1,0:T(8,128)(2,1)S(1)}, bf16[128,1792]{1,0:T(8,128)(2,1)S(1)}, u32[]{:S(2)}, u32[]{:S(2)}) collective-permute-start(bf16[128,1792]{1,0:T(8,128)(2,1)S(1)} %get-tuple-element.59), channel_id=1, source_target_pairs={{0,12},{1,13},{2,14},{3,15},{4,0},{5,1},{6,2},{7,3},{8,4},{9,5},{1... | collective-permute-start | bytes 1376264 | tf_op jit(solution)/shard_map/ppermute | solution.py:258
  181.5 14.9 %collective-permute-start.27 = (bf16[128,1792]{1,0:T(8,128)(2,1)S(1)}, bf16[128,1792]{1,0:T(8,128)(2,1)S(1)}, u32[]{:S(2)}, u32[]{:S(2)}) collective-permute-start(bf16[128,1792]{1,0:T(8,128)(2,1)S(1)} %add_convert_fusion.2), channel_id=1, source_target_pairs={{0,1},{1,2},{2,3},{3,0},{4,5},{5,6},{6,7},{7,4},{8,9},{9,10},{10,1... | collective-permute-start | bytes 1376264 | tf_op jit(solution)/shard_map/ppermute | solution.py:258
  207.6 23.1 %collective-permute-start.32 = (bf16[2,16,1792]{2,1,0:T(8,128)(2,1)S(1)}, bf16[2,16,1792]{2,1,0:T(8,128)(2,1)S(1)}, u32[]{:S(2)}, u32[]{:S(2)}) collective-permute-start(bf16[2,16,1792]{2,1,0:T(8,128)(2,1)S(1)} %get-tuple-element.82), channel_id=1, source_target_pairs={{0,16},{1,17},{2,18},{3,19},{4,20},{5,21},{6,22},{7,23},{8,24},{9,... | collective-permute-start | bytes 344072 | tf_op jit(solution)/shard_map/ppermute | solution.py:258
  (23 other events, 268.6 us)

commit v5 on v4

--- a/solution.py
+++ b/solution.py
@@ -79,23 +79,30 @@
 
 def settle_kernel(position, *refs):
     own, moved, outs = refs[:2], refs[2:8], refs[8:]
-    count = outs[0].shape[1]
-    for k, out in enumerate(outs):
+    count = outs[0].shape[2]
+    for k in range(2 * outs[0].shape[0]):
         start = pl.multiple_of((position[0] ^ k) * count, count)
         cut = pl.ds(start, count)
         for e in range(2):
             total = own[e][cut].astype(jnp.float32)
             for part in moved[3 * e : 3 * e + 3]:
                 total = total + part[cut].astype(jnp.float32)
-            out[e] = total.astype(out.dtype)
+            outs[k % 2][k // 2, e] = total.astype(outs[0].dtype)
+
+
+def join_kernel(left, right, *outs):
+    for j, out in enumerate(outs):
+        out[0] = left[j + 1]
+        out[1] = right[j + 1]
 
 
 def combine_kernel(hidden_ref, target_ref, gate_ref, *refs):
-    pieces, out_ref = refs[:-1], refs[-1]
+    left, right, *rest, out_ref = refs
     tokens, width = hidden_ref.shape
-    returned = jnp.concatenate(
-        [piece[e] for piece in pieces for e in range(piece.shape[0])], axis=0
-    )
+    blocks = [left[0], right[0]]
+    for ref in rest:
+        blocks += [ref[0], ref[1]]
+    returned = jnp.concatenate([block[e] for block in blocks for e in range(2)], axis=0)
     col = lax.broadcasted_iota(jnp.int32, (tokens, returned.shape[0]), 1)
     moved = jnp.zeros((tokens, width), jnp.float32)
     for choice in range(2):
@@ -152,9 +159,9 @@
 
 
 def pack(index, *sources):
-    steps = 4
     _, rows, width = sources[0].shape
     count = len(sources)
+    steps = 2 * count
     return pl.pallas_call(
         pack_kernel,
         grid=(steps,),
@@ -333,20 +340,21 @@
             total = total + piece.astype(jnp.float32)
         return total.astype(bf16)
 
-    last_other = send_all([add(late[e][0], pass_other[e]) for e in range(2)], ring, -1)
-    last_mine = send_all([add(late[e][1], pass_mine[e]) for e in range(2)], ring, 1)
-    swapped = send_all(
-        [add(own[e][1], first_other[e], last_other[e]) for e in range(2)], far, 2
+    last_other = send_all([add(late[e][0], pass_other[e]) for e in range(2)], ring, -1
+    )
+    last_mine = send_all([add(late[e][1], pass_mine[e]) for e in range(2)], ring, 1
+    )
+    swapped = send_all([add(own[e][1], first_other[e], last_other[e]) for e in range(2)], far, 2
     )
     position = lax.axis_index("ep")
-    pieces = pl.pallas_call(
+    pairs = groups // 2
+    half_pieces = jax.ShapeDtypeStruct((pairs, experts_local, capacity, model_width), bf16)
+    both_pieces = jax.ShapeDtypeStruct((2, experts_local, capacity, model_width), bf16)
+    left, right = pl.pallas_call(
         settle_kernel,
         in_specs=[pl.BlockSpec(memory_space=pltpu.SMEM)] + on_chip(8),
-        out_specs=tuple(on_chip(groups)),
-        out_shape=tuple(
-            jax.ShapeDtypeStruct((experts_local, capacity, model_width), bf16)
-            for _ in range(groups)
-        ),
+        out_specs=tuple(on_chip(2)),
+        out_shape=(half_pieces, half_pieces),
         compiler_params=grant(12),
         name="settle",
     )(
@@ -368,18 +376,27 @@
 
         return hop(sizes, move)
 
-    back = list(pieces)
-    for k in (4, 5, 2, 3, 6, 7, 1):
-        back[k] = send(pieces[k], toggle(k))
+    right = send(right, toggle(1))
+    joined = pl.pallas_call(
+        join_kernel,
+        in_specs=on_chip(2),
+        out_specs=tuple(on_chip(pairs - 1)),
+        out_shape=(both_pieces,) * (pairs - 1),
+        compiler_params=grant(6),
+        name="join",
+    )(left, right)
+    back = []
+    for j, value in enumerate(joined):
+        back.append(send(value, toggle(2 * j + 2)))
     place = ((expert_ids // experts_local) ^ position) * experts_local
     place = (place + expert_ids % experts_local) * capacity + slot_index
     combined = pl.pallas_call(
         combine_kernel,
         out_shape=jax.ShapeDtypeStruct((tokens, model_width), bf16),
-        in_specs=on_chip(3 + groups),
+        in_specs=on_chip(5 + len(back)),
         compiler_params=grant(12),
         name="combine",
-    )(hidden, jnp.where(slot_index >= 0, place, -1).reshape(tokens, 2), gates, *back)
+    )(hidden, jnp.where(slot_index >= 0, place, -1).reshape(tokens, 2), gates, left, right, *back)
     return combined.reshape(frames_local, sites_local, model_width)
 
 

time: 246 us -> 246 us (level)
    ppermute x39 -> x36, starting transfers between devices: 66.7 us -> 68.7 us  [send(): return lax.ppermute(value, ('ep', 'tp'), pairs)]
    ppermute x39 -> x36, waiting for transfers between devices: 76.8 us -> 77.2 us  [send(): return lax.ppermute(value, ('ep', 'tp'), pairs)]
  transfers between devices with their start and end apart: 41 -> 38, of which waited for: 18 -> 19; matrix products, arithmetic and copies ran while one was open for 0% -> 0% of each run, Pallas kernels for 23% -> 22%
where the time goes in v5:
time: 246 us; the launch traced here: 245 us
  waiting for transfers between devices  85.2 us (35%)
  starting transfers between devices  79.1 us (32%)
  Pallas kernels  55.5 us (23%)
  blocking collectives  21.4 us (9%)
  local copies, waits for them, and re-layouts  2.96 us (1%)
    ppermute x36, waiting for transfers between devices, send(): return lax.ppermute(value, ('ep', 'tp'), pairs)  77.2 us
    ppermute x36, starting transfers between devices, send(): return lax.ppermute(value, ('ep', 'tp'), pairs)  68.7 us
    pallas_call x8, Pallas kernels, mlp(): pl.pallas_call(lambda *refs: mlp_kernel(len(pieces), *refs), in_specs=on_...  29.2 us
    all_to_all x1, blocking collectives, block(): lax.all_to_all(rows.reshape(groups, experts_local, capacity, model_width)...  21.4 us
    pallas_call x4, Pallas kernels, pack(): pl.pallas_call(pack_kernel, grid=(steps,), in_specs=[pl.BlockSpec((None,...  13.2 us
    pallas_call x2, Pallas kernels, land(): pl.pallas_call(lambda *refs: land_kernel(index, *refs), in_specs=[pl.Bloc...  7.69 us
    all_to_all x1, waiting for transfers between devices, block(): lax.all_to_all(spread, 'ep', split_axis=0, concat_axis=0, tiled=True)  7.17 us
    all_to_all x1, starting transfers between devices, block(): lax.all_to_all(spread, 'ep', split_axis=0, concat_axis=0, tiled=True)  5.96 us
  transfers between devices with their start and end apart: 38, of which 19 were waited for; matrix products, arithmetic and copies ran while one was open for 0% of the time, Pallas kernels for 22%

profile of v5, /device:TPU:1, one launch (start us, length us, event | category | flops | bytes accessed | tf_op | source)
XLA Modules:
  0.0 245.1 jit_solution(836412601981687696)
XLA Ops:
  2.6 6.0 %all-to-all-start = ((bf16[8,3,4,8,896]{4,3,2,1,0:T(8,128)(2,1)}), bf16[8,3,4,8,896]{4,3,2,1,0:T(8,128)(2,1)S(1)}, u32[]{:S(2)}, u32[]{:S(2)}) async-start(bf16[8,3,4,8,896]{4,3,2,1,0:T(8,128)(2,1)} %bitcast.2), calls=%async_computation | async-start | bytes 2752512 | tf_op jit(solution)/shard_map/all_to_all | solution.py:246
  8.5 4.2 %pack.5 = bf16[2,448,1792]{2,1,0:T(8,128)(2,1)} custom-call(bf16[2,448,1792]{2,1,0:T(8,128)(2,1)} %bitcast.32, bf16[2,448,1792]{2,1,0:T(8,128)(2,1)} %refs_2_.3), custom_call_target="tpu_custom_call" | custom-call | tf_op jit(solution)/shard_map/pack/pallas_call | solution.py:165
  14.0 4.2 %pack.7 = bf16[2,448,1792]{2,1,0:T(8,128)(2,1)} custom-call(bf16[2,448,1792]{2,1,0:T(8,128)(2,1)} %bitcast.33, bf16[2,448,1792]{2,1,0:T(8,128)(2,1)} %refs_2_.3), custom_call_target="tpu_custom_call" | custom-call | tf_op jit(solution)/shard_map/pack/pallas_call | solution.py:165
  19.8 7.2 %all-to-all-done.qkv_ref = bf16[8,3,4,8,896]{4,3,2,1,0:T(8,128)(2,1)S(1)} async-done(((bf16[8,3,4,8,896]{4,3,2,1,0:T(8,128)(2,1)}), bf16[8,3,4,8,896]{4,3,2,1,0:T(8,128)(2,1)S(1)}, u32[]{:S(2)}, u32[]{:S(2)}) %all-to-all-start) | async-done | bytes 1376288 | tf_op jit(solution)/shard_map/all_to_all | solution.py:246
  30.0 4.4 %all-to-all-start.1 = ((bf16[8,4,8,896]{3,2,1,0:T(8,128)(2,1)}), bf16[8,4,8,896]{3,2,1,0:T(8,128)(2,1)S(1)}, u32[]{:S(2)}, u32[]{:S(2)}) async-start(bf16[8,4,8,896]{3,2,1,0:T(8,128)(2,1)} %attend.1), calls=%async_computation.1 | async-start | bytes 917504 | tf_op jit(solution)/shard_map/all_to_all | solution.py:254
  43.7 21.4 %all_to_all.15 = bf16[8,2,16,1792]{3,2,1,0:T(8,128)(2,1)S(1)} all-to-all(bf16[8,2,16,1792]{3,2,1,0:T(8,128)(2,1)S(1)} %bitcast.24), channel_id=1, replica_groups=mesh['ep'=8,'tp'=16] {'ep'}, dimensions={0} | all-to-all | bytes 1835008 | tf_op jit(solution)/shard_map/all_to_all | solution.py:295
  68.3 5.4 %collective-permute-start.3 = (bf16[128,1792]{1,0:T(8,128)(2,1)S(1)}, bf16[128,1792]{1,0:T(8,128)(2,1)S(1)}, u32[]{:S(2)}, u32[]{:S(2)}) collective-permute-start(bf16[128,1792]{1,0:T(8,128)(2,1)S(1)} %bitcast.16), channel_id=1, source_target_pairs={{0,8},{1,9},{2,10},{3,11},{4,12},{5,13},{6,14},{7,15},{8,0},{9,1},... | collective-permute-start | bytes 1376264 | tf_op jit(solution)/shard_map/ppermute | solution.py:265
  78.0 7.0 %collective-permute-start.11 = (bf16[128,1792]{1,0:T(8,128)(2,1)S(1)}, bf16[128,1792]{1,0:T(8,128)(2,1)S(1)}, u32[]{:S(2)}, u32[]{:S(2)}) collective-permute-start(bf16[128,1792]{1,0:T(8,128)(2,1)S(1)} %bitcast.17), channel_id=1, source_target_pairs={{0,1},{1,2},{2,3},{3,0},{4,5},{5,6},{6,7},{7,4},{8,9},{9,10},{10,1... | collective-permute-start | bytes 1376264 | tf_op jit(solution)/shard_map/ppermute | solution.py:265
  85.0 6.9 %collective-permute-done.6.refs_0_ = bf16[128,1792]{1,0:T(8,128)(2,1)S(1)} collective-permute-done((bf16[128,1792]{1,0:T(8,128)(2,1)S(1)}, bf16[128,1792]{1,0:T(8,128)(2,1)S(1)}, u32[]{:S(2)}, u32[]{:S(2)}) %collective-permute-start.6) | collective-permute-done | bytes 458784 | tf_op jit(solution)/shard_map/ppermute | solution.py:265
  101.9 3.8 %land.2.refs_2_ = bf16[2,3,448,1792]{3,2,1,0:T(8,128)(2,1)S(1)} custom-call(bf16[2,448,1792]{2,1,0:T(8,128)(2,1)} %bitcast.30, bf16[2,448,1792]{2,1,0:T(8,128)(2,1)} %bitcast.34, bf16[2,448,1792]{2,1,0:T(8,128)(2,1)} %refs_2_.3, bf16[1,448,1792]{2,1,0:T(8,128)(2,1)} %collective-permute-done.1.refs_3_, bf16[2,448,1792]{2,1,0:T(8,128)(2,1)} %collective-permute-done.2.refs_4_), custom_call_target="tpu_custom_call" | custom-call | tf_op jit(solution)/shard_map/land/pallas_call | solution.py:195
  105.8 3.6 %mlp.8 = (bf16[128,1792]{1,0:T(8,128)(2,1)S(1)}, bf16[128,1792]{1,0:T(8,128)(2,1)S(1)}) custom-call(bf16[128,1792]{1,0:T(8,128)(2,1)S(1)} %bitcast.22, bf16[128,1792]{1,0:T(8,128)(2,1)S(1)} %collective-permute-done.refs_1_, bf16[2,3,448,1792]{3,2,1,0:T(8,128)(2,1)S(1)} %land.2.refs_2_), custom_call_target="tpu_custom_call" | custom-call | tf_op jit(solution)/shard_map/mlp/pallas_call | solution.py:145
  111.0 3.8 %land.3.refs_2_ = bf16[2,3,448,1792]{3,2,1,0:T(8,128)(2,1)S(1)} custom-call(bf16[2,448,1792]{2,1,0:T(8,128)(2,1)} %bitcast.31, bf16[2,448,1792]{2,1,0:T(8,128)(2,1)} %bitcast.35, bf16[2,448,1792]{2,1,0:T(8,128)(2,1)} %refs_2_.3, bf16[1,448,1792]{2,1,0:T(8,128)(2,1)} %copy-done.1, bf16[2,448,1792]{2,1,0:T(8,128)(2,1)} %collective-permute-done.5.refs_4_), custom_call_target="tpu_custom_call" | custom-call | tf_op jit(solution)/shard_map/land/pallas_call | solution.py:195
  114.9 3.6 %mlp.9 = (bf16[128,1792]{1,0:T(8,128)(2,1)S(1)}, bf16[128,1792]{1,0:T(8,128)(2,1)S(1)}) custom-call(bf16[128,1792]{1,0:T(8,128)(2,1)S(1)} %bitcast.18, bf16[128,1792]{1,0:T(8,128)(2,1)S(1)} %collective-permute-done.3.refs_1_, bf16[2,3,448,1792]{3,2,1,0:T(8,128)(2,1)S(1)} %land.3.refs_2_), custom_call_target="tpu_custom_call" | custom-call | tf_op jit(solution)/shard_map/mlp/pallas_call | solution.py:145
  140.9 3.7 %mlp.14 = (f32[128,1792]{1,0:T(8,128)S(1)}, f32[128,1792]{1,0:T(8,128)S(1)}) custom-call(bf16[128,1792]{1,0:T(8,128)(2,1)S(1)} %collective-permute-done.9.refs_0_, bf16[128,1792]{1,0:T(8,128)(2,1)S(1)} %collective-permute-done.10.refs_1_, bf16[2,3,448,1792]{3,2,1,0:T(8,128)(2,1)S(1)} %land.2.refs_2_), custom_call_target="tpu_custom_call" | custom-call | tf_op jit(solution)/shard_map/mlp/pallas_call | solution.py:145
  150.0 3.7 %mlp.15 = (f32[128,1792]{1,0:T(8,128)S(1)}, f32[128,1792]{1,0:T(8,128)S(1)}) custom-call(bf16[128,1792]{1,0:T(8,128)(2,1)S(1)} %collective-permute-done.24.refs_0_, bf16[128,1792]{1,0:T(8,128)(2,1)S(1)} %collective-permute-done.25.refs_1_, bf16[2,3,448,1792]{3,2,1,0:T(8,128)(2,1)S(1)} %land.3.refs_2_), custom_call_target="tpu_custom_call" | custom-call | tf_op jit(solution)/shard_map/mlp/pallas_call | solution.py:145
  153.9 8.4 %collective-permute-done.17 = bf16[128,1792]{1,0:T(8,128)(2,1)S(1)} collective-permute-done((bf16[128,1792]{1,0:T(8,128)(2,1)S(1)}, bf16[128,1792]{1,0:T(8,128)(2,1)S(1)}, u32[]{:S(2)}, u32[]{:S(2)}) %collective-permute-start.17) | collective-permute-done | bytes 458784 | tf_op jit(solution)/shard_map/ppermute | solution.py:265
  164.2 5.7 %collective-permute-done.29 = bf16[128,1792]{1,0:T(8,128)(2,1)S(1)} collective-permute-done((bf16[128,1792]{1,0:T(8,128)(2,1)S(1)}, bf16[128,1792]{1,0:T(8,128)(2,1)S(1)}, u32[]{:S(2)}, u32[]{:S(2)}) %collective-permute-start.29) | collective-permute-done | bytes 458784 | tf_op jit(solution)/shard_map/ppermute | solution.py:265
  170.0 8.5 %collective-permute-done.26 = bf16[128,1792]{1,0:T(8,128)(2,1)S(1)} collective-permute-done((bf16[128,1792]{1,0:T(8,128)(2,1)S(1)}, bf16[128,1792]{1,0:T(8,128)(2,1)S(1)}, u32[]{:S(2)}, u32[]{:S(2)}) %collective-permute-start.26) | collective-permute-done | bytes 458784 | tf_op jit(solution)/shard_map/ppermute | solution.py:265
  180.4 5.7 %collective-permute-done.30 = bf16[128,1792]{1,0:T(8,128)(2,1)S(1)} collective-permute-done((bf16[128,1792]{1,0:T(8,128)(2,1)S(1)}, bf16[128,1792]{1,0:T(8,128)(2,1)S(1)}, u32[]{:S(2)}, u32[]{:S(2)}) %collective-permute-start.30) | collective-permute-done | bytes 458784 | tf_op jit(solution)/shard_map/ppermute | solution.py:265
  187.9 5.6 %collective-permute-done.21 = bf16[128,1792]{1,0:T(8,128)(2,1)S(1)} collective-permute-done((bf16[128,1792]{1,0:T(8,128)(2,1)S(1)}, bf16[128,1792]{1,0:T(8,128)(2,1)S(1)}, u32[]{:S(2)}, u32[]{:S(2)}) %collective-permute-start.21) | collective-permute-done | bytes 458784 | tf_op jit(solution)/shard_map/ppermute | solution.py:265
  195.2 7.1 %collective-permute-done.31.refs_7_ = bf16[128,1792]{1,0:T(8,128)(2,1)S(1)} collective-permute-done((bf16[128,1792]{1,0:T(8,128)(2,1)S(1)}, bf16[128,1792]{1,0:T(8,128)(2,1)S(1)}, u32[]{:S(2)}, u32[]{:S(2)}) %collective-permute-start.31) | collective-permute-done | bytes 458784 | tf_op jit(solution)/shard_map/ppermute | solution.py:265
  202.3 3.7 %collective-permute-done.22.refs_4_ = bf16[128,1792]{1,0:T(8,128)(2,1)S(1)} collective-permute-done((bf16[128,1792]{1,0:T(8,128)(2,1)S(1)}, bf16[128,1792]{1,0:T(8,128)(2,1)S(1)}, u32[]{:S(2)}, u32[]{:S(2)}) %collective-permute-start.22) | collective-permute-done | bytes 458784 | tf_op jit(solution)/shard_map/ppermute | solution.py:265
  206.5 18.1 %collective-permute-start.32 = (bf16[4,2,16,1792]{3,2,1,0:T(8,128)(2,1)S(1)}, bf16[4,2,16,1792]{3,2,1,0:T(8,128)(2,1)S(1)}, u32[]{:S(2)}, u32[]{:S(2)}) collective-permute-start(bf16[4,2,16,1792]{3,2,1,0:T(8,128)(2,1)S(1)} %get-tuple-element.79), channel_id=1, source_target_pairs={{0,16},{1,17},{2,18},{3,19},{4,20},{5,21},{6,22},{7,23},{8,24},{9,... | collective-permute-start | bytes 1376264 | tf_op jit(solution)/shard_map/ppermute | solution.py:265
  234.8 7.0 %collective-permute-done.34.refs_3_ = bf16[2,2,16,1792]{3,2,1,0:T(8,128)(2,1)S(1)} collective-permute-done((bf16[2,2,16,1792]{3,2,1,0:T(8,128)(2,1)S(1)}, bf16[2,2,16,1792]{3,2,1,0:T(8,128)(2,1)S(1)}, u32[]{:S(2)}, u32[]{:S(2)}) %collective-permute-start.34) | collective-permute-done | bytes 229408 | tf_op jit(solution)/shard_map/ppermute | solution.py:265
  (98 shorter events, 85.9 us)
Async XLA Ops:
  2.6 24.4 %all-to-all-start = ((bf16[8,3,4,8,896]{4,3,2,1,0:T(8,128)(2,1)}), bf16[8,3,4,8,896]{4,3,2,1,0:T(8,128)(2,1)S(1)}, u32[]{:S(2)}, u32[]{:S(2)}) async-start(bf16[8,3,4,8,896]{4,3,2,1,0:T(8,128)(2,1)} %bitcast.2), calls=%async_computation | async-start | bytes 2752512 | tf_op jit(solution)/shard_map/all_to_all | solution.py:246
  12.8 81.4 %collective-permute-start.2 = (bf16[2,448,1792]{2,1,0:T(8,128)(2,1)}, bf16[2,448,1792]{2,1,0:T(8,128)(2,1)}, u32[]{:S(2)}, u32[]{:S(2)}) collective-permute-start(bf16[2,448,1792]{2,1,0:T(8,128)(2,1)} %pack.5), channel_id=1, source_target_pairs={{0,3},{1,0},{2,1},{3,2},{4,7},{5,4},{6,5},{7,6},{8,11},{9,8},{10,9... | collective-permute-start | bytes 9633800 | tf_op jit(solution)/shard_map/ppermute | solution.py:265
  18.2 91.2 %collective-permute-start.5 = (bf16[2,448,1792]{2,1,0:T(8,128)(2,1)}, bf16[2,448,1792]{2,1,0:T(8,128)(2,1)}, u32[]{:S(2)}, u32[]{:S(2)}) collective-permute-start(bf16[2,448,1792]{2,1,0:T(8,128)(2,1)} %pack.7), channel_id=1, source_target_pairs={{0,12},{1,13},{2,14},{3,15},{4,0},{5,1},{6,2},{7,3},{8,4},{9,5},{1... | collective-permute-start | bytes 9633800 | tf_op jit(solution)/shard_map/ppermute | solution.py:265
  30.0 13.0 %all-to-all-start.1 = ((bf16[8,4,8,896]{3,2,1,0:T(8,128)(2,1)}), bf16[8,4,8,896]{3,2,1,0:T(8,128)(2,1)S(1)}, u32[]{:S(2)}, u32[]{:S(2)}) async-start(bf16[8,4,8,896]{3,2,1,0:T(8,128)(2,1)} %attend.1), calls=%async_computation.1 | async-start | bytes 917504 | tf_op jit(solution)/shard_map/all_to_all | solution.py:254
  36.7 31.6 %collective-permute-start.1 = (bf16[1,448,1792]{2,1,0:T(8,128)(2,1)}, bf16[1,448,1792]{2,1,0:T(8,128)(2,1)}, u32[]{:S(2)}, u32[]{:S(2)}) collective-permute-start(bf16[1,448,1792]{2,1,0:T(8,128)(2,1)} %pack.4), channel_id=1, source_target_pairs={{0,3},{1,0},{2,1},{3,2},{4,7},{5,4},{6,5},{7,6},{8,11},{9,8},{10,9... | collective-permute-start | bytes 4816904 | tf_op jit(solution)/shard_map/ppermute | solution.py:265
  40.4 34.6 %collective-permute-start.4 = (bf16[1,448,1792]{2,1,0:T(8,128)(2,1)}, bf16[1,448,1792]{2,1,0:T(8,128)(2,1)S(1)}, u32[]{:S(2)}, u32[]{:S(2)}) collective-permute-start(bf16[1,448,1792]{2,1,0:T(8,128)(2,1)} %pack.6), channel_id=1, source_target_pairs={{0,12},{1,13},{2,14},{3,15},{4,0},{5,1},{6,2},{7,3},{8,4},{9,5},{1... | collective-permute-start | bytes 4816904 | tf_op jit(solution)/shard_map/ppermute | solution.py:265
  68.3 16.7 %collective-permute-start.3 = (bf16[128,1792]{1,0:T(8,128)(2,1)S(1)}, bf16[128,1792]{1,0:T(8,128)(2,1)S(1)}, u32[]{:S(2)}, u32[]{:S(2)}) collective-permute-start(bf16[128,1792]{1,0:T(8,128)(2,1)S(1)} %bitcast.16), channel_id=1, source_target_pairs={{0,8},{1,9},{2,10},{3,11},{4,12},{5,13},{6,14},{7,15},{8,0},{9,1},... | collective-permute-start | bytes 1376264 | tf_op jit(solution)/shard_map/ppermute | solution.py:265
  75.0 16.9 %collective-permute-start.6 = (bf16[128,1792]{1,0:T(8,128)(2,1)S(1)}, bf16[128,1792]{1,0:T(8,128)(2,1)S(1)}, u32[]{:S(2)}, u32[]{:S(2)}) collective-permute-start(bf16[128,1792]{1,0:T(8,128)(2,1)S(1)} %bitcast.21), channel_id=1, source_target_pairs={{0,4},{1,5},{2,6},{3,7},{4,8},{5,9},{6,10},{7,11},{8,12},{9,13},{1... | collective-permute-start | bytes 1376264 | tf_op jit(solution)/shard_map/ppermute | solution.py:265
  78.0 16.2 %collective-permute-start.11 = (bf16[128,1792]{1,0:T(8,128)(2,1)S(1)}, bf16[128,1792]{1,0:T(8,128)(2,1)S(1)}, u32[]{:S(2)}, u32[]{:S(2)}) collective-permute-start(bf16[128,1792]{1,0:T(8,128)(2,1)S(1)} %bitcast.17), channel_id=1, source_target_pairs={{0,1},{1,2},{2,3},{3,0},{4,5},{5,6},{6,7},{7,4},{8,9},{9,10},{10,1... | collective-permute-start | bytes 1376264 | tf_op jit(solution)/shard_map/ppermute | solution.py:265
  94.2 28.0 %collective-permute-start.15 = (bf16[128,1792]{1,0:T(8,128)(2,1)S(1)}, bf16[128,1792]{1,0:T(8,128)(2,1)S(1)}, u32[]{:S(2)}, u32[]{:S(2)}) collective-permute-start(bf16[128,1792]{1,0:T(8,128)(2,1)S(1)} %collective-permute-done.6.refs_0_), channel_id=1, source_target_pairs={{0,4},{1,5},{2,6},{3,7},{4,8},{5,9},{6,10},{7,11},{8,12},{9,13},{1... | collective-permute-start | bytes 1376264 | tf_op jit(solution)/shard_map/ppermute | solution.py:265
  94.2 34.5 %collective-permute-start.12 = (bf16[128,1792]{1,0:T(8,128)(2,1)S(1)}, bf16[128,1792]{1,0:T(8,128)(2,1)S(1)}, u32[]{:S(2)}, u32[]{:S(2)}) collective-permute-start(bf16[128,1792]{1,0:T(8,128)(2,1)S(1)} %collective-permute-done.11.refs_0_), channel_id=1, source_target_pairs={{0,1},{1,2},{2,3},{3,0},{4,5},{5,6},{6,7},{7,4},{8,9},{9,10},{10,1... | collective-permute-start | bytes 1376264 | tf_op jit(solution)/shard_map/ppermute | solution.py:265
  96.7 33.5 %collective-permute-start.16 = (bf16[128,1792]{1,0:T(8,128)(2,1)S(1)}, bf16[128,1792]{1,0:T(8,128)(2,1)S(1)}, u32[]{:S(2)}, u32[]{:S(2)}) collective-permute-start(bf16[128,1792]{1,0:T(8,128)(2,1)S(1)} %collective-permute-done.7.refs_1_), channel_id=1, source_target_pairs={{0,12},{1,13},{2,14},{3,15},{4,0},{5,1},{6,2},{7,3},{8,4},{9,5},{1... | collective-permute-start | bytes 1376264 | tf_op jit(solution)/shard_map/ppermute | solution.py:265
  101.9 32.2 %collective-permute-start.14 = (bf16[128,1792]{1,0:T(8,128)(2,1)S(1)}, bf16[128,1792]{1,0:T(8,128)(2,1)S(1)}, u32[]{:S(2)}, u32[]{:S(2)}) collective-permute-start(bf16[128,1792]{1,0:T(8,128)(2,1)S(1)} %collective-permute-done.13.refs_1_), channel_id=1, source_target_pairs={{0,3},{1,0},{2,1},{3,2},{4,7},{5,4},{6,5},{7,6},{8,11},{9,8},{10,9... | collective-permute-start | bytes 1376264 | tf_op jit(solution)/shard_map/ppermute | solution.py:265
  109.4 31.3 %collective-permute-start.10 = (bf16[128,1792]{1,0:T(8,128)(2,1)S(1)}, bf16[128,1792]{1,0:T(8,128)(2,1)S(1)}, u32[]{:S(2)}, u32[]{:S(2)}) collective-permute-start(bf16[128,1792]{1,0:T(8,128)(2,1)S(1)} %bitcast.23), channel_id=1, source_target_pairs={{0,12},{1,13},{2,14},{3,15},{4,0},{5,1},{6,2},{7,3},{8,4},{9,5},{1... | collective-permute-start | bytes 1376264 | tf_op jit(solution)/shard_map/ppermute | solution.py:265
  122.2 18.6 %collective-permute-start.9 = (bf16[128,1792]{1,0:T(8,128)(2,1)S(1)}, bf16[128,1792]{1,0:T(8,128)(2,1)S(1)}, u32[]{:S(2)}, u32[]{:S(2)}) collective-permute-start(bf16[128,1792]{1,0:T(8,128)(2,1)S(1)} %collective-permute-done.refs_1_), channel_id=1, source_target_pairs={{0,4},{1,5},{2,6},{3,7},{4,8},{5,9},{6,10},{7,11},{8,12},{9,13},{1... | collective-permute-start | bytes 1376264 | tf_op jit(solution)/shard_map/ppermute | solution.py:265
  128.7 15.9 %collective-permute-start.25 = (bf16[128,1792]{1,0:T(8,128)(2,1)S(1)}, bf16[128,1792]{1,0:T(8,128)(2,1)S(1)}, u32[]{:S(2)}, u32[]{:S(2)}) collective-permute-start(bf16[128,1792]{1,0:T(8,128)(2,1)S(1)} %bitcast.19), channel_id=1, source_target_pairs={{0,3},{1,0},{2,1},{3,2},{4,7},{5,4},{6,5},{7,6},{8,11},{9,8},{10,9... | collective-permute-start | bytes 1376264 | tf_op jit(solution)/shard_map/ppermute | solution.py:265
  130.2 17.1 %collective-permute-start.24 = (bf16[128,1792]{1,0:T(8,128)(2,1)S(1)}, bf16[128,1792]{1,0:T(8,128)(2,1)S(1)}, u32[]{:S(2)}, u32[]{:S(2)}) collective-permute-start(bf16[128,1792]{1,0:T(8,128)(2,1)S(1)} %collective-permute-done.3.refs_1_), channel_id=1, source_target_pairs={{0,1},{1,2},{2,3},{3,0},{4,5},{5,6},{6,7},{7,4},{8,9},{9,10},{10,1... | collective-permute-start | bytes 1376264 | tf_op jit(solution)/shard_map/ppermute | solution.py:265
  134.1 19.6 %collective-permute-start.20 = (bf16[128,1792]{1,0:T(8,128)(2,1)S(1)}, bf16[128,1792]{1,0:T(8,128)(2,1)S(1)}, u32[]{:S(2)}, u32[]{:S(2)}) collective-permute-start(bf16[128,1792]{1,0:T(8,128)(2,1)S(1)} %get-tuple-element.65), channel_id=1, source_target_pairs={{0,12},{1,13},{2,14},{3,15},{4,0},{5,1},{6,2},{7,3},{8,4},{9,5},{1... | collective-permute-start | bytes 1376264 | tf_op jit(solution)/shard_map/ppermute | solution.py:265
  140.7 39.6 %collective-permute-start.28 = (bf16[128,1792]{1,0:T(8,128)(2,1)S(1)}, bf16[128,1792]{1,0:T(8,128)(2,1)S(1)}, u32[]{:S(2)}, u32[]{:S(2)}) collective-permute-start(bf16[128,1792]{1,0:T(8,128)(2,1)S(1)} %get-tuple-element.61), channel_id=1, source_target_pairs={{0,1},{1,2},{2,3},{3,0},{4,5},{5,6},{6,7},{7,4},{8,9},{9,10},{10,1... | collective-permute-start | bytes 1376264 | tf_op jit(solution)/shard_map/ppermute | solution.py:265
  140.8 45.5 %collective-permute-start.19 = (bf16[128,1792]{1,0:T(8,128)(2,1)S(1)}, bf16[128,1792]{1,0:T(8,128)(2,1)S(1)}, u32[]{:S(2)}, u32[]{:S(2)}) collective-permute-start(bf16[128,1792]{1,0:T(8,128)(2,1)S(1)} %get-tuple-element.57), channel_id=1, source_target_pairs={{0,4},{1,5},{2,6},{3,7},{4,8},{5,9},{6,10},{7,11},{8,12},{9,13},{1... | collective-permute-start | bytes 1376264 | tf_op jit(solution)/shard_map/ppermute | solution.py:265
  144.6 49.1 %collective-permute-start.23 = (bf16[128,1792]{1,0:T(8,128)(2,1)S(1)}, bf16[128,1792]{1,0:T(8,128)(2,1)S(1)}, u32[]{:S(2)}, u32[]{:S(2)}) collective-permute-start(bf16[128,1792]{1,0:T(8,128)(2,1)S(1)} %get-tuple-element.60), channel_id=1, source_target_pairs={{0,3},{1,0},{2,1},{3,2},{4,7},{5,4},{6,5},{7,6},{8,11},{9,8},{10,9... | collective-permute-start | bytes 1376264 | tf_op jit(solution)/shard_map/ppermute | solution.py:265
  147.3 47.9 %collective-permute-start.8 = (bf16[128,1792]{1,0:T(8,128)(2,1)S(1)}, bf16[128,1792]{1,0:T(8,128)(2,1)S(1)}, u32[]{:S(2)}, u32[]{:S(2)}) collective-permute-start(bf16[128,1792]{1,0:T(8,128)(2,1)S(1)} %get-tuple-element.56), channel_id=1, source_target_pairs={{0,12},{1,13},{2,14},{3,15},{4,0},{5,1},{6,2},{7,3},{8,4},{9,5},{1... | collective-permute-start | bytes 1376264 | tf_op jit(solution)/shard_map/ppermute | solution.py:265
  180.4 14.9 %collective-permute-start.27 = (bf16[128,1792]{1,0:T(8,128)(2,1)S(1)}, bf16[128,1792]{1,0:T(8,128)(2,1)S(1)}, u32[]{:S(2)}, u32[]{:S(2)}) collective-permute-start(bf16[128,1792]{1,0:T(8,128)(2,1)S(1)} %add_convert_fusion.2), channel_id=1, source_target_pairs={{0,1},{1,2},{2,3},{3,0},{4,5},{5,6},{6,7},{7,4},{8,9},{9,10},{10,1... | collective-permute-start | bytes 1376264 | tf_op jit(solution)/shard_map/ppermute | solution.py:265
  206.5 19.5 %collective-permute-start.32 = (bf16[4,2,16,1792]{3,2,1,0:T(8,128)(2,1)S(1)}, bf16[4,2,16,1792]{3,2,1,0:T(8,128)(2,1)S(1)}, u32[]{:S(2)}, u32[]{:S(2)}) collective-permute-start(bf16[4,2,16,1792]{3,2,1,0:T(8,128)(2,1)S(1)} %get-tuple-element.79), channel_id=1, source_target_pairs={{0,16},{1,17},{2,18},{3,19},{4,20},{5,21},{6,22},{7,23},{8,24},{9,... | collective-permute-start | bytes 1376264 | tf_op jit(solution)/shard_map/ppermute | solution.py:265
  (20 other events, 236.9 us)
